TPU v7x, 256 devices: a whole 4x4x8 slice. The times are simulated.
256 devices in a mesh: ctx: 8 (over z_lo, core), ep: 32 (over y, x, z_hi).
Axes of the slice: x: 4, y: 4, z: 8 (z_hi: 2, z_lo: 4; z = z_hi * 4 + z_lo), core: 2. Of those that a mesh axis runs over, the one named last changes fastest.
Arguments:
- queries: bfloat16 [32768, 2048], P(('ctx', 'ep')), may hold values from -40 to 40
- keys: bfloat16 [32768, 256], P(('ctx', 'ep')), may hold values from -40 to 40
- values: bfloat16 [32768, 256], P(('ctx', 'ep')), may hold values from -6 to 6
- prior_out: bfloat16 [32768, 2048], P(('ctx', 'ep')), may hold values from -6 to 6
- prior_lse: float32 [32768, 16], P(('ctx', 'ep')), may hold values from 4 to 8
- residual: bfloat16 [32768, 2048], P(('ctx', 'ep')), may hold values from -40 to 40
- out_proj: bfloat16 [2048, 2048], P(('ctx', 'ep')), may hold values from -0.5 to 0.5
- norm_gain: float32 [2048], replicated, may hold values from 0.5 to 1.5
- expert_in: bfloat16 [32, 2048, 1536], P('ep'), may hold values from -0.125 to 0.125
- expert_out: bfloat16 [32, 768, 2048], P('ep'), may hold values from -0.21875 to 0.21875
- expert_ids: int32 [32768, 8], P(('ctx', 'ep')), may hold values from 0 to 31, as said below
- route_weight: float32 [32768, 8], P(('ctx', 'ep')), may hold values from 0.05 to 0.6
Outputs:
- layer_out: bfloat16 [32768, 2048], P(('ctx', 'ep'))
- attended: bfloat16 [32768, 2048], P(('ctx', 'ep'))
Inputs may be any that keep to these rules, and one draw needn't show every extreme that they name: `expert_ids`: each row names 8 different experts. In the rows of one device no expert is named more than 40 times, and one expert is named exactly 40 times in the rows of every device.
All inputs are finite; a program needn't handle non-finite values.
Results may differ from a plain program's by a relative error of at most 0.0061.
Values may be sent and summed in bfloat16 or wider, within the bound.
A program may use at most 128 MiB of HBM per device.

v0:
```python
import math

import jax
import jax.numpy as jnp
from jax import lax
from jax.sharding import PartitionSpec as P

HEADS = 16
KVH = 2
HD = 128
GROUP = 8


def passed_along(shard, axis, by):
    devices = lax.axis_size(axis)
    return lax.ppermute(shard, axis, [(i, (i + by) % devices) for i in range(devices)])


def run_expert(inputs, weight_in, weight_out, hidden_units):
    flat_in = inputs.reshape(-1, inputs.shape[-1])
    gate_up = jnp.dot(flat_in, weight_in, preferred_element_type=jnp.float32)
    activated = (jax.nn.silu(gate_up[:, :hidden_units]) * gate_up[:, hidden_units:]).astype(
        jnp.bfloat16
    )
    replies = jnp.dot(activated, weight_out, preferred_element_type=jnp.float32).astype(
        jnp.bfloat16
    )
    return replies.reshape(inputs.shape[:-1] + (weight_out.shape[-1],))


def shards(
    queries,
    keys,
    values,
    prior_out,
    prior_lse,
    residual,
    out_proj,
    norm_gain,
    expert_in,
    expert_out,
    expert_ids,
    route_weight,
):
    local_rows = queries.shape[0]
    ctx_count = lax.axis_size("ctx")
    ctx_here = lax.axis_index("ctx")
    ep_count = lax.axis_size("ep")
    reach_steps = min(2, ctx_count - 1)
    kv_pair = jnp.stack([keys, values])
    arrived = []
    current = kv_pair
    for stride in range(reach_steps):
        current = passed_along(current, "ctx", 1)
        arrived.append(current)
    window = jnp.concatenate(arrived, axis=1)
    width_kv = window.shape[1]
    key_win = window[0].reshape(width_kv, KVH, HD)
    value_win = window[1].reshape(width_kv, KVH, HD)
    query_blk = queries.reshape(local_rows, KVH, GROUP, HD)
    scores = jnp.einsum(
        "ighd,jgd->ghij", query_blk, key_win, preferred_element_type=jnp.float32
    ) / math.sqrt(HD)
    positions = jnp.arange(width_kv, dtype=jnp.int32)
    key_local = positions % local_rows
    key_ctx = (ctx_here - (positions // local_rows + 1)) % ctx_count
    query_local = jnp.arange(local_rows, dtype=jnp.int32)[:, None]
    visible = (key_local[None, :] < query_local) | (key_local[None, :] == query_local) & (
        key_ctx[None, :] <= ctx_here
    )
    scores = jnp.where(visible, scores, -jnp.inf)
    lse_prior = prior_lse.reshape(local_rows, KVH, GROUP).transpose(1, 2, 0)
    top_score = jnp.maximum(lse_prior, jnp.max(scores, axis=-1))
    weights = jnp.exp(scores - top_score[..., None])
    prior_weight = jnp.exp(lse_prior - top_score)
    totals = prior_weight + jnp.sum(weights, axis=-1)
    gathered = jnp.einsum(
        "ghij,jgd->ighd",
        weights.astype(jnp.bfloat16),
        value_win,
        preferred_element_type=jnp.float32,
    )
    prior_part = (
        prior_out.reshape(local_rows, KVH, GROUP, HD).astype(jnp.float32)
        * prior_weight.transpose(2, 0, 1)[..., None]
    )
    attended = ((prior_part + gathered) / totals.transpose(2, 0, 1)[..., None]).astype(jnp.bfloat16)
    attended = attended.reshape(local_rows, HEADS * HD)
    model_width = out_proj.shape[1]
    projected = jnp.dot(
        attended,
        lax.all_gather(out_proj, ("ctx", "ep"), axis=0, tiled=True),
        preferred_element_type=jnp.float32,
    )
    mixed_state = (residual.astype(jnp.float32) + projected).astype(jnp.bfloat16)
    state_f = lax.optimization_barrier(mixed_state).astype(jnp.float32)
    normed = (
        state_f * lax.rsqrt(jnp.mean(state_f * state_f, axis=-1, keepdims=True) + 1e-06) * norm_gain
    ).astype(jnp.bfloat16)
    experts_all = ep_count * expert_in.shape[0]
    top_count = expert_ids.shape[1]
    capacity = max(
        local_rows // 4, top_count * ((local_rows + experts_all - 2) // (experts_all - 1))
    )
    flat_ids = expert_ids.reshape(-1)
    one_hot = (flat_ids[:, None] == jnp.arange(experts_all, dtype=jnp.int32)[None, :]).astype(
        jnp.int32
    )
    earlier = jnp.cumsum(one_hot, axis=0) - one_hot
    slot_ids = flat_ids * capacity + jnp.sum(earlier * one_hot, axis=1)
    outgoing = jnp.zeros((experts_all * capacity, model_width), jnp.bfloat16)
    outgoing = (
        outgoing.at[slot_ids]
        .set(jnp.repeat(normed, top_count, axis=0))
        .reshape(experts_all, capacity, model_width)
    )
    weight_in = expert_in[0]
    weight_out = expert_out[0]
    hidden_units = weight_out.shape[0]
    replies = run_expert(
        lax.all_to_all(outgoing, "ep", split_axis=0, concat_axis=0, tiled=True),
        weight_in,
        weight_out,
        hidden_units,
    )
    returned = lax.all_to_all(replies, "ep", split_axis=0, concat_axis=0, tiled=True)
    picked = returned.reshape(experts_all * capacity, model_width)[slot_ids].reshape(
        local_rows, top_count, model_width
    )
    combined = jnp.sum(route_weight[:, :, None] * picked.astype(jnp.float32), axis=1)
    layer_out = (state_f + combined).astype(jnp.bfloat16)
    return (layer_out, attended)


def solution(mesh):
    return jax.shard_map(
        shards,
        mesh=mesh,
        in_specs=(
            P(("ctx", "ep"), None),
            P(("ctx", "ep"), None),
            P(("ctx", "ep"), None),
            P(("ctx", "ep"), None),
            P(("ctx", "ep"), None),
            P(("ctx", "ep"), None),
            P(("ctx", "ep"), None),
            P(),
            P("ep", None, None),
            P("ep", None, None),
            P(("ctx", "ep"), None),
            P(("ctx", "ep"), None),
        ),
        out_specs=(P(("ctx", "ep"), None), P(("ctx", "ep"), None)),
        check_vma=False,
    )
```

profile of v0, /device:TPU:94, one launch (start us, length us, event | category | flops | bytes accessed | tf_op | source)
XLA Modules:
  0.0 1033.1 jit_solution(17184374419318209309)
XLA Ops:
  7.9 1.2 copy.21
  9.1 1.0 copy.22
  10.7 0.8 copy.28
  11.6 9.0 reduce-window.6
  21.3 0.7 broadcast_multiply_fusion
  22.3 2.1 collective-permute-start.1
  24.4 2.0 copy.38
  26.4 2.3 copy.20
  28.7 1.0 constant_dynamic-update-slice_fusion.1
  29.8 1.6 fusion.39
  31.7 1.3 fusion.16
  33.1 665.9 %all-gather.2.cloned.1.call-done = bf16[2048,2048]{1,0:T(8,128)(2,1)} async-done(((bf16[8,2048]{1,0:T(8,128)(2,1)}), bf16[2048,2048]{1,0:T(8,128)(2,1)}) %all-gather.2.cloned.1.call-update) | async-done | bytes 8388624 | tf_op jit(solution)/shard_map/all_gather | solution.py:92
  698.9 4.9 fusion.8
  704.6 1.0 fusion.19
  705.6 10.1 scatter_custom_fusion
  715.7 142.1 %all_to_all.10 = bf16[32,40,2048]{2,1,0:T(8,128)(2,1)S(1)} all-to-all(bf16[32,40,2048]{2,1,0:T(8,128)(2,1)} %bitcast.79), channel_id=1, replica_groups=mesh['ctx'=8,'ep'=32] {'ep'}, dimensions={0} | all-to-all | bytes 10485760 | tf_op jit(solution)/shard_map/all_to_all | solution.py:121
  857.8 10.5 %fusion.1 = f32[1280,1536]{1,0:T(8,128)S(1)} fusion(bf16[1280,2048]{1,0:T(8,128)(2,1)S(1)} %bitcast.81, bf16[1,2048,1536]{2,1,0:T(8,128)(2,1)} %param.20), kind=kOutput, calls=%fused_computation.5 | convolution fusion | flops 8053063680 | bytes 19398656 | tf_op jit(solution)/shard_map/dot_general | solution.py:21
  868.3 6.1 convolution_convert_fusion
  874.4 11.5 %all-to-all-start.1 = ((bf16[32,40,2048]{2,1,0:T(8,128)(2,1)}), bf16[32,40,2048]{2,1,0:T(8,128)(2,1)}, u32[]{:S(2)}, u32[]{:S(2)}) async-start(bf16[32,40,2048]{2,1,0:T(8,128)(2,1)} %bitcast.80), calls=%async_computation.1 | async-start | bytes 10485760 | tf_op jit(solution)/shard_map/all_to_all | solution.py:126
  886.1 2.0 copy.32
  888.1 118.6 %all-to-all-done.1 = bf16[32,40,2048]{2,1,0:T(8,128)(2,1)} async-done(((bf16[32,40,2048]{2,1,0:T(8,128)(2,1)}), bf16[32,40,2048]{2,1,0:T(8,128)(2,1)}, u32[]{:S(2)}, u32[]{:S(2)}) %all-to-all-start.1) | async-done | bytes 5242912 | tf_op jit(solution)/shard_map/all_to_all | solution.py:126
  1006.7 12.0 %gather_fusion = bf16[1024,2048]{1,0:T(8,128)(2,1)} fusion(bf16[1280,2048]{1,0:T(8,128)(2,1)} %bitcast.25, s32[1024]{0:T(1024)S(1)} %broadcast_clamp_fusion), kind=kCustom, calls=%fused_computation | custom fusion | bytes 8392704 | tf_op jit(solution)/shard_map/gather | solution.py:127
  1018.8 6.6 fusion
  1025.3 0.9 fusion.20
  (45 shorter events, 3.7 us)
Async XLA Ops:
  7.2 861.1 %copy-start = (bf16[1,768,2048]{2,1,0:T(8,128)(2,1)S(1)}, bf16[1,768,2048]{2,1,0:T(8,128)(2,1)}, u32[]{:S(2)}) copy-start(bf16[1,768,2048]{2,1,0:T(8,128)(2,1)} %param.21) | copy-start | bytes 9437188
  7.2 691.8 %all-gather.2.cloned.1.call-start = ((), (), s32[]{:S(2)}) async-start(), calls=%async_computation.2 | async-start | bytes 8421376 | tf_op jit(solution)/shard_map/all_gather | solution.py:92
  10.0 21.3 %copy-start.4 = (f32[128,16]{0,1:T(8,128)S(1)}, f32[128,16]{0,1:T(8,128)}, u32[]{:S(2)}) copy-start(f32[128,16]{0,1:T(8,128)} %param.16) | copy-start | bytes 24580
  10.7 11.6 %collective-permute-start = (bf16[2,128,256]{1,2,0:T(8,128)(2,1)}, bf16[2,128,256]{1,2,0:T(8,128)(2,1)}, u32[]{:S(2)}, u32[]{:S(2)}) collective-permute-start(bf16[2,128,256]{1,2,0:T(8,128)(2,1)} %pad_maximum_fusion), channel_id=1, source_target_pairs={{0,32},{32,64},{64,96},{96,128},{128,160},{160,192},{192,224},{224... | collective-permute-start | bytes 393224 | tf_op jit(solution)/shard_map/ppermute | solution.py:16
  22.3 7.4 collective-permute-start.1
  28.7 3.0 copy-start.3
  698.9 5.7 copy-start.5
  703.8 0.8 copy-start.1
  874.4 11.5 %copy-start.6 = (f32[128,8]{0,1:T(8,128)S(1)}, f32[128,8]{0,1:T(8,128)}, u32[]{:S(2)}) copy-start(f32[128,8]{0,1:T(8,128)} %param.23) | copy-start | bytes 12292
  874.4 132.3 %all-to-all-start.1 = ((bf16[32,40,2048]{2,1,0:T(8,128)(2,1)}), bf16[32,40,2048]{2,1,0:T(8,128)(2,1)}, u32[]{:S(2)}, u32[]{:S(2)}) async-start(bf16[32,40,2048]{2,1,0:T(8,128)(2,1)} %bitcast.80), calls=%async_computation.1 | async-start | bytes 10485760 | tf_op jit(solution)/shard_map/all_to_all | solution.py:126
  1018.8 6.6 copy-start.2
Sparse Core Ops, SparseCore 0:
  9.9 689.0 all-gather.1
where the time goes:
time: 1050 us; the launch traced here: 1030 us
  waiting for transfers between devices  785 us (75%)
  blocking collectives  142 us (14%)
  local copies, waits for them, and re-layouts  33.8 us (3%)
  matrix products  24.4 us (2%)
  other arithmetic  19.7 us (2%)
  between operations  14.3 us (1%)
  starting transfers between devices  13.7 us (1%)
    all_gather x1, waiting for transfers between devices, shards(): lax.all_gather(out_proj, ('ctx', 'ep'), axis=0, tiled=True)  666 us
    all_to_all x1, blocking collectives, shards(): lax.all_to_all(outgoing, 'ep', split_axis=0, concat_axis=0, tiled=True)  142 us
    all_to_all x1, waiting for transfers between devices, shards(): lax.all_to_all(replies, 'ep', split_axis=0, concat_axis=0, tiled=True)  119 us
  transfers between devices with their start and end apart: 4, of which 2 were waited for; matrix products, arithmetic and copies ran while one was open for 2% of the time, Pallas kernels for 0%

commit v1 on v0

--- a/solution.py
+++ b/solution.py
@@ -87,11 +87,16 @@
     attended = ((prior_part + gathered) / totals.transpose(2, 0, 1)[..., None]).astype(jnp.bfloat16)
     attended = attended.reshape(local_rows, HEADS * HD)
     model_width = out_proj.shape[1]
-    projected = jnp.dot(
-        attended,
-        lax.all_gather(out_proj, ("ctx", "ep"), axis=0, tiled=True),
-        preferred_element_type=jnp.float32,
+    weight_rows = lax.all_gather(
+        lax.all_gather(out_proj, "ctx", axis=0, tiled=True), "ep", axis=0, tiled=True
     )
+    block_rows = out_proj.shape[0]
+    attended_perm = (
+        attended.reshape(local_rows, ctx_count, ep_count, block_rows)
+        .transpose(0, 2, 1, 3)
+        .reshape(local_rows, HEADS * HD)
+    )
+    projected = jnp.dot(attended_perm, weight_rows, preferred_element_type=jnp.float32)
     mixed_state = (residual.astype(jnp.float32) + projected).astype(jnp.bfloat16)
     state_f = lax.optimization_barrier(mixed_state).astype(jnp.float32)
     normed = (

time: 1050 us -> 500 us (0.48)
  waiting for transfers between devices: 785 us -> 192 us
  blocking collectives: 142 us -> 196 us
    all_gather x1, waiting for transfers between devices: 666 us -> 127 us  [shards(): lax.all_gather(lax.all_gather(out_proj, 'ctx', axis=0, tiled=True), 'ep',...]
    all_to_all x1, waiting for transfers between devices: 119 us -> 64.7 us  [shards(): lax.all_to_all(replies, 'ep', split_axis=0, concat_axis=0, tiled=True)]
    all_to_all x1, blocking collectives: 142 us -> 182 us  [shards(): lax.all_to_all(outgoing, 'ep', split_axis=0, concat_axis=0, tiled=True)]
    all_gather x0 -> x1, blocking collectives: none -> 13.9 us  [shards(): lax.all_gather(out_proj, 'ctx', axis=0, tiled=True)]
  transfers between devices with their start and end apart: 4 -> 4, of which waited for: 2 -> 2; matrix products, arithmetic and copies ran while one was open for 2% -> 5% of each run, Pallas kernels for 0% -> 0%
where the time goes in v1:
time: 500 us; the launch traced here: 492 us
  blocking collectives  196 us (39%)
  waiting for transfers between devices  192 us (38%)
  local copies, waits for them, and re-layouts  35.4 us (7%)
  matrix products  23.6 us (5%)
  other arithmetic  19.7 us (4%)
  between operations  14.3 us (3%)
  starting transfers between devices  11.3 us (2%)
    all_to_all x1, blocking collectives, shards(): lax.all_to_all(outgoing, 'ep', split_axis=0, concat_axis=0, tiled=True)  182 us
    all_gather x1, waiting for transfers between devices, shards(): lax.all_gather(lax.all_gather(out_proj, 'ctx', axis=0, tiled=True), 'ep',...  127 us
    all_to_all x1, waiting for transfers between devices, shards(): lax.all_to_all(replies, 'ep', split_axis=0, concat_axis=0, tiled=True)  64.7 us
    all_gather x1, blocking collectives, shards(): lax.all_gather(out_proj, 'ctx', axis=0, tiled=True)  13.9 us
    gather x1, local copies, waits for them, and re-layouts, shards(): returned.reshape(experts_all * capacity, model_width)[slot_ids]  12 us
    dot_general x1, matrix products, run_expert(): gate_up = jnp.dot(flat_in, weight_in, preferred_element_type=jnp.float32)  10.5 us
    scatter x1, local copies, waits for them, and re-layouts, shards(): outgoing = outgoing.at[slot_ids].set(jnp.repeat(normed, top_count, axis=0...  10.1 us
  transfers between devices with their start and end apart: 4, of which 2 were waited for; matrix products, arithmetic and copies ran while one was open for 5% of the time, Pallas kernels for 0%

profile of v1, /device:TPU:94, one launch (start us, length us, event | category | flops | bytes accessed | tf_op | source)
XLA Modules:
  0.0 492.1 jit_solution(16304300256929290591)
XLA Ops:
  7.2 13.9 %all_gather.6 = bf16[64,2048]{1,0:T(8,128)(2,1)} all-gather(bf16[8,2048]{1,0:T(8,128)(2,1)} %param.18), channel_id=1, replica_groups=mesh['ctx'=8,'ep'=32] {'ctx'}, dimensions={0}, use_global_device_ids=true | all-gather | bytes 294912 | tf_op jit(solution)/shard_map/all_gather | solution.py:91
  21.2 1.0 copy.21
  22.1 1.0 copy.22
  25.0 9.0 %reduce-window.6 = s32[32,8,128]{2,1,0:T(8,128)S(1)} reduce-window(s32[32,8,128]{2,1,0:T(8,128)S(1)} %fusion.29, s32[]{:T(128)} %constant.58.clone.1), window={size=1x1x128 pad=0_0x0_0x127_0}, to_apply=%region_2.3 | reduce-window | flops 4161536 | bytes 262148 | tf_op jit(solution)/shard_map/reduce-window
  35.7 3.5 collective-permute-start.1
  39.2 2.0 copy.39
  41.2 2.3 copy.20
  43.5 1.0 constant_dynamic-update-slice_fusion.1
  44.6 1.6 fusion.39
  47.1 0.8 copy-done.3
  47.9 0.9 copy.26
  48.8 126.8 %all-gather.2.cloned.1.call-done = bf16[2048,2048]{1,0:T(8,128)(2,1)} async-done(((bf16[64,2048]{1,0:T(8,128)(2,1)}), bf16[2048,2048]{1,0:T(8,128)(2,1)}) %all-gather.2.cloned.1.call-update) | async-done | bytes 8388624 | tf_op jit(solution)/shard_map/all_gather | solution.py:90
  175.7 4.9 fusion.8
  181.4 1.0 fusion.19
  182.3 10.1 %scatter_custom_fusion = bf16[1280,2048]{1,0:T(8,128)(2,1)} fusion(s32[1024]{0:T(1024)S(1)} %bitcast.99, bf16[]{:T(256)} %constant.69.clone.1, bf16[128,2048]{1,0:T(8,128)(2,1)} %fusion.19), kind=kCustom, calls=%fused_computation.7 | custom fusion | bytes 5767170 | tf_op jit(solution)/shard_map/scatter | solution.py:119
  192.4 182.4 %all_to_all.10 = bf16[32,40,2048]{2,1,0:T(8,128)(2,1)S(1)} all-to-all(bf16[32,40,2048]{2,1,0:T(8,128)(2,1)} %bitcast.83), channel_id=1, replica_groups=mesh['ctx'=8,'ep'=32] {'ep'}, dimensions={0} | all-to-all | bytes 10485760 | tf_op jit(solution)/shard_map/all_to_all | solution.py:126
  374.8 10.5 %fusion.1 = f32[1280,1536]{1,0:T(8,128)S(1)} fusion(bf16[1280,2048]{1,0:T(8,128)(2,1)S(1)} %bitcast.85, bf16[1,2048,1536]{2,1,0:T(8,128)(2,1)} %param.20), kind=kOutput, calls=%fused_computation.5 | convolution fusion | flops 8053063680 | bytes 19398656 | tf_op jit(solution)/shard_map/dot_general | solution.py:21
  385.4 6.1 %convolution_convert_fusion = bf16[1280,2048]{1,0:T(8,128)(2,1)} fusion(bf16[1,768,2048]{2,1,0:T(8,128)(2,1)S(1)} %copy-done, f32[1280,1536]{1,0:T(8,128)S(1)} %fusion.1), kind=kOutput, calls=%fused_computation.4 | convolution fusion | flops 4035051520 | bytes 16252928 | tf_op jit(solution)/shard_map/dot_general | solution.py:25
  391.5 7.4 %all-to-all-start.1 = ((bf16[32,40,2048]{2,1,0:T(8,128)(2,1)}), bf16[32,40,2048]{2,1,0:T(8,128)(2,1)}, u32[]{:S(2)}, u32[]{:S(2)}) async-start(bf16[32,40,2048]{2,1,0:T(8,128)(2,1)} %bitcast.84), calls=%async_computation.1 | async-start | bytes 10485760 | tf_op jit(solution)/shard_map/all_to_all | solution.py:131
  399.0 2.0 copy.33
  401.1 64.7 %all-to-all-done.1 = bf16[32,40,2048]{2,1,0:T(8,128)(2,1)} async-done(((bf16[32,40,2048]{2,1,0:T(8,128)(2,1)}), bf16[32,40,2048]{2,1,0:T(8,128)(2,1)}, u32[]{:S(2)}, u32[]{:S(2)}) %all-to-all-start.1) | async-done | bytes 5242912 | tf_op jit(solution)/shard_map/all_to_all | solution.py:131
  465.7 12.0 %gather_fusion = bf16[1024,2048]{1,0:T(8,128)(2,1)} fusion(bf16[1280,2048]{1,0:T(8,128)(2,1)} %bitcast.27, s32[1024]{0:T(1024)S(1)} %broadcast_clamp_fusion), kind=kCustom, calls=%fused_computation | custom fusion | bytes 8392704 | tf_op jit(solution)/shard_map/gather | solution.py:132
  477.8 6.6 %fusion = f32[128,2048]{1,0:T(8,128)S(1)} fusion(bf16[1024,2048]{1,0:T(8,128)(2,1)} %gather_fusion, f32[128,8]{1,0:T(8,128)S(1)} %copy.27), kind=kLoop, calls=%fused_computation.3 | loop fusion | flops 6029312 | bytes 5246976 | tf_op jit(solution)/shard_map/reduce_sum | solution.py:135
  484.4 0.9 fusion.20
  (49 shorter events, 5.4 us)
Async XLA Ops:
  7.2 378.2 %copy-start = (bf16[1,768,2048]{2,1,0:T(8,128)(2,1)S(1)}, bf16[1,768,2048]{2,1,0:T(8,128)(2,1)}, u32[]{:S(2)}) copy-start(bf16[1,768,2048]{2,1,0:T(8,128)(2,1)} %param.21) | copy-start | bytes 9437188
  7.2 168.5 %all-gather.2.cloned.1.call-start = ((), (), s32[]{:S(2)}) async-start(), calls=%async_computation.2 | async-start | bytes 8650752 | tf_op jit(solution)/shard_map/all_gather | solution.py:90
  23.1 23.1 %copy-start.5 = (f32[128,16]{0,1:T(8,128)S(1)}, f32[128,16]{0,1:T(8,128)}, u32[]{:S(2)}) copy-start(f32[128,16]{0,1:T(8,128)} %param.16) | copy-start | bytes 24580
  23.8 11.9 %collective-permute-start = (bf16[2,128,256]{1,2,0:T(8,128)(2,1)}, bf16[2,128,256]{1,2,0:T(8,128)(2,1)}, u32[]{:S(2)}, u32[]{:S(2)}) collective-permute-start(bf16[2,128,256]{1,2,0:T(8,128)(2,1)} %pad_maximum_fusion), channel_id=1, source_target_pairs={{0,32},{32,64},{64,96},{96,128},{128,160},{160,192},{192,224},{224... | collective-permute-start | bytes 393224 | tf_op jit(solution)/shard_map/ppermute | solution.py:16
  35.7 8.8 %collective-permute-start.1 = (bf16[2,128,256]{1,2,0:T(8,128)(2,1)}, bf16[2,128,256]{1,2,0:T(8,128)(2,1)S(1)}, u32[]{:S(2)}, u32[]{:S(2)}) collective-permute-start(bf16[2,128,256]{1,2,0:T(8,128)(2,1)} %collective-permute-done), channel_id=1, source_target_pairs={{0,32},{32,64},{64,96},{96,128},{128,160},{160,192},{192,224},{224... | collective-permute-start | bytes 393224 | tf_op jit(solution)/shard_map/ppermute | solution.py:16
  43.5 3.0 copy-start.4
  47.1 0.8 copy-start.3
  175.7 5.7 %copy-start.6 = (f32[2048]{0:T(1024)S(1)}, f32[2048]{0:T(1024)}, u32[]{:S(2)}) copy-start(f32[2048]{0:T(1024)} %param.19) | copy-start | bytes 24580
  180.6 0.8 copy-start.1
  391.5 7.4 %copy-start.7 = (f32[128,8]{0,1:T(8,128)S(1)}, f32[128,8]{0,1:T(8,128)}, u32[]{:S(2)}) copy-start(f32[128,8]{0,1:T(8,128)} %param.23) | copy-start | bytes 12292
  391.5 74.3 %all-to-all-start.1 = ((bf16[32,40,2048]{2,1,0:T(8,128)(2,1)}), bf16[32,40,2048]{2,1,0:T(8,128)(2,1)}, u32[]{:S(2)}, u32[]{:S(2)}) async-start(bf16[32,40,2048]{2,1,0:T(8,128)(2,1)} %bitcast.84), calls=%async_computation.1 | async-start | bytes 10485760 | tf_op jit(solution)/shard_map/all_to_all | solution.py:131
  477.8 6.6 %copy-start.2 = (bf16[128,2048]{1,0:T(8,128)(2,1)S(1)}, bf16[128,2048]{1,0:T(8,128)(2,1)}, u32[]{:S(2)}) copy-start(bf16[128,2048]{1,0:T(8,128)(2,1)} %copy-done.1) | copy-start | bytes 1572868
Sparse Core Ops, SparseCore 0:
  21.3 154.3 all-gather.1

commit v2 on v1

--- a/solution.py
+++ b/solution.py
@@ -87,16 +87,25 @@
     attended = ((prior_part + gathered) / totals.transpose(2, 0, 1)[..., None]).astype(jnp.bfloat16)
     attended = attended.reshape(local_rows, HEADS * HD)
     model_width = out_proj.shape[1]
-    weight_rows = lax.all_gather(
-        lax.all_gather(out_proj, "ctx", axis=0, tiled=True), "ep", axis=0, tiled=True
-    )
+    column_half = model_width // 2
+    core = ctx_here % 2
+    column_rows = lax.all_gather(out_proj, "ctx", axis=0, tiled=True)
+    own_half = lax.dynamic_slice_in_dim(column_rows, core * column_half, column_half, axis=1)
+    own_half = lax.all_gather(own_half, "ep", axis=0, tiled=True)
+    other_half = lax.ppermute(own_half, "ctx", [(i, i ^ 1) for i in range(ctx_count)])
     block_rows = out_proj.shape[0]
     attended_perm = (
         attended.reshape(local_rows, ctx_count, ep_count, block_rows)
         .transpose(0, 2, 1, 3)
         .reshape(local_rows, HEADS * HD)
     )
-    projected = jnp.dot(attended_perm, weight_rows, preferred_element_type=jnp.float32)
+    own_part = jnp.dot(attended_perm, own_half, preferred_element_type=jnp.float32)
+    other_part = jnp.dot(attended_perm, other_half, preferred_element_type=jnp.float32)
+    projected = jnp.zeros((local_rows, model_width), jnp.float32)
+    projected = lax.dynamic_update_slice_in_dim(projected, own_part, core * column_half, axis=1)
+    projected = lax.dynamic_update_slice_in_dim(
+        projected, other_part, (1 - core) * column_half, axis=1
+    )
     mixed_state = (residual.astype(jnp.float32) + projected).astype(jnp.bfloat16)
     state_f = lax.optimization_barrier(mixed_state).astype(jnp.float32)
     normed = (

time: 500 us -> 472 us (0.944); the launches traced: 492 us -> 471 us
  blocking collectives: 196 us -> 141 us
  waiting for transfers between devices: 192 us -> 228 us
    all_to_all x1, blocking collectives: 182 us -> 128 us  [shards(): lax.all_to_all(outgoing, 'ep', split_axis=0, concat_axis=0, tiled=True)]
    all_to_all x1, waiting for transfers between devices: 64.7 us -> 117 us  [shards(): lax.all_to_all(replies, 'ep', split_axis=0, concat_axis=0, tiled=True)]
    all_gather x1, waiting for transfers between devices: 127 us -> 112 us  [shards(): own_half = lax.all_gather(own_half, 'ep', axis=0, tiled=True)]
  transfers between devices with their start and end apart: 4 -> 5, of which waited for: 2 -> 2; matrix products, arithmetic and copies ran while one was open for 5% -> 5% of each run, Pallas kernels for 0% -> 0%
where the time goes in v2:
time: 472 us; the launch traced here: 471 us
  waiting for transfers between devices  228 us (48%)
  blocking collectives  141 us (30%)
  local copies, waits for them, and re-layouts  36 us (8%)
  matrix products  22.4 us (5%)
  other arithmetic  19.8 us (4%)
  between operations  14.4 us (3%)
  starting transfers between devices  9.49 us (2%)
    all_to_all x1, blocking collectives, shards(): lax.all_to_all(outgoing, 'ep', split_axis=0, concat_axis=0, tiled=True)  128 us
    all_to_all x1, waiting for transfers between devices, shards(): lax.all_to_all(replies, 'ep', split_axis=0, concat_axis=0, tiled=True)  117 us
    all_gather x1, waiting for transfers between devices, shards(): own_half = lax.all_gather(own_half, 'ep', axis=0, tiled=True)  112 us
    all_gather x1, blocking collectives, shards(): column_rows = lax.all_gather(out_proj, 'ctx', axis=0, tiled=True)  12.8 us
    gather x1, local copies, waits for them, and re-layouts, shards(): returned.reshape(experts_all * capacity, model_width)[slot_ids]  12 us
    dot_general x1, matrix products, run_expert(): gate_up = jnp.dot(flat_in, weight_in, preferred_element_type=jnp.float32)  10.5 us
    scatter x1, local copies, waits for them, and re-layouts, shards(): outgoing = outgoing.at[slot_ids].set(jnp.repeat(normed, top_count, axis=0...  10.1 us
    unnamed x27, local copies, waits for them, and re-layouts  9.98 us
  transfers between devices with their start and end apart: 5, of which 2 were waited for; matrix products, arithmetic and copies ran while one was open for 5% of the time, Pallas kernels for 0%

profile of v2, /device:TPU:94, one launch (start us, length us, event | category | flops | bytes accessed | tf_op | source)
XLA Modules:
  0.0 471.1 jit_solution(506274494953376835)
XLA Ops:
  7.2 12.8 %all_gather.6 = bf16[64,2048]{1,0:T(8,128)(2,1)S(1)} all-gather(bf16[8,2048]{1,0:T(8,128)(2,1)} %param.18), channel_id=1, replica_groups=mesh['ctx'=8,'ep'=32] {'ctx'}, dimensions={0}, use_global_device_ids=true | all-gather | bytes 294912 | tf_op jit(solution)/shard_map/all_gather | solution.py:92
  20.8 111.6 %all-gather.2.cloned.1.call-done = bf16[2048,1024]{1,0:T(8,128)(2,1)} async-done(((bf16[64,1024]{1,0:T(8,128)(2,1)}), bf16[2048,1024]{1,0:T(8,128)(2,1)}) %all-gather.2.cloned.1.call-update) | async-done | bytes 4194320 | tf_op jit(solution)/shard_map/all_gather | solution.py:94
  132.4 0.9 copy.21
  133.3 1.0 copy.22
  135.5 0.8 copy.29
  136.4 9.0 %reduce-window.6 = s32[32,8,128]{2,1,0:T(8,128)S(1)} reduce-window(s32[32,8,128]{2,1,0:T(8,128)S(1)} %fusion.28, s32[]{:T(128)} %constant.73.clone.1), window={size=1x1x128 pad=0_0x0_0x127_0}, to_apply=%region_2.3 | reduce-window | flops 4161536 | bytes 262148 | tf_op jit(solution)/shard_map/reduce-window
  147.2 2.0 copy.39
  149.1 2.3 copy.20
  151.5 1.0 constant_dynamic-update-slice_fusion.1
  152.5 1.6 fusion.38
  156.0 0.9 copy-done.3
  156.8 0.7 convolution_dynamic-update-slice_fusion.1
  157.6 3.0 convolution_dynamic-update-slice_fusion
  161.5 1.0 fusion.18
  162.5 10.1 %scatter_custom_fusion = bf16[1280,2048]{1,0:T(8,128)(2,1)} fusion(s32[1024]{0:T(1024)S(1)} %bitcast.102, bf16[]{:T(256)} %constant.86.clone.1, bf16[128,2048]{1,0:T(8,128)(2,1)} %fusion.18), kind=kCustom, calls=%fused_computation.7 | custom fusion | bytes 5767170 | tf_op jit(solution)/shard_map/scatter | solution.py:128
  172.5 127.9 %all_to_all.10 = bf16[32,40,2048]{2,1,0:T(8,128)(2,1)S(1)} all-to-all(bf16[32,40,2048]{2,1,0:T(8,128)(2,1)} %bitcast.85), channel_id=1, replica_groups=mesh['ctx'=8,'ep'=32] {'ep'}, dimensions={0} | all-to-all | bytes 10485760 | tf_op jit(solution)/shard_map/all_to_all | solution.py:135
  300.4 10.5 %fusion.1 = f32[1280,1536]{1,0:T(8,128)S(1)} fusion(bf16[1280,2048]{1,0:T(8,128)(2,1)S(1)} %bitcast.87, bf16[1,2048,1536]{2,1,0:T(8,128)(2,1)} %param.20), kind=kOutput, calls=%fused_computation.5 | convolution fusion | flops 8053063680 | bytes 19398656 | tf_op jit(solution)/shard_map/dot_general | solution.py:21
  311.0 6.1 %convolution_convert_fusion = bf16[1280,2048]{1,0:T(8,128)(2,1)} fusion(bf16[1,768,2048]{2,1,0:T(8,128)(2,1)S(1)} %copy-done, f32[1280,1536]{1,0:T(8,128)S(1)} %fusion.1), kind=kOutput, calls=%fused_computation.4 | convolution fusion | flops 4035051520 | bytes 16252928 | tf_op jit(solution)/shard_map/dot_general | solution.py:25
  317.1 8.9 %all-to-all-start.1 = ((bf16[32,40,2048]{2,1,0:T(8,128)(2,1)}), bf16[32,40,2048]{2,1,0:T(8,128)(2,1)}, u32[]{:S(2)}, u32[]{:S(2)}) async-start(bf16[32,40,2048]{2,1,0:T(8,128)(2,1)} %bitcast.86), calls=%async_computation.1 | async-start | bytes 10485760 | tf_op jit(solution)/shard_map/all_to_all | solution.py:140
  326.0 2.0 copy.33
  328.1 116.6 %all-to-all-done.1 = bf16[32,40,2048]{2,1,0:T(8,128)(2,1)} async-done(((bf16[32,40,2048]{2,1,0:T(8,128)(2,1)}), bf16[32,40,2048]{2,1,0:T(8,128)(2,1)}, u32[]{:S(2)}, u32[]{:S(2)}) %all-to-all-start.1) | async-done | bytes 5242912 | tf_op jit(solution)/shard_map/all_to_all | solution.py:140
  444.7 12.0 %gather_fusion = bf16[1024,2048]{1,0:T(8,128)(2,1)} fusion(bf16[1280,2048]{1,0:T(8,128)(2,1)} %bitcast.28, s32[1024]{0:T(1024)S(1)} %broadcast_clamp_fusion), kind=kCustom, calls=%fused_computation | custom fusion | bytes 8392704 | tf_op jit(solution)/shard_map/gather | solution.py:141
  456.7 6.6 %fusion = f32[128,2048]{1,0:T(8,128)S(1)} fusion(bf16[1024,2048]{1,0:T(8,128)(2,1)} %gather_fusion, f32[128,8]{1,0:T(8,128)S(1)} %copy.27), kind=kLoop, calls=%fused_computation.3 | loop fusion | flops 6029312 | bytes 5246976 | tf_op jit(solution)/shard_map/reduce_sum | solution.py:144
  463.3 0.9 fusion.19
  (59 shorter events, 6.5 us)
Async XLA Ops:
  7.2 303.8 %copy-start = (bf16[1,768,2048]{2,1,0:T(8,128)(2,1)S(1)}, bf16[1,768,2048]{2,1,0:T(8,128)(2,1)}, u32[]{:S(2)}) copy-start(bf16[1,768,2048]{2,1,0:T(8,128)(2,1)} %param.21) | copy-start | bytes 9437188
  7.2 125.2 %all-gather.2.cloned.1.call-start = ((), (), s32[]{:S(2)}) async-start(), calls=%async_computation.2 | async-start | bytes 4325376 | tf_op jit(solution)/shard_map/all_gather | solution.py:94
  132.4 25.2 %collective-permute-start.2 = (bf16[2048,1024]{1,0:T(8,128)(2,1)}, bf16[2048,1024]{1,0:T(8,128)(2,1)}, u32[]{:S(2)}, u32[]{:S(2)}) collective-permute-start(bf16[2048,1024]{1,0:T(8,128)(2,1)} %all-gather.2.cloned.1.call-done), channel_id=1, source_target_pairs={{0,32},{32,0},{64,96},{96,64},{128,160},{160,128},{192,224},{224,1... | collective-permute-start | bytes 12582920 | tf_op jit(solution)/shard_map/ppermute | solution.py:95
  134.3 19.8 %copy-start.7 = (f32[128,16]{0,1:T(8,128)S(1)}, f32[128,16]{0,1:T(8,128)}, u32[]{:S(2)}) copy-start(f32[128,16]{0,1:T(8,128)} %param.16) | copy-start | bytes 24580
  135.0 12.1 %collective-permute-start = (bf16[2,128,256]{1,2,0:T(8,128)(2,1)}, bf16[2,128,256]{1,2,0:T(8,128)(2,1)}, u32[]{:S(2)}, u32[]{:S(2)}) collective-permute-start(bf16[2,128,256]{1,2,0:T(8,128)(2,1)} %pad_maximum_fusion), channel_id=1, source_target_pairs={{0,32},{32,64},{64,96},{96,128},{128,160},{160,192},{192,224},{224... | collective-permute-start | bytes 393224 | tf_op jit(solution)/shard_map/ppermute | solution.py:16
  147.1 5.4 %collective-permute-start.1 = (bf16[2,128,256]{1,2,0:T(8,128)(2,1)}, bf16[2,128,256]{1,2,0:T(8,128)(2,1)S(1)}, u32[]{:S(2)}, u32[]{:S(2)}) collective-permute-start(bf16[2,128,256]{1,2,0:T(8,128)(2,1)} %collective-permute-done), channel_id=1, source_target_pairs={{0,32},{32,64},{64,96},{96,128},{128,160},{160,192},{192,224},{224... | collective-permute-start | bytes 393224 | tf_op jit(solution)/shard_map/ppermute | solution.py:16
  151.4 3.0 copy-start.5
  154.5 2.4 copy-start.3
  155.0 0.8 copy-start.4
  156.8 3.7 copy-start.6
  157.6 3.9 copy-start.8
  160.7 0.8 copy-start.1
  317.1 8.9 %copy-start.9 = (f32[128,8]{0,1:T(8,128)S(1)}, f32[128,8]{0,1:T(8,128)}, u32[]{:S(2)}) copy-start(f32[128,8]{0,1:T(8,128)} %param.23) | copy-start | bytes 12292
  317.1 127.6 %all-to-all-start.1 = ((bf16[32,40,2048]{2,1,0:T(8,128)(2,1)}), bf16[32,40,2048]{2,1,0:T(8,128)(2,1)}, u32[]{:S(2)}, u32[]{:S(2)}) async-start(bf16[32,40,2048]{2,1,0:T(8,128)(2,1)} %bitcast.86), calls=%async_computation.1 | async-start | bytes 10485760 | tf_op jit(solution)/shard_map/all_to_all | solution.py:140
  456.7 6.6 %copy-start.2 = (bf16[128,2048]{1,0:T(8,128)(2,1)S(1)}, bf16[128,2048]{1,0:T(8,128)(2,1)}, u32[]{:S(2)}) copy-start(bf16[128,2048]{1,0:T(8,128)(2,1)} %copy-done.1) | copy-start | bytes 1572868
Sparse Core Ops, SparseCore 0:
  20.9 111.4 all-gather.1

commit v3 on v2

--- a/solution.py
+++ b/solution.py
@@ -1,9 +1,14 @@
+import functools
 import math
 
 import jax
 import jax.numpy as jnp
 from jax import lax
+from jax.experimental import pallas as pl
+from jax.experimental.pallas import tpu as pltpu
 from jax.sharding import PartitionSpec as P
+
+MESH = pl.DeviceIdType.MESH
 
 HEADS = 16
 KVH = 2
@@ -14,6 +19,93 @@
 def passed_along(shard, axis, by):
     devices = lax.axis_size(axis)
     return lax.ppermute(shard, axis, [(i, (i + by) % devices) for i in range(devices)])
+
+
+def exchange_kernel(per_peer, src_ref, dst_ref, send_sem, recv_sem, local_sem):
+    n_ep = lax.axis_size("ep")
+    n_ctx = lax.axis_size("ctx")
+    me = lax.axis_index("ep")
+    ctx_me = lax.axis_index("ctx")
+    ctx_far = (ctx_me + n_ctx // 2) % n_ctx
+
+    def peer(j):
+        p = (me + j) % n_ep
+        same = 1 - (p + me) % 2
+        return p, same * ctx_me + (1 - same) * ctx_far
+
+    def chunk(p):
+        return src_ref.at[p] if per_peer else src_ref.at[0]
+
+    barrier = pltpu.get_barrier_semaphore()
+
+    def greet(j, carry):
+        p, c = peer(j)
+        pl.semaphore_signal(barrier, inc=1, device_id=(c, p), device_id_type=MESH)
+        return carry
+
+    lax.fori_loop(1, n_ep, greet, 0)
+    pl.semaphore_wait(barrier, n_ep - 1)
+
+    local = pltpu.make_async_copy(chunk(me), dst_ref.at[me], local_sem)
+    local.start()
+
+    def send(j, carry):
+        p, c = peer(j)
+        pltpu.make_async_remote_copy(
+            src_ref=chunk(p),
+            dst_ref=dst_ref.at[me],
+            send_sem=send_sem.at[p],
+            recv_sem=recv_sem.at[me],
+            device_id=(c, p),
+            device_id_type=MESH,
+        ).start()
+        return carry
+
+    lax.fori_loop(1, n_ep, send, 0)
+
+    def finish(j, carry):
+        p, c = peer(j)
+        pltpu.make_async_remote_copy(
+            src_ref=chunk(p),
+            dst_ref=dst_ref.at[me],
+            send_sem=send_sem.at[p],
+            recv_sem=recv_sem.at[me],
+            device_id=(c, p),
+            device_id_type=MESH,
+        ).wait_send()
+        pltpu.make_async_remote_copy(
+            src_ref=chunk(p),
+            dst_ref=dst_ref.at[p],
+            send_sem=send_sem.at[p],
+            recv_sem=recv_sem.at[p],
+            device_id=(c, p),
+            device_id_type=MESH,
+        ).wait_recv()
+        return carry
+
+    lax.fori_loop(1, n_ep, finish, 0)
+    local.wait()
+
+
+def exchange(src, per_peer, collective_id):
+    n_ep = lax.axis_size("ep")
+    block = src.shape[1:]
+    moved = n_ep * math.prod(block) * src.dtype.itemsize
+    return pl.pallas_call(
+        functools.partial(exchange_kernel, per_peer),
+        out_shape=jax.ShapeDtypeStruct((n_ep,) + block, src.dtype),
+        in_specs=[pl.BlockSpec(memory_space=pl.ANY)],
+        out_specs=pl.BlockSpec(memory_space=pl.ANY),
+        scratch_shapes=[
+            pltpu.SemaphoreType.DMA((n_ep,)),
+            pltpu.SemaphoreType.DMA((n_ep,)),
+            pltpu.SemaphoreType.DMA,
+        ],
+        compiler_params=pltpu.CompilerParams(
+            collective_id=collective_id, has_side_effects=True
+        ),
+        cost_estimate=pl.CostEstimate(flops=0, transcendentals=0, bytes_accessed=2 * moved),
+    )(src)
 
 
 def run_expert(inputs, weight_in, weight_out, hidden_units):
@@ -91,7 +183,7 @@
     core = ctx_here % 2
     column_rows = lax.all_gather(out_proj, "ctx", axis=0, tiled=True)
     own_half = lax.dynamic_slice_in_dim(column_rows, core * column_half, column_half, axis=1)
-    own_half = lax.all_gather(own_half, "ep", axis=0, tiled=True)
+    own_half = exchange(own_half[None], False, 0).reshape(-1, column_half)
     other_half = lax.ppermute(own_half, "ctx", [(i, i ^ 1) for i in range(ctx_count)])
     block_rows = out_proj.shape[0]
     attended_perm = (

time: 472 us -> 454 us (0.962)
  the two profiles are of different devices: /device:TPU:94 before, /device:TPU:129 now
where the time goes in v3:
time: 454 us; the launch traced here: 453 us
  blocking collectives  145 us (32%)
  waiting for transfers between devices  120 us (26%)
  Pallas kernels  98.2 us (22%)
  local copies, waits for them, and re-layouts  33.7 us (7%)
  matrix products  22.4 us (5%)
  other arithmetic  19.1 us (4%)
  starting transfers between devices  14 us (3%)
    all_to_all x1, blocking collectives, shards(): lax.all_to_all(outgoing, 'ep', split_axis=0, concat_axis=0, tiled=True)  130 us
    all_to_all x1, waiting for transfers between devices, shards(): lax.all_to_all(replies, 'ep', split_axis=0, concat_axis=0, tiled=True)  120 us
    pallas_call x1, Pallas kernels, exchange(): pl.pallas_call(functools.partial(exchange_kernel, per_peer), out_shape=ja...  98.2 us
    all_gather x1, blocking collectives, shards(): column_rows = lax.all_gather(out_proj, 'ctx', axis=0, tiled=True)  15 us
    gather x1, local copies, waits for them, and re-layouts, shards(): returned.reshape(experts_all * capacity, model_width)[slot_ids]  12 us
    dot_general x1, matrix products, run_expert(): gate_up = jnp.dot(flat_in, weight_in, preferred_element_type=jnp.float32)  10.5 us
    scatter x1, local copies, waits for them, and re-layouts, shards(): outgoing = outgoing.at[slot_ids].set(jnp.repeat(normed, top_count, axis=0...  10.1 us
    another operation x3, other arithmetic  9.14 us
  transfers between devices with their start and end apart: 4, of which 1 were waited for; matrix products, arithmetic and copies ran while one was open for 5% of the time, Pallas kernels for 0%

profile of v3, /device:TPU:129, one launch (start us, length us, event | category | flops | bytes accessed | tf_op | source)
XLA Modules:
  0.0 453.0 jit_solution(5429834348392085075)
XLA Ops:
  0.7 15.0 %all_gather.3 = bf16[64,2048]{1,0:T(8,128)(2,1)S(1)} all-gather(bf16[8,2048]{1,0:T(8,128)(2,1)} %param.18), channel_id=1, replica_groups=mesh['ctx'=8,'ep'=32] {'ctx'}, dimensions={0}, use_global_device_ids=true | all-gather | bytes 294912 | tf_op jit(solution)/shard_map/all_gather | solution.py:184
  16.4 98.2 %shard_map.131 = bf16[32,64,1024]{2,1,0:T(8,128)(2,1)} custom-call(bf16[1,64,1024]{2,1,0:T(8,128)(2,1)} %dynamic-slice_bitcast_fusion.src_ref), custom_call_target="tpu_custom_call" | custom-call | bytes 8388608 | tf_op jit(solution)/shard_map/pallas_call | solution.py:94
  114.6 1.0 collective-permute-start.2
  116.5 4.6 %collective-permute-start = (bf16[2,128,256]{1,2,0:T(8,128)(2,1)}, bf16[2,128,256]{1,2,0:T(8,128)(2,1)}, u32[]{:S(2)}, u32[]{:S(2)}) collective-permute-start(bf16[2,128,256]{1,2,0:T(8,128)(2,1)} %pad_maximum_fusion), channel_id=1, source_target_pairs={{0,32},{32,64},{64,96},{96,128},{128,160},{160,192},{192,224},{224... | collective-permute-start | bytes 393224 | tf_op jit(solution)/shard_map/ppermute | solution.py:21
  121.4 9.0 %reduce-window.6 = s32[32,8,128]{2,1,0:T(8,128)S(1)} reduce-window(s32[32,8,128]{2,1,0:T(8,128)S(1)} %fusion.28, s32[]{:T(128)} %constant.73.clone.1), window={size=1x1x128 pad=0_0x0_0x127_0}, to_apply=%region_2.3 | reduce-window | flops 4161536 | bytes 262148 | tf_op jit(solution)/shard_map/reduce-window
  131.9 2.0 copy.39
  133.9 2.3 copy.20
  136.2 1.0 constant_dynamic-update-slice_fusion.1
  137.3 1.6 fusion.38
  139.9 0.7 copy-done.4
  140.7 0.9 copy-done.1
  141.6 0.7 convolution_dynamic-update-slice_fusion.1
  142.4 2.9 convolution_dynamic-update-slice_fusion
  146.2 1.0 fusion.18
  147.2 10.1 %scatter_custom_fusion = bf16[1280,2048]{1,0:T(8,128)(2,1)} fusion(s32[1024]{0:T(1024)S(1)} %bitcast.107, bf16[]{:T(256)} %constant.86.clone.1, bf16[128,2048]{1,0:T(8,128)(2,1)} %fusion.18), kind=kCustom, calls=%fused_computation.7 | custom fusion | bytes 5767170 | tf_op jit(solution)/shard_map/scatter | solution.py:220
  157.3 129.8 %all_to_all.10 = bf16[32,40,2048]{2,1,0:T(8,128)(2,1)S(1)} all-to-all(bf16[32,40,2048]{2,1,0:T(8,128)(2,1)} %bitcast.88), channel_id=1, replica_groups=mesh['ctx'=8,'ep'=32] {'ep'}, dimensions={0} | all-to-all | bytes 10485760 | tf_op jit(solution)/shard_map/all_to_all | solution.py:227
  287.1 10.5 %fusion.1 = f32[1280,1536]{1,0:T(8,128)S(1)} fusion(bf16[1280,2048]{1,0:T(8,128)(2,1)S(1)} %bitcast.92, bf16[1,2048,1536]{2,1,0:T(8,128)(2,1)} %param.20), kind=kOutput, calls=%fused_computation.5 | convolution fusion | flops 8053063680 | bytes 19398656 | tf_op jit(solution)/shard_map/dot_general | solution.py:113
  297.6 6.1 %convolution_convert_fusion = bf16[1280,2048]{1,0:T(8,128)(2,1)} fusion(bf16[1,768,2048]{2,1,0:T(8,128)(2,1)S(1)} %copy-done, f32[1280,1536]{1,0:T(8,128)S(1)} %fusion.1), kind=kOutput, calls=%fused_computation.4 | convolution fusion | flops 4035051520 | bytes 16252928 | tf_op jit(solution)/shard_map/dot_general | solution.py:117
  303.7 7.8 %all-to-all-start.1 = ((bf16[32,40,2048]{2,1,0:T(8,128)(2,1)}), bf16[32,40,2048]{2,1,0:T(8,128)(2,1)}, u32[]{:S(2)}, u32[]{:S(2)}) async-start(bf16[32,40,2048]{2,1,0:T(8,128)(2,1)} %bitcast.91), calls=%async_computation.1 | async-start | bytes 10485760 | tf_op jit(solution)/shard_map/all_to_all | solution.py:232
  311.6 2.0 copy.33
  313.6 119.8 %all-to-all-done.1 = bf16[32,40,2048]{2,1,0:T(8,128)(2,1)} async-done(((bf16[32,40,2048]{2,1,0:T(8,128)(2,1)}), bf16[32,40,2048]{2,1,0:T(8,128)(2,1)}, u32[]{:S(2)}, u32[]{:S(2)}) %all-to-all-start.1) | async-done | bytes 5242912 | tf_op jit(solution)/shard_map/all_to_all | solution.py:232
  433.5 12.0 %gather_fusion = bf16[1024,2048]{1,0:T(8,128)(2,1)} fusion(bf16[1280,2048]{1,0:T(8,128)(2,1)} %bitcast.30, s32[1024]{0:T(1024)S(1)} %broadcast_clamp_fusion), kind=kCustom, calls=%fused_computation | custom fusion | bytes 8392704 | tf_op jit(solution)/shard_map/gather | solution.py:233
  445.5 6.6 %fusion = f32[128,2048]{1,0:T(8,128)S(1)} fusion(bf16[1024,2048]{1,0:T(8,128)(2,1)} %gather_fusion, f32[128,8]{1,0:T(8,128)S(1)} %copy.27), kind=kLoop, calls=%fused_computation.3 | loop fusion | flops 6029312 | bytes 5246976 | tf_op jit(solution)/shard_map/reduce_sum | solution.py:236
  452.1 0.9 fusion.19
  (63 shorter events, 5.4 us)
Async XLA Ops:
  0.6 296.9 %copy-start = (bf16[1,768,2048]{2,1,0:T(8,128)(2,1)S(1)}, bf16[1,768,2048]{2,1,0:T(8,128)(2,1)}, u32[]{:S(2)}) copy-start(bf16[1,768,2048]{2,1,0:T(8,128)(2,1)} %param.21) | copy-start | bytes 9437188
  0.6 114.9 %copy-start.7 = (bf16[128,256]{1,0:T(8,128)(2,1)S(1)}, bf16[128,256]{1,0:T(8,128)(2,1)}, u32[]{:S(2)}) copy-start(bf16[128,256]{1,0:T(8,128)(2,1)} %param.13) | copy-start | bytes 196612
  0.7 115.0 %copy-start.8 = (bf16[128,256]{1,0:T(8,128)(2,1)S(1)}, bf16[128,256]{1,0:T(8,128)(2,1)}, u32[]{:S(2)}) copy-start(bf16[128,256]{1,0:T(8,128)(2,1)} %param.14) | copy-start | bytes 196612
  0.7 120.5 %copy-start.10 = (s32[128,8]{0,1:T(8,128)S(1)}, s32[128,8]{0,1:T(8,128)}, u32[]{:S(2)}) copy-start(s32[128,8]{0,1:T(8,128)} %param.22) | copy-start | bytes 12292
  114.6 27.8 %collective-permute-start.2 = (bf16[2048,1024]{1,0:T(8,128)(2,1)}, bf16[2048,1024]{1,0:T(8,128)(2,1)}, u32[]{:S(2)}, u32[]{:S(2)}) collective-permute-start(bf16[2048,1024]{1,0:T(8,128)(2,1)} %bitcast.89), channel_id=1, source_target_pairs={{0,32},{32,0},{64,96},{96,64},{128,160},{160,128},{192,224},{224,1... | collective-permute-start | bytes 12582920 | tf_op jit(solution)/shard_map/ppermute | solution.py:187
  115.8 23.1 %copy-start.9 = (f32[128,16]{0,1:T(8,128)S(1)}, f32[128,16]{0,1:T(8,128)}, u32[]{:S(2)}) copy-start(f32[128,16]{0,1:T(8,128)} %param.16) | copy-start | bytes 24580
  116.5 14.8 %collective-permute-start = (bf16[2,128,256]{1,2,0:T(8,128)(2,1)}, bf16[2,128,256]{1,2,0:T(8,128)(2,1)}, u32[]{:S(2)}, u32[]{:S(2)}) collective-permute-start(bf16[2,128,256]{1,2,0:T(8,128)(2,1)} %pad_maximum_fusion), channel_id=1, source_target_pairs={{0,32},{32,64},{64,96},{96,128},{128,160},{160,192},{192,224},{224... | collective-permute-start | bytes 393224 | tf_op jit(solution)/shard_map/ppermute | solution.py:21
  131.4 5.9 %collective-permute-start.1 = (bf16[2,128,256]{1,2,0:T(8,128)(2,1)}, bf16[2,128,256]{1,2,0:T(8,128)(2,1)S(1)}, u32[]{:S(2)}, u32[]{:S(2)}) collective-permute-start(bf16[2,128,256]{1,2,0:T(8,128)(2,1)} %collective-permute-done), channel_id=1, source_target_pairs={{0,32},{32,64},{64,96},{96,128},{128,160},{160,192},{192,224},{224... | collective-permute-start | bytes 393224 | tf_op jit(solution)/shard_map/ppermute | solution.py:21
  136.2 3.0 copy-start.5
  139.2 2.4 copy-start.1
  139.8 0.8 copy-start.4
  141.6 3.7 copy-start.6
  142.3 3.9 copy-start.11
  145.4 0.8 copy-start.2
  303.7 7.8 %copy-start.12 = (f32[128,8]{0,1:T(8,128)S(1)}, f32[128,8]{0,1:T(8,128)}, u32[]{:S(2)}) copy-start(f32[128,8]{0,1:T(8,128)} %param.23) | copy-start | bytes 12292
  303.7 129.8 %all-to-all-start.1 = ((bf16[32,40,2048]{2,1,0:T(8,128)(2,1)}), bf16[32,40,2048]{2,1,0:T(8,128)(2,1)}, u32[]{:S(2)}, u32[]{:S(2)}) async-start(bf16[32,40,2048]{2,1,0:T(8,128)(2,1)} %bitcast.91), calls=%async_computation.1 | async-start | bytes 10485760 | tf_op jit(solution)/shard_map/all_to_all | solution.py:232
  445.5 6.6 %copy-start.3 = (bf16[128,2048]{1,0:T(8,128)(2,1)S(1)}, bf16[128,2048]{1,0:T(8,128)(2,1)}, u32[]{:S(2)}) copy-start(bf16[128,2048]{1,0:T(8,128)(2,1)} %copy-done.2) | copy-start | bytes 1572868

commit v4 on v3

--- a/solution.py
+++ b/solution.py
@@ -224,12 +224,12 @@
     weight_out = expert_out[0]
     hidden_units = weight_out.shape[0]
     replies = run_expert(
-        lax.all_to_all(outgoing, "ep", split_axis=0, concat_axis=0, tiled=True),
+        exchange(outgoing, True, 1),
         weight_in,
         weight_out,
         hidden_units,
     )
-    returned = lax.all_to_all(replies, "ep", split_axis=0, concat_axis=0, tiled=True)
+    returned = exchange(replies, True, 2)
     picked = returned.reshape(experts_all * capacity, model_width)[slot_ids].reshape(
         local_rows, top_count, model_width
     )

time: 454 us -> 450 us (level)
  the two profiles are of different devices: /device:TPU:129 before, /device:TPU:94 now
where the time goes in v4:
time: 450 us; the launch traced here: 446 us
  Pallas kernels  351 us (78%)
  local copies, waits for them, and re-layouts  33.5 us (7%)
  matrix products  26.4 us (6%)
  other arithmetic  19.8 us (4%)
  blocking collectives  12.8 us (3%)
    pallas_call x3, Pallas kernels, exchange(): pl.pallas_call(functools.partial(exchange_kernel, per_peer), out_shape=ja...  351 us
    all_gather x1, blocking collectives, shards(): column_rows = lax.all_gather(out_proj, 'ctx', axis=0, tiled=True)  12.8 us
    dot_general x1, matrix products, run_expert(): gate_up = jnp.dot(flat_in, weight_in, preferred_element_type=jnp.float32)  12.1 us
    gather x1, local copies, waits for them, and re-layouts, shards(): returned.reshape(experts_all * capacity, model_width)[slot_ids]  12.1 us
    scatter x1, local copies, waits for them, and re-layouts, shards(): outgoing = outgoing.at[slot_ids].set(jnp.repeat(normed, top_count, axis=0...  10.1 us
    another operation x3, other arithmetic  9.14 us
  transfers between devices with their start and end apart: 3, of which 0 were waited for; matrix products, arithmetic and copies ran while one was open for 6% of the time, Pallas kernels for 0%

profile of v4, /device:TPU:94, one launch (start us, length us, event | category | flops | bytes accessed | tf_op | source)
XLA Modules:
  0.0 445.6 jit_solution(16446477957012788415)
XLA Ops:
  0.7 12.8 %all_gather.3 = bf16[64,2048]{1,0:T(8,128)(2,1)S(1)} all-gather(bf16[8,2048]{1,0:T(8,128)(2,1)} %param.18), channel_id=1, replica_groups=mesh['ctx'=8,'ep'=32] {'ctx'}, dimensions={0}, use_global_device_ids=true | all-gather | bytes 294912 | tf_op jit(solution)/shard_map/all_gather | solution.py:184
  13.5 0.7 dynamic-slice_bitcast_fusion.src_ref
  14.2 103.2 %shard_map.131 = bf16[32,64,1024]{2,1,0:T(8,128)(2,1)} custom-call(bf16[1,64,1024]{2,1,0:T(8,128)(2,1)} %dynamic-slice_bitcast_fusion.src_ref), custom_call_target="tpu_custom_call" | custom-call | bytes 8388608 | tf_op jit(solution)/shard_map/pallas_call | solution.py:94
  117.8 0.7 pad_maximum_fusion
  119.2 9.0 %reduce-window.6 = s32[32,8,128]{2,1,0:T(8,128)S(1)} reduce-window(s32[32,8,128]{2,1,0:T(8,128)S(1)} %fusion.28, s32[]{:T(128)} %constant.73.clone.1), window={size=1x1x128 pad=0_0x0_0x127_0}, to_apply=%region_2.3 | reduce-window | flops 4161536 | bytes 262148 | tf_op jit(solution)/shard_map/reduce-window
  128.6 0.7 broadcast_multiply_fusion
  130.0 2.0 copy.39
  131.9 2.3 copy.20
  134.2 0.8 copy.27
  135.1 1.6 fusion.38
  137.7 0.8 copy-done.4
  138.5 0.9 copy.26
  139.4 2.0 copy.33
  141.6 3.2 convolution_dynamic-update-slice_fusion.1
  144.8 2.9 convolution_dynamic-update-slice_fusion
  148.7 1.0 fusion.18
  149.7 10.1 %scatter_custom_fusion = bf16[1280,2048]{1,0:T(8,128)(2,1)} fusion(s32[1024]{0:T(1024)S(1)} %bitcast.109, bf16[]{:T(256)} %constant.86.clone.1, bf16[128,2048]{1,0:T(8,128)(2,1)} %fusion.18), kind=kCustom, calls=%fused_computation.7 | custom fusion | bytes 5767170 | tf_op jit(solution)/shard_map/scatter | solution.py:220
  159.8 125.3 %shard_map.132 = bf16[32,40,2048]{2,1,0:T(8,128)(2,1)} custom-call(bf16[32,40,2048]{2,1,0:T(8,128)(2,1)} %bitcast.89), custom_call_target="tpu_custom_call" | custom-call | bytes 10485760 | tf_op jit(solution)/shard_map/pallas_call | solution.py:94
  285.0 12.1 %fusion.1 = f32[1280,1536]{1,0:T(8,128)S(1)} fusion(bf16[1280,2048]{1,0:T(8,128)(2,1)} %bitcast.92, bf16[1,2048,1536]{2,1,0:T(8,128)(2,1)} %param.20), kind=kOutput, calls=%fused_computation.5 | convolution fusion | flops 8053063680 | bytes 19398656 | tf_op jit(solution)/shard_map/dot_general | solution.py:113
  297.1 6.1 %convolution_convert_fusion = bf16[1280,2048]{1,0:T(8,128)(2,1)} fusion(bf16[1,768,2048]{2,1,0:T(8,128)(2,1)S(1)} %copy-done, f32[1280,1536]{1,0:T(8,128)S(1)} %fusion.1), kind=kOutput, calls=%fused_computation.4 | convolution fusion | flops 4035051520 | bytes 16252928 | tf_op jit(solution)/shard_map/dot_general | solution.py:117
  303.2 122.8 %shard_map.133 = bf16[32,40,2048]{2,1,0:T(8,128)(2,1)} custom-call(bf16[32,40,2048]{2,1,0:T(8,128)(2,1)} %bitcast.93), custom_call_target="tpu_custom_call" | custom-call | bytes 10485760 | tf_op jit(solution)/shard_map/pallas_call | solution.py:94
  426.0 12.1 %gather_fusion = bf16[1024,2048]{1,0:T(8,128)(2,1)} fusion(bf16[1280,2048]{1,0:T(8,128)(2,1)} %bitcast.88, s32[1024]{0:T(1024)S(1)} %broadcast_clamp_fusion), kind=kCustom, calls=%fused_computation | custom fusion | bytes 8392704 | tf_op jit(solution)/shard_map/gather | solution.py:233
  438.1 6.6 %fusion = f32[128,2048]{1,0:T(8,128)S(1)} fusion(bf16[1024,2048]{1,0:T(8,128)(2,1)} %gather_fusion, f32[128,8]{1,0:T(8,128)S(1)} %copy.27), kind=kLoop, calls=%fused_computation.3 | loop fusion | flops 6029312 | bytes 5246976 | tf_op jit(solution)/shard_map/reduce_sum | solution.py:236
  444.7 0.9 fusion.19
  (60 shorter events, 4.0 us)
Async XLA Ops:
  0.6 296.5 %copy-start = (bf16[1,768,2048]{2,1,0:T(8,128)(2,1)S(1)}, bf16[1,768,2048]{2,1,0:T(8,128)(2,1)}, u32[]{:S(2)}) copy-start(bf16[1,768,2048]{2,1,0:T(8,128)(2,1)} %param.21) | copy-start | bytes 9437188
  0.6 116.9 %copy-start.7 = (bf16[128,256]{1,0:T(8,128)(2,1)S(1)}, bf16[128,256]{1,0:T(8,128)(2,1)}, u32[]{:S(2)}) copy-start(bf16[128,256]{1,0:T(8,128)(2,1)} %param.13) | copy-start | bytes 196612
  0.7 117.0 %copy-start.8 = (bf16[128,256]{1,0:T(8,128)(2,1)S(1)}, bf16[128,256]{1,0:T(8,128)(2,1)}, u32[]{:S(2)}) copy-start(bf16[128,256]{1,0:T(8,128)(2,1)} %param.14) | copy-start | bytes 196612
  0.7 118.3 %copy-start.10 = (s32[128,8]{0,1:T(8,128)S(1)}, s32[128,8]{0,1:T(8,128)}, u32[]{:S(2)}) copy-start(s32[128,8]{0,1:T(8,128)} %param.22) | copy-start | bytes 12292
  117.4 27.4 %collective-permute-start.2 = (bf16[2048,1024]{1,0:T(8,128)(2,1)}, bf16[2048,1024]{1,0:T(8,128)(2,1)}, u32[]{:S(2)}, u32[]{:S(2)}) collective-permute-start(bf16[2048,1024]{1,0:T(8,128)(2,1)} %bitcast.90), channel_id=1, source_target_pairs={{0,32},{32,0},{64,96},{96,64},{128,160},{160,128},{192,224},{224,1... | collective-permute-start | bytes 12582920 | tf_op jit(solution)/shard_map/ppermute | solution.py:187
  117.8 19.0 %copy-start.9 = (f32[128,16]{0,1:T(8,128)S(1)}, f32[128,16]{0,1:T(8,128)}, u32[]{:S(2)}) copy-start(f32[128,16]{0,1:T(8,128)} %param.16) | copy-start | bytes 24580
  118.4 11.4 %collective-permute-start = (bf16[2,128,256]{1,2,0:T(8,128)(2,1)}, bf16[2,128,256]{1,2,0:T(8,128)(2,1)S(1)}, u32[]{:S(2)}, u32[]{:S(2)}) collective-permute-start(bf16[2,128,256]{1,2,0:T(8,128)(2,1)} %pad_maximum_fusion), channel_id=1, source_target_pairs={{0,32},{32,64},{64,96},{96,128},{128,160},{160,192},{192,224},{224... | collective-permute-start | bytes 393224 | tf_op jit(solution)/shard_map/ppermute | solution.py:21
  129.8 5.2 %collective-permute-start.1 = (bf16[2,128,256]{1,2,0:T(8,128)(2,1)S(1)}, bf16[2,128,256]{1,2,0:T(8,128)(2,1)S(1)}, u32[]{:S(2)}, u32[]{:S(2)}) collective-permute-start(bf16[2,128,256]{1,2,0:T(8,128)(2,1)S(1)} %collective-permute-done), channel_id=1, source_target_pairs={{0,32},{32,64},{64,96},{96,128},{128,160},{160,192},{192,224},{224... | collective-permute-start | bytes 393224 | tf_op jit(solution)/shard_map/ppermute | solution.py:21
  135.0 2.1 copy-start.5
  137.7 0.8 copy-start.4
  141.5 3.3 copy-start.3
  141.6 6.2 %copy-start.6 = (bf16[128,2048]{1,0:T(8,128)(2,1)S(1)}, bf16[128,2048]{1,0:T(8,128)(2,1)}, u32[]{:S(2)}) copy-start(bf16[128,2048]{1,0:T(8,128)(2,1)} %param.17) | copy-start | bytes 1572868
  144.8 3.9 copy-start.11
  147.9 0.8 copy-start.1
  438.1 6.6 %copy-start.2 = (bf16[128,2048]{1,0:T(8,128)(2,1)S(1)}, bf16[128,2048]{1,0:T(8,128)(2,1)}, u32[]{:S(2)}) copy-start(bf16[128,2048]{1,0:T(8,128)(2,1)} %copy-done.1) | copy-start | bytes 1572868

commit v5 on v4

--- a/solution.py
+++ b/solution.py
@@ -21,7 +21,7 @@
     return lax.ppermute(shard, axis, [(i, (i + by) % devices) for i in range(devices)])
 
 
-def exchange_kernel(per_peer, src_ref, dst_ref, send_sem, recv_sem, local_sem):
+def exchange_kernel(per_peer, src_ref, out_ref, dst_ref, send_sem, recv_sem, local_sem):
     n_ep = lax.axis_size("ep")
     n_ctx = lax.axis_size("ctx")
     me = lax.axis_index("ep")
@@ -85,6 +85,9 @@
 
     lax.fori_loop(1, n_ep, finish, 0)
     local.wait()
+    flush = pltpu.make_async_copy(dst_ref, out_ref, local_sem)
+    flush.start()
+    flush.wait()
 
 
 def exchange(src, per_peer, collective_id):
@@ -94,9 +97,10 @@
     return pl.pallas_call(
         functools.partial(exchange_kernel, per_peer),
         out_shape=jax.ShapeDtypeStruct((n_ep,) + block, src.dtype),
-        in_specs=[pl.BlockSpec(memory_space=pl.ANY)],
+        in_specs=[pl.BlockSpec(memory_space=pltpu.VMEM)],
         out_specs=pl.BlockSpec(memory_space=pl.ANY),
         scratch_shapes=[
+            pltpu.VMEM((n_ep,) + block, src.dtype),
             pltpu.SemaphoreType.DMA((n_ep,)),
             pltpu.SemaphoreType.DMA((n_ep,)),
             pltpu.SemaphoreType.DMA,

time: 450 us -> 462 us (1.027)
  Pallas kernels: 351 us -> 363 us
    pallas_call x3, Pallas kernels: 351 us -> 363 us  [exchange(): pl.pallas_call(functools.partial(exchange_kernel, per_peer), out_shape=ja...]
where the time goes in v5:
time: 462 us; the launch traced here: 457 us
  Pallas kernels  363 us (79%)
  local copies, waits for them, and re-layouts  33.5 us (7%)
  matrix products  26.4 us (6%)
  other arithmetic  19.8 us (4%)
  blocking collectives  12.8 us (3%)
    pallas_call x3, Pallas kernels, exchange(): pl.pallas_call(functools.partial(exchange_kernel, per_peer), out_shape=ja...  363 us
    all_gather x1, blocking collectives, shards(): column_rows = lax.all_gather(out_proj, 'ctx', axis=0, tiled=True)  12.8 us
    dot_general x1, matrix products, run_expert(): gate_up = jnp.dot(flat_in, weight_in, preferred_element_type=jnp.float32)  12.1 us
    gather x1, local copies, waits for them, and re-layouts, shards(): returned.reshape(experts_all * capacity, model_width)[slot_ids]  12.1 us
    scatter x1, local copies, waits for them, and re-layouts, shards(): outgoing = outgoing.at[slot_ids].set(jnp.repeat(normed, top_count, axis=0...  10.1 us
  transfers between devices with their start and end apart: 3, of which 0 were waited for; matrix products, arithmetic and copies ran while one was open for 6% of the time, Pallas kernels for 0%

profile of v5, /device:TPU:94, one launch (start us, length us, event | category | flops | bytes accessed | tf_op | source)
XLA Modules:
  0.0 457.2 jit_solution(18430713643990530988)
XLA Ops:
  0.7 12.8 %all_gather.3 = bf16[64,2048]{1,0:T(8,128)(2,1)S(1)} all-gather(bf16[8,2048]{1,0:T(8,128)(2,1)} %param.18), channel_id=1, replica_groups=mesh['ctx'=8,'ep'=32] {'ctx'}, dimensions={0}, use_global_device_ids=true | all-gather | bytes 294912 | tf_op jit(solution)/shard_map/all_gather | solution.py:188
  13.5 0.7 dynamic-slice_bitcast_fusion.src_ref
  14.2 105.8 %shard_map.131 = bf16[32,64,1024]{2,1,0:T(8,128)(2,1)} custom-call(bf16[1,64,1024]{2,1,0:T(8,128)(2,1)} %dynamic-slice_bitcast_fusion.src_ref), custom_call_target="tpu_custom_call" | custom-call | bytes 8388608 | tf_op jit(solution)/shard_map/pallas_call | solution.py:97
  120.4 0.7 pad_maximum_fusion
  121.8 9.0 %reduce-window.6 = s32[32,8,128]{2,1,0:T(8,128)S(1)} reduce-window(s32[32,8,128]{2,1,0:T(8,128)S(1)} %fusion.28, s32[]{:T(128)} %constant.73.clone.1), window={size=1x1x128 pad=0_0x0_0x127_0}, to_apply=%region_2.3 | reduce-window | flops 4161536 | bytes 262148 | tf_op jit(solution)/shard_map/reduce-window
  131.2 0.7 broadcast_multiply_fusion
  132.6 2.0 copy.39
  134.5 2.3 copy.20
  136.8 0.8 copy.27
  137.7 1.6 fusion.38
  140.3 0.8 copy-done.4
  141.1 0.9 copy.26
  142.1 2.0 copy.33
  144.2 3.2 convolution_dynamic-update-slice_fusion.1
  147.4 2.9 convolution_dynamic-update-slice_fusion
  151.3 1.0 fusion.18
  152.3 10.1 %scatter_custom_fusion = bf16[1280,2048]{1,0:T(8,128)(2,1)} fusion(s32[1024]{0:T(1024)S(1)} %bitcast.109, bf16[]{:T(256)} %constant.86.clone.1, bf16[128,2048]{1,0:T(8,128)(2,1)} %fusion.18), kind=kCustom, calls=%fused_computation.7 | custom fusion | bytes 5767170 | tf_op jit(solution)/shard_map/scatter | solution.py:224
  162.4 129.6 %shard_map.132 = bf16[32,40,2048]{2,1,0:T(8,128)(2,1)} custom-call(bf16[32,40,2048]{2,1,0:T(8,128)(2,1)} %bitcast.89), custom_call_target="tpu_custom_call" | custom-call | bytes 10485760 | tf_op jit(solution)/shard_map/pallas_call | solution.py:97
  292.0 12.1 %fusion.1 = f32[1280,1536]{1,0:T(8,128)S(1)} fusion(bf16[1280,2048]{1,0:T(8,128)(2,1)} %bitcast.92, bf16[1,2048,1536]{2,1,0:T(8,128)(2,1)} %param.20), kind=kOutput, calls=%fused_computation.5 | convolution fusion | flops 8053063680 | bytes 19398656 | tf_op jit(solution)/shard_map/dot_general | solution.py:117
  304.1 6.1 %convolution_convert_fusion = bf16[1280,2048]{1,0:T(8,128)(2,1)} fusion(bf16[1,768,2048]{2,1,0:T(8,128)(2,1)S(1)} %copy-done, f32[1280,1536]{1,0:T(8,128)S(1)} %fusion.1), kind=kOutput, calls=%fused_computation.4 | convolution fusion | flops 4035051520 | bytes 16252928 | tf_op jit(solution)/shard_map/dot_general | solution.py:121
  310.2 127.5 %shard_map.133 = bf16[32,40,2048]{2,1,0:T(8,128)(2,1)} custom-call(bf16[32,40,2048]{2,1,0:T(8,128)(2,1)} %bitcast.93), custom_call_target="tpu_custom_call" | custom-call | bytes 10485760 | tf_op jit(solution)/shard_map/pallas_call | solution.py:97
  437.6 12.1 %gather_fusion = bf16[1024,2048]{1,0:T(8,128)(2,1)} fusion(bf16[1280,2048]{1,0:T(8,128)(2,1)} %bitcast.88, s32[1024]{0:T(1024)S(1)} %broadcast_clamp_fusion), kind=kCustom, calls=%fused_computation | custom fusion | bytes 8392704 | tf_op jit(solution)/shard_map/gather | solution.py:237
  449.7 6.6 %fusion = f32[128,2048]{1,0:T(8,128)S(1)} fusion(bf16[1024,2048]{1,0:T(8,128)(2,1)} %gather_fusion, f32[128,8]{1,0:T(8,128)S(1)} %copy.27), kind=kLoop, calls=%fused_computation.3 | loop fusion | flops 6029312 | bytes 5246976 | tf_op jit(solution)/shard_map/reduce_sum | solution.py:240
  456.3 0.9 fusion.19
  (60 shorter events, 4.0 us)
Async XLA Ops:
  0.6 303.4 %copy-start = (bf16[1,768,2048]{2,1,0:T(8,128)(2,1)S(1)}, bf16[1,768,2048]{2,1,0:T(8,128)(2,1)}, u32[]{:S(2)}) copy-start(bf16[1,768,2048]{2,1,0:T(8,128)(2,1)} %param.21) | copy-start | bytes 9437188
  0.6 119.5 %copy-start.7 = (bf16[128,256]{1,0:T(8,128)(2,1)S(1)}, bf16[128,256]{1,0:T(8,128)(2,1)}, u32[]{:S(2)}) copy-start(bf16[128,256]{1,0:T(8,128)(2,1)} %param.13) | copy-start | bytes 196612
  0.7 119.6 %copy-start.8 = (bf16[128,256]{1,0:T(8,128)(2,1)S(1)}, bf16[128,256]{1,0:T(8,128)(2,1)}, u32[]{:S(2)}) copy-start(bf16[128,256]{1,0:T(8,128)(2,1)} %param.14) | copy-start | bytes 196612
  0.7 120.9 %copy-start.10 = (s32[128,8]{0,1:T(8,128)S(1)}, s32[128,8]{0,1:T(8,128)}, u32[]{:S(2)}) copy-start(s32[128,8]{0,1:T(8,128)} %param.22) | copy-start | bytes 12292
  120.0 27.4 %collective-permute-start.2 = (bf16[2048,1024]{1,0:T(8,128)(2,1)}, bf16[2048,1024]{1,0:T(8,128)(2,1)}, u32[]{:S(2)}, u32[]{:S(2)}) collective-permute-start(bf16[2048,1024]{1,0:T(8,128)(2,1)} %bitcast.90), channel_id=1, source_target_pairs={{0,32},{32,0},{64,96},{96,64},{128,160},{160,128},{192,224},{224,1... | collective-permute-start | bytes 12582920 | tf_op jit(solution)/shard_map/ppermute | solution.py:191
  120.4 19.0 %copy-start.9 = (f32[128,16]{0,1:T(8,128)S(1)}, f32[128,16]{0,1:T(8,128)}, u32[]{:S(2)}) copy-start(f32[128,16]{0,1:T(8,128)} %param.16) | copy-start | bytes 24580
  121.0 11.4 %collective-permute-start = (bf16[2,128,256]{1,2,0:T(8,128)(2,1)}, bf16[2,128,256]{1,2,0:T(8,128)(2,1)S(1)}, u32[]{:S(2)}, u32[]{:S(2)}) collective-permute-start(bf16[2,128,256]{1,2,0:T(8,128)(2,1)} %pad_maximum_fusion), channel_id=1, source_target_pairs={{0,32},{32,64},{64,96},{96,128},{128,160},{160,192},{192,224},{224... | collective-permute-start | bytes 393224 | tf_op jit(solution)/shard_map/ppermute | solution.py:21
  132.4 5.2 %collective-permute-start.1 = (bf16[2,128,256]{1,2,0:T(8,128)(2,1)S(1)}, bf16[2,128,256]{1,2,0:T(8,128)(2,1)S(1)}, u32[]{:S(2)}, u32[]{:S(2)}) collective-permute-start(bf16[2,128,256]{1,2,0:T(8,128)(2,1)S(1)} %collective-permute-done), channel_id=1, source_target_pairs={{0,32},{32,64},{64,96},{96,128},{128,160},{160,192},{192,224},{224... | collective-permute-start | bytes 393224 | tf_op jit(solution)/shard_map/ppermute | solution.py:21
  137.6 2.1 copy-start.5
  140.3 0.8 copy-start.4
  144.1 3.3 copy-start.3
  144.2 6.2 %copy-start.6 = (bf16[128,2048]{1,0:T(8,128)(2,1)S(1)}, bf16[128,2048]{1,0:T(8,128)(2,1)}, u32[]{:S(2)}) copy-start(bf16[128,2048]{1,0:T(8,128)(2,1)} %param.17) | copy-start | bytes 1572868
  147.4 3.9 copy-start.11
  150.5 0.8 copy-start.1
  449.7 6.6 %copy-start.2 = (bf16[128,2048]{1,0:T(8,128)(2,1)S(1)}, bf16[128,2048]{1,0:T(8,128)(2,1)}, u32[]{:S(2)}) copy-start(bf16[128,2048]{1,0:T(8,128)(2,1)} %copy-done.1) | copy-start | bytes 1572868

commit v6 on v4

--- a/solution.py
+++ b/solution.py
@@ -28,8 +28,10 @@
     ctx_me = lax.axis_index("ctx")
     ctx_far = (ctx_me + n_ctx // 2) % n_ctx
 
+    core = ctx_me % 2
+
     def peer(j):
-        p = (me + j) % n_ep
+        p = (me + j + core * (n_ep - 2 * j)) % n_ep
         same = 1 - (p + me) % 2
         return p, same * ctx_me + (1 - same) * ctx_far
 

time: 450 us -> 445 us (0.989)
  Pallas kernels: 351 us -> 346 us
    pallas_call x3, Pallas kernels: 351 us -> 346 us  [exchange(): pl.pallas_call(functools.partial(exchange_kernel, per_peer), out_shape=ja...]
where the time goes in v6:
time: 445 us; the launch traced here: 440 us
  Pallas kernels  346 us (78%)
  local copies, waits for them, and re-layouts  33.5 us (8%)
  matrix products  26.4 us (6%)
  other arithmetic  19.8 us (4%)
  blocking collectives  12.8 us (3%)
    pallas_call x3, Pallas kernels, exchange(): pl.pallas_call(functools.partial(exchange_kernel, per_peer), out_shape=ja...  346 us
    all_gather x1, blocking collectives, shards(): column_rows = lax.all_gather(out_proj, 'ctx', axis=0, tiled=True)  12.8 us
    dot_general x1, matrix products, run_expert(): gate_up = jnp.dot(flat_in, weight_in, preferred_element_type=jnp.float32)  12.1 us
    gather x1, local copies, waits for them, and re-layouts, shards(): returned.reshape(experts_all * capacity, model_width)[slot_ids]  12.1 us
    scatter x1, local copies, waits for them, and re-layouts, shards(): outgoing = outgoing.at[slot_ids].set(jnp.repeat(normed, top_count, axis=0...  10.1 us
    another operation x3, other arithmetic  9.14 us
  transfers between devices with their start and end apart: 3, of which 0 were waited for; matrix products, arithmetic and copies ran while one was open for 6% of the time, Pallas kernels for 0%

profile of v6, /device:TPU:94, one launch (start us, length us, event | category | flops | bytes accessed | tf_op | source)
XLA Modules:
  0.0 440.2 jit_solution(13826888086852421845)
XLA Ops:
  0.7 12.8 %all_gather.3 = bf16[64,2048]{1,0:T(8,128)(2,1)S(1)} all-gather(bf16[8,2048]{1,0:T(8,128)(2,1)} %param.18), channel_id=1, replica_groups=mesh['ctx'=8,'ep'=32] {'ctx'}, dimensions={0}, use_global_device_ids=true | all-gather | bytes 294912 | tf_op jit(solution)/shard_map/all_gather | solution.py:186
  13.5 0.7 dynamic-slice_bitcast_fusion.src_ref
  14.2 101.2 %shard_map.131 = bf16[32,64,1024]{2,1,0:T(8,128)(2,1)} custom-call(bf16[1,64,1024]{2,1,0:T(8,128)(2,1)} %dynamic-slice_bitcast_fusion.src_ref), custom_call_target="tpu_custom_call" | custom-call | bytes 8388608 | tf_op jit(solution)/shard_map/pallas_call | solution.py:96
  115.7 0.7 pad_maximum_fusion
  117.2 9.0 %reduce-window.6 = s32[32,8,128]{2,1,0:T(8,128)S(1)} reduce-window(s32[32,8,128]{2,1,0:T(8,128)S(1)} %fusion.28, s32[]{:T(128)} %constant.73.clone.1), window={size=1x1x128 pad=0_0x0_0x127_0}, to_apply=%region_2.3 | reduce-window | flops 4161536 | bytes 262148 | tf_op jit(solution)/shard_map/reduce-window
  126.6 0.7 broadcast_multiply_fusion
  127.9 2.0 copy.39
  129.9 2.3 copy.20
  132.2 0.8 copy.27
  133.1 1.6 fusion.38
  135.7 0.8 copy-done.4
  136.5 0.9 copy.26
  137.4 2.0 copy.33
  139.6 3.2 convolution_dynamic-update-slice_fusion.1
  142.8 2.9 convolution_dynamic-update-slice_fusion
  146.7 1.0 fusion.18
  147.7 10.1 %scatter_custom_fusion = bf16[1280,2048]{1,0:T(8,128)(2,1)} fusion(s32[1024]{0:T(1024)S(1)} %bitcast.109, bf16[]{:T(256)} %constant.86.clone.1, bf16[128,2048]{1,0:T(8,128)(2,1)} %fusion.18), kind=kCustom, calls=%fused_computation.7 | custom fusion | bytes 5767170 | tf_op jit(solution)/shard_map/scatter | solution.py:222
  157.7 122.4 %shard_map.132 = bf16[32,40,2048]{2,1,0:T(8,128)(2,1)} custom-call(bf16[32,40,2048]{2,1,0:T(8,128)(2,1)} %bitcast.89), custom_call_target="tpu_custom_call" | custom-call | bytes 10485760 | tf_op jit(solution)/shard_map/pallas_call | solution.py:96
  280.1 12.1 %fusion.1 = f32[1280,1536]{1,0:T(8,128)S(1)} fusion(bf16[1280,2048]{1,0:T(8,128)(2,1)} %bitcast.92, bf16[1,2048,1536]{2,1,0:T(8,128)(2,1)} %param.20), kind=kOutput, calls=%fused_computation.5 | convolution fusion | flops 8053063680 | bytes 19398656 | tf_op jit(solution)/shard_map/dot_general | solution.py:115
  292.2 6.1 %convolution_convert_fusion = bf16[1280,2048]{1,0:T(8,128)(2,1)} fusion(bf16[1,768,2048]{2,1,0:T(8,128)(2,1)S(1)} %copy-done, f32[1280,1536]{1,0:T(8,128)S(1)} %fusion.1), kind=kOutput, calls=%fused_computation.4 | convolution fusion | flops 4035051520 | bytes 16252928 | tf_op jit(solution)/shard_map/dot_general | solution.py:119
  298.3 122.4 %shard_map.133 = bf16[32,40,2048]{2,1,0:T(8,128)(2,1)} custom-call(bf16[32,40,2048]{2,1,0:T(8,128)(2,1)} %bitcast.93), custom_call_target="tpu_custom_call" | custom-call | bytes 10485760 | tf_op jit(solution)/shard_map/pallas_call | solution.py:96
  420.7 12.1 %gather_fusion = bf16[1024,2048]{1,0:T(8,128)(2,1)} fusion(bf16[1280,2048]{1,0:T(8,128)(2,1)} %bitcast.88, s32[1024]{0:T(1024)S(1)} %broadcast_clamp_fusion), kind=kCustom, calls=%fused_computation | custom fusion | bytes 8392704 | tf_op jit(solution)/shard_map/gather | solution.py:235
  432.7 6.6 %fusion = f32[128,2048]{1,0:T(8,128)S(1)} fusion(bf16[1024,2048]{1,0:T(8,128)(2,1)} %gather_fusion, f32[128,8]{1,0:T(8,128)S(1)} %copy.27), kind=kLoop, calls=%fused_computation.3 | loop fusion | flops 6029312 | bytes 5246976 | tf_op jit(solution)/shard_map/reduce_sum | solution.py:238
  439.3 0.9 fusion.19
  (60 shorter events, 4.0 us)
Async XLA Ops:
  0.6 291.5 %copy-start = (bf16[1,768,2048]{2,1,0:T(8,128)(2,1)S(1)}, bf16[1,768,2048]{2,1,0:T(8,128)(2,1)}, u32[]{:S(2)}) copy-start(bf16[1,768,2048]{2,1,0:T(8,128)(2,1)} %param.21) | copy-start | bytes 9437188
  0.6 114.8 %copy-start.7 = (bf16[128,256]{1,0:T(8,128)(2,1)S(1)}, bf16[128,256]{1,0:T(8,128)(2,1)}, u32[]{:S(2)}) copy-start(bf16[128,256]{1,0:T(8,128)(2,1)} %param.13) | copy-start | bytes 196612
  0.7 115.0 %copy-start.8 = (bf16[128,256]{1,0:T(8,128)(2,1)S(1)}, bf16[128,256]{1,0:T(8,128)(2,1)}, u32[]{:S(2)}) copy-start(bf16[128,256]{1,0:T(8,128)(2,1)} %param.14) | copy-start | bytes 196612
  0.7 116.2 %copy-start.10 = (s32[128,8]{0,1:T(8,128)S(1)}, s32[128,8]{0,1:T(8,128)}, u32[]{:S(2)}) copy-start(s32[128,8]{0,1:T(8,128)} %param.22) | copy-start | bytes 12292
  115.4 27.4 %collective-permute-start.2 = (bf16[2048,1024]{1,0:T(8,128)(2,1)}, bf16[2048,1024]{1,0:T(8,128)(2,1)}, u32[]{:S(2)}, u32[]{:S(2)}) collective-permute-start(bf16[2048,1024]{1,0:T(8,128)(2,1)} %bitcast.90), channel_id=1, source_target_pairs={{0,32},{32,0},{64,96},{96,64},{128,160},{160,128},{192,224},{224,1... | collective-permute-start | bytes 12582920 | tf_op jit(solution)/shard_map/ppermute | solution.py:189
  115.7 19.0 %copy-start.9 = (f32[128,16]{0,1:T(8,128)S(1)}, f32[128,16]{0,1:T(8,128)}, u32[]{:S(2)}) copy-start(f32[128,16]{0,1:T(8,128)} %param.16) | copy-start | bytes 24580
  116.4 11.4 %collective-permute-start = (bf16[2,128,256]{1,2,0:T(8,128)(2,1)}, bf16[2,128,256]{1,2,0:T(8,128)(2,1)S(1)}, u32[]{:S(2)}, u32[]{:S(2)}) collective-permute-start(bf16[2,128,256]{1,2,0:T(8,128)(2,1)} %pad_maximum_fusion), channel_id=1, source_target_pairs={{0,32},{32,64},{64,96},{96,128},{128,160},{160,192},{192,224},{224... | collective-permute-start | bytes 393224 | tf_op jit(solution)/shard_map/ppermute | solution.py:21
  127.8 5.2 %collective-permute-start.1 = (bf16[2,128,256]{1,2,0:T(8,128)(2,1)S(1)}, bf16[2,128,256]{1,2,0:T(8,128)(2,1)S(1)}, u32[]{:S(2)}, u32[]{:S(2)}) collective-permute-start(bf16[2,128,256]{1,2,0:T(8,128)(2,1)S(1)} %collective-permute-done), channel_id=1, source_target_pairs={{0,32},{32,64},{64,96},{96,128},{128,160},{160,192},{192,224},{224... | collective-permute-start | bytes 393224 | tf_op jit(solution)/shard_map/ppermute | solution.py:21
  133.0 2.1 copy-start.5
  135.6 0.8 copy-start.4
  139.5 3.3 copy-start.3
  139.6 6.2 %copy-start.6 = (bf16[128,2048]{1,0:T(8,128)(2,1)S(1)}, bf16[128,2048]{1,0:T(8,128)(2,1)}, u32[]{:S(2)}) copy-start(bf16[128,2048]{1,0:T(8,128)(2,1)} %param.17) | copy-start | bytes 1572868
  142.7 3.9 copy-start.11
  145.8 0.8 copy-start.1
  432.7 6.6 %copy-start.2 = (bf16[128,2048]{1,0:T(8,128)(2,1)S(1)}, bf16[128,2048]{1,0:T(8,128)(2,1)}, u32[]{:S(2)}) copy-start(bf16[128,2048]{1,0:T(8,128)(2,1)} %copy-done.1) | copy-start | bytes 1572868

commit v7 on v6

--- a/solution.py
+++ b/solution.py
@@ -211,15 +211,20 @@
         local_rows // 4, top_count * ((local_rows + experts_all - 2) // (experts_all - 1))
     )
     flat_ids = expert_ids.reshape(-1)
+    picks = flat_ids.shape[0]
     one_hot = (flat_ids[:, None] == jnp.arange(experts_all, dtype=jnp.int32)[None, :]).astype(
-        jnp.int32
-    )
-    earlier = jnp.cumsum(one_hot, axis=0) - one_hot
-    slot_ids = flat_ids * capacity + jnp.sum(earlier * one_hot, axis=1)
-    outgoing = jnp.zeros((experts_all * capacity, model_width), jnp.bfloat16)
+        jnp.bfloat16
+    )
+    pick_pos = jnp.arange(picks, dtype=jnp.int32)
+    before = (pick_pos[None, :] < pick_pos[:, None]).astype(jnp.bfloat16)
+    earlier = jnp.dot(before, one_hot, preferred_element_type=jnp.float32)
+    rank = jnp.sum(earlier * one_hot.astype(jnp.float32), axis=1).astype(jnp.int32)
+    slot_ids = (flat_ids * capacity + rank).reshape(local_rows, top_count)
+    slot_pos = jnp.arange(experts_all * capacity, dtype=jnp.int32)
+    take = jnp.any(slot_ids[None, :, :] == slot_pos[:, None, None], axis=2).astype(jnp.bfloat16)
     outgoing = (
-        outgoing.at[slot_ids]
-        .set(jnp.repeat(normed, top_count, axis=0))
+        jnp.dot(take, normed, preferred_element_type=jnp.float32)
+        .astype(jnp.bfloat16)
         .reshape(experts_all, capacity, model_width)
     )
     weight_in = expert_in[0]
@@ -232,10 +237,18 @@
         hidden_units,
     )
     returned = exchange(replies, True, 2)
-    picked = returned.reshape(experts_all * capacity, model_width)[slot_ids].reshape(
-        local_rows, top_count, model_width
-    )
-    combined = jnp.sum(route_weight[:, :, None] * picked.astype(jnp.float32), axis=1)
+    spread = jnp.sum(
+        jnp.where(
+            slot_ids[:, :, None] == slot_pos[None, None, :], route_weight[:, :, None], 0.0
+        ),
+        axis=1,
+    )
+    combined = jnp.dot(
+        spread,
+        returned.reshape(experts_all * capacity, model_width).astype(jnp.float32),
+        precision=lax.Precision.HIGHEST,
+        preferred_element_type=jnp.float32,
+    )
     layer_out = (state_f + combined).astype(jnp.bfloat16)
     return (layer_out, attended)
 

time: 445 us -> 423 us (0.951)
  local copies, waits for them, and re-layouts: 33.5 us -> 10.7 us
  other arithmetic: 19.8 us -> 8.61 us
  matrix products: 26.4 us -> 36.9 us
    gather x1 -> x0, local copies, waits for them, and re-layouts: 12.1 us -> none  [shards(): returned.reshape(experts_all * capacity, model_width)[slot_ids]]
    dot_general x0 -> x3, matrix products: none -> 10.3 us  [the longest x1 5.85 us: shards(): jnp.dot(spread, returned.reshape(experts_all * capacity, model_width).ast...]
    scatter x1 -> x0, local copies, waits for them, and re-layouts: 10.1 us -> none  [shards(): outgoing = outgoing.at[slot_ids].set(jnp.repeat(normed, top_count, axis=0...]
    another operation x3 -> x0, other arithmetic: 9.14 us -> none
    reduce_or x0 -> x1, other arithmetic: none -> 4.64 us  [shards(): jnp.any(slot_ids[None, :, :] == slot_pos[:, None, None], axis=2)]
  transfers between devices with their start and end apart: 3 -> 3, of which waited for: 0 -> 1; matrix products, arithmetic and copies ran while one was open for 6% -> 6% of each run, Pallas kernels for 0% -> 0%
where the time goes in v7:
time: 423 us; the launch traced here: 418 us
  Pallas kernels  345 us (82%)
  matrix products  36.9 us (9%)
  blocking collectives  12.8 us (3%)
  local copies, waits for them, and re-layouts  10.7 us (3%)
  other arithmetic  8.61 us (2%)
    pallas_call x3, Pallas kernels, exchange(): pl.pallas_call(functools.partial(exchange_kernel, per_peer), out_shape=ja...  345 us
    all_gather x1, blocking collectives, shards(): column_rows = lax.all_gather(out_proj, 'ctx', axis=0, tiled=True)  12.8 us
    dot_general x1, matrix products, run_expert(): gate_up = jnp.dot(flat_in, weight_in, preferred_element_type=jnp.float32)  12.1 us
  transfers between devices with their start and end apart: 3, of which 1 were waited for; matrix products, arithmetic and copies ran while one was open for 6% of the time, Pallas kernels for 0%

profile of v7, /device:TPU:94, one launch (start us, length us, event | category | flops | bytes accessed | tf_op | source)
XLA Modules:
  0.0 417.7 jit_solution(7978668630790889900)
XLA Ops:
  0.7 12.8 %all_gather.3 = bf16[64,2048]{1,0:T(8,128)(2,1)S(1)} all-gather(bf16[8,2048]{1,0:T(8,128)(2,1)} %param.18), channel_id=1, replica_groups=mesh['ctx'=8,'ep'=32] {'ctx'}, dimensions={0}, use_global_device_ids=true | all-gather | bytes 294912 | tf_op jit(solution)/shard_map/all_gather | solution.py:186
  13.5 0.7 dynamic-slice_bitcast_fusion.src_ref
  14.2 101.2 %shard_map.131 = bf16[32,64,1024]{2,1,0:T(8,128)(2,1)} custom-call(bf16[1,64,1024]{2,1,0:T(8,128)(2,1)} %dynamic-slice_bitcast_fusion.src_ref), custom_call_target="tpu_custom_call" | custom-call | bytes 8388608 | tf_op jit(solution)/shard_map/pallas_call | solution.py:96
  115.7 0.7 pad_maximum_fusion
  117.1 0.5 fusion.15
  118.1 2.5 select_reduce_fusion
  120.7 2.0 collective-permute-done
  123.0 4.6 %fusion.2 = pred[1280,128]{1,0:T(8,128)(4,1)S(1)} fusion(s32[128,8]{0,1:T(8,128)S(1)} %multiply_add_fusion), kind=kLoop, calls=%fused_computation.7 | loop fusion | flops 2457600 | bytes 167936 | tf_op jit(solution)/shard_map/reduce_or | solution.py:224
  127.7 2.0 copy.64
  129.6 2.3 copy.47
  132.0 1.0 constant_dynamic-update-slice_fusion
  133.0 1.6 fusion.38
  135.0 0.5 fusion.13
  135.5 0.8 copy-done.3
  136.4 0.9 copy.53
  137.3 2.0 copy.58
  139.5 3.1 convolution_dynamic-update-slice_fusion.1
  142.6 2.9 convolution_dynamic-update-slice_fusion
  145.9 3.9 convolution_convert_fusion.1
  149.9 121.6 %shard_map.132 = bf16[32,40,2048]{2,1,0:T(8,128)(2,1)} custom-call(bf16[32,40,2048]{2,1,0:T(8,128)(2,1)} %bitcast.65), custom_call_target="tpu_custom_call" | custom-call | bytes 10485760 | tf_op jit(solution)/shard_map/pallas_call | solution.py:96
  271.4 12.1 %fusion = f32[1280,1536]{1,0:T(8,128)S(1)} fusion(bf16[1280,2048]{1,0:T(8,128)(2,1)} %bitcast.69, bf16[1,2048,1536]{2,1,0:T(8,128)(2,1)} %param.20), kind=kOutput, calls=%fused_computation.2 | convolution fusion | flops 8053063680 | bytes 19398656 | tf_op jit(solution)/shard_map/dot_general | solution.py:115
  283.5 6.3 %convolution_convert_fusion = bf16[1280,2048]{1,0:T(8,128)(2,1)} fusion(bf16[1,768,2048]{2,1,0:T(8,128)(2,1)S(1)} %copy-done, f32[1280,1536]{1,0:T(8,128)S(1)} %fusion), kind=kOutput, calls=%fused_computation | convolution fusion | flops 4035051520 | bytes 16252928 | tf_op jit(solution)/shard_map/dot_general | solution.py:119
  289.8 122.0 %shard_map.133 = bf16[32,40,2048]{2,1,0:T(8,128)(2,1)} custom-call(bf16[32,40,2048]{2,1,0:T(8,128)(2,1)} %bitcast.70), custom_call_target="tpu_custom_call" | custom-call | bytes 10485760 | tf_op jit(solution)/shard_map/pallas_call | solution.py:96
  411.9 5.8 %fusion.6 = bf16[128,2048]{1,0:T(8,128)(2,1)} fusion(f32[128,1280]{1,0:T(8,128)} %select_reduce_fusion, bf16[1280,2048]{1,0:T(8,128)(2,1)} %bitcast.66, bf16[128,2048]{1,0:T(8,128)(2,1)} %copy-done.1), kind=kOutput, calls=%fused_computation.14 | convolution fusion | flops 4027318272 | bytes 6946816 | tf_op jit(solution)/shard_map/dot_general | solution.py:246
  (50 shorter events, 2.7 us)
Async XLA Ops:
  0.6 282.9 %copy-start = (bf16[1,768,2048]{2,1,0:T(8,128)(2,1)S(1)}, bf16[1,768,2048]{2,1,0:T(8,128)(2,1)}, u32[]{:S(2)}) copy-start(bf16[1,768,2048]{2,1,0:T(8,128)(2,1)} %param.21) | copy-start | bytes 9437188
  0.6 114.8 %copy-start.6 = (bf16[128,256]{1,0:T(8,128)(2,1)S(1)}, bf16[128,256]{1,0:T(8,128)(2,1)}, u32[]{:S(2)}) copy-start(bf16[128,256]{1,0:T(8,128)(2,1)} %param.13) | copy-start | bytes 196612
  0.7 115.0 %copy-start.7 = (bf16[128,256]{1,0:T(8,128)(2,1)S(1)}, bf16[128,256]{1,0:T(8,128)(2,1)}, u32[]{:S(2)}) copy-start(bf16[128,256]{1,0:T(8,128)(2,1)} %param.14) | copy-start | bytes 196612
  0.7 116.2 %copy-start.9 = (s32[128,8]{0,1:T(8,128)S(1)}, s32[128,8]{0,1:T(8,128)}, u32[]{:S(2)}) copy-start(s32[128,8]{0,1:T(8,128)} %param.22) | copy-start | bytes 12292
  0.7 117.3 %copy-start.11 = (f32[128,8]{0,1:T(8,128)S(1)}, f32[128,8]{0,1:T(8,128)}, u32[]{:S(2)}) copy-start(f32[128,8]{0,1:T(8,128)} %param.23) | copy-start | bytes 12292
  115.4 27.2 %collective-permute-start.2 = (bf16[2048,1024]{1,0:T(8,128)(2,1)}, bf16[2048,1024]{1,0:T(8,128)(2,1)}, u32[]{:S(2)}, u32[]{:S(2)}) collective-permute-start(bf16[2048,1024]{1,0:T(8,128)(2,1)} %bitcast.67), channel_id=1, source_target_pairs={{0,32},{32,0},{64,96},{96,64},{128,160},{160,128},{192,224},{224,1... | collective-permute-start | bytes 12582920 | tf_op jit(solution)/shard_map/ppermute | solution.py:189
  116.4 6.2 %collective-permute-start = (bf16[2,128,256]{1,2,0:T(8,128)(2,1)}, bf16[2,128,256]{1,2,0:T(8,128)(2,1)S(1)}, u32[]{:S(2)}, u32[]{:S(2)}) collective-permute-start(bf16[2,128,256]{1,2,0:T(8,128)(2,1)} %pad_maximum_fusion), channel_id=1, source_target_pairs={{0,32},{32,64},{64,96},{96,128},{128,160},{160,192},{192,224},{224... | collective-permute-start | bytes 393224 | tf_op jit(solution)/shard_map/ppermute | solution.py:21
  117.6 17.0 %copy-start.8 = (f32[128,16]{0,1:T(8,128)S(1)}, f32[128,16]{0,1:T(8,128)}, u32[]{:S(2)}) copy-start(f32[128,16]{0,1:T(8,128)} %param.16) | copy-start | bytes 24580
  122.7 9.3 %collective-permute-start.1 = (bf16[2,128,256]{1,2,0:T(8,128)(2,1)S(1)}, bf16[2,128,256]{1,2,0:T(8,128)(2,1)}, u32[]{:S(2)}, u32[]{:S(2)}) collective-permute-start(bf16[2,128,256]{1,2,0:T(8,128)(2,1)S(1)} %collective-permute-done), channel_id=1, source_target_pairs={{0,32},{32,64},{64,96},{96,128},{128,160},{160,192},{192,224},{224... | collective-permute-start | bytes 393224 | tf_op jit(solution)/shard_map/ppermute | solution.py:21
  132.0 3.0 copy-start.4
  135.5 0.8 copy-start.3
  139.3 3.3 copy-start.2
  139.4 6.1 %copy-start.5 = (bf16[128,2048]{1,0:T(8,128)(2,1)S(1)}, bf16[128,2048]{1,0:T(8,128)(2,1)}, u32[]{:S(2)}) copy-start(bf16[128,2048]{1,0:T(8,128)(2,1)} %param.17) | copy-start | bytes 1572868
  142.6 3.3 copy-start.10
  145.7 4.1 copy-start.1

commit v8 on v7

--- a/solution.py
+++ b/solution.py
@@ -87,6 +87,93 @@
 
     lax.fori_loop(1, n_ep, finish, 0)
     local.wait()
+
+
+def share_kernel(src_ref, dst_ref, send_sem, recv_sem, local_sem):
+    n_ep = lax.axis_size("ep")
+    n_ctx = lax.axis_size("ctx")
+    half = n_ep // 2
+    me = lax.axis_index("ep")
+    ctx_me = lax.axis_index("ctx")
+    core = ctx_me % 2
+    z_near = ctx_me // 2
+    z_far = (z_near + n_ctx // 4) % (n_ctx // 2)
+    mine = me // half
+    owned = 1 - (mine + core) % 2
+
+    def peer(j):
+        d = core * half + (me + j) % half
+        same = 1 - (d + me) % 2
+        z = same * z_near + (1 - same) * z_far
+        return d, z * 2 + mine
+
+    def each_remote(body):
+        def step(j, carry):
+            d, c = peer(j)
+
+            @pl.when(d != me)
+            def _():
+                body(d, c)
+
+            return carry
+
+        lax.fori_loop(0, half, step, 0)
+
+    barrier = pltpu.get_barrier_semaphore()
+    each_remote(
+        lambda d, c: pl.semaphore_signal(barrier, inc=1, device_id=(c, d), device_id_type=MESH)
+    )
+    pl.semaphore_wait(barrier, half - owned)
+
+    @pl.when(owned == 1)
+    def _():
+        local = pltpu.make_async_copy(src_ref.at[0], dst_ref.at[me % half], local_sem)
+        local.start()
+        local.wait()
+
+    def copy_to(d, c):
+        return pltpu.make_async_remote_copy(
+            src_ref=src_ref.at[0],
+            dst_ref=dst_ref.at[me % half],
+            send_sem=send_sem.at[d % half],
+            recv_sem=recv_sem.at[me % half],
+            device_id=(c, d),
+            device_id_type=MESH,
+        )
+
+    def copy_from(d, c):
+        return pltpu.make_async_remote_copy(
+            src_ref=src_ref.at[0],
+            dst_ref=dst_ref.at[d % half],
+            send_sem=send_sem.at[d % half],
+            recv_sem=recv_sem.at[d % half],
+            device_id=(c, d),
+            device_id_type=MESH,
+        )
+
+    each_remote(lambda d, c: copy_to(d, c).start())
+    each_remote(lambda d, c: copy_to(d, c).wait_send())
+    each_remote(lambda d, c: copy_from(d, c).wait_recv())
+
+
+def share(src, collective_id):
+    half = lax.axis_size("ep") // 2
+    moved = half * math.prod(src.shape) * src.dtype.itemsize
+    return pl.pallas_call(
+        share_kernel,
+        out_shape=jax.ShapeDtypeStruct((half,) + src.shape, src.dtype),
+        in_specs=[pl.BlockSpec(memory_space=pl.ANY)],
+        out_specs=pl.BlockSpec(memory_space=pl.ANY),
+        scratch_shapes=[
+            pltpu.SemaphoreType.DMA((half,)),
+            pltpu.SemaphoreType.DMA((half,)),
+            pltpu.SemaphoreType.DMA,
+        ],
+        compiler_params=pltpu.CompilerParams(
+            collective_id=collective_id, has_side_effects=True
+        ),
+        cost_estimate=pl.CostEstimate(flops=0, transcendentals=0, bytes_accessed=2 * moved),
+    )(src[None])
 
 
 def exchange(src, per_peer, collective_id):
@@ -181,24 +268,22 @@
     attended = ((prior_part + gathered) / totals.transpose(2, 0, 1)[..., None]).astype(jnp.bfloat16)
     attended = attended.reshape(local_rows, HEADS * HD)
     model_width = out_proj.shape[1]
-    column_half = model_width // 2
     core = ctx_here % 2
     column_rows = lax.all_gather(out_proj, "ctx", axis=0, tiled=True)
-    own_half = lax.dynamic_slice_in_dim(column_rows, core * column_half, column_half, axis=1)
-    own_half = exchange(own_half[None], False, 0).reshape(-1, column_half)
-    other_half = lax.ppermute(own_half, "ctx", [(i, i ^ 1) for i in range(ctx_count)])
+    own_rows = share(column_rows, 0).reshape(-1, model_width)
+    other_rows = lax.ppermute(own_rows, "ctx", [(i, i ^ 1) for i in range(ctx_count)])
     block_rows = out_proj.shape[0]
     attended_perm = (
         attended.reshape(local_rows, ctx_count, ep_count, block_rows)
         .transpose(0, 2, 1, 3)
         .reshape(local_rows, HEADS * HD)
     )
-    own_part = jnp.dot(attended_perm, own_half, preferred_element_type=jnp.float32)
-    other_part = jnp.dot(attended_perm, other_half, preferred_element_type=jnp.float32)
-    projected = jnp.zeros((local_rows, model_width), jnp.float32)
-    projected = lax.dynamic_update_slice_in_dim(projected, own_part, core * column_half, axis=1)
-    projected = lax.dynamic_update_slice_in_dim(
-        projected, other_part, (1 - core) * column_half, axis=1
+    k_half = own_rows.shape[0]
+    first, second = attended_perm[:, :k_half], attended_perm[:, k_half:]
+    own_cols = jnp.where(core == 0, first, second)
+    other_cols = jnp.where(core == 0, second, first)
+    projected = jnp.dot(own_cols, own_rows, preferred_element_type=jnp.float32) + jnp.dot(
+        other_cols, other_rows, preferred_element_type=jnp.float32
     )
     mixed_state = (residual.astype(jnp.float32) + projected).astype(jnp.bfloat16)
     state_f = lax.optimization_barrier(mixed_state).astype(jnp.float32)

time: 423 us -> 423 us (level)
    pallas_call x3 -> x2, Pallas kernels: 345 us -> 244 us  [exchange(): pl.pallas_call(functools.partial(exchange_kernel, per_peer), out_shape=ja...]
    pallas_call x0 -> x1, Pallas kernels: none -> 99.7 us  [share(): pl.pallas_call(share_kernel, out_shape=jax.ShapeDtypeStruct((half,) + src...]
where the time goes in v8:
time: 423 us; the launch traced here: 418 us
  Pallas kernels  344 us (81%)
  matrix products  36.9 us (9%)
  blocking collectives  13.9 us (3%)
  local copies, waits for them, and re-layouts  9.95 us (2%)
  other arithmetic  8.49 us (2%)
    pallas_call x2, Pallas kernels, exchange(): pl.pallas_call(functools.partial(exchange_kernel, per_peer), out_shape=ja...  244 us
    pallas_call x1, Pallas kernels, share(): pl.pallas_call(share_kernel, out_shape=jax.ShapeDtypeStruct((half,) + src...  99.7 us
    all_gather x1, blocking collectives, shards(): column_rows = lax.all_gather(out_proj, 'ctx', axis=0, tiled=True)  13.9 us
    dot_general x1, matrix products, run_expert(): gate_up = jnp.dot(flat_in, weight_in, preferred_element_type=jnp.float32)  12.1 us
  transfers between devices with their start and end apart: 3, of which 1 were waited for; matrix products, arithmetic and copies ran while one was open for 6% of the time, Pallas kernels for 0%

profile of v8, /device:TPU:94, one launch (start us, length us, event | category | flops | bytes accessed | tf_op | source)
XLA Modules:
  0.0 417.9 jit_solution(7614693215106806770)
XLA Ops:
  0.7 13.9 %all_gather.3 = bf16[64,2048]{1,0:T(8,128)(2,1)} all-gather(bf16[8,2048]{1,0:T(8,128)(2,1)} %param.18), channel_id=1, replica_groups=mesh['ctx'=8,'ep'=32] {'ctx'}, dimensions={0}, use_global_device_ids=true | all-gather | bytes 294912 | tf_op jit(solution)/shard_map/all_gather | solution.py:272
  14.6 99.7 %shard_map.131 = bf16[16,64,2048]{2,1,0:T(8,128)(2,1)} custom-call(bf16[1,64,2048]{2,1,0:T(8,128)(2,1)} %bitcast.73), custom_call_target="tpu_custom_call" | custom-call | bytes 8388608 | tf_op jit(solution)/shard_map/pallas_call | solution.py:162
  114.3 0.6 collective-permute-start.2
  115.2 0.7 pad_maximum_fusion
  116.1 0.5 fusion.17
  117.1 2.5 select_reduce_fusion
  119.7 2.4 collective-permute-done
  122.5 4.6 %fusion.2 = pred[1280,128]{1,0:T(8,128)(4,1)S(1)} fusion(s32[128,8]{0,1:T(8,128)S(1)} %multiply_add_fusion), kind=kLoop, calls=%fused_computation.7 | loop fusion | flops 2457600 | bytes 167936 | tf_op jit(solution)/shard_map/reduce_or | solution.py:309
  127.2 2.0 copy.64
  129.1 2.3 copy.47
  131.5 1.0 constant_dynamic-update-slice_fusion
  132.5 1.6 fusion.49
  134.4 0.5 fusion.15
  135.0 0.8 copy-done.2
  135.8 0.9 copy.53
  136.8 2.0 copy.58
  138.8 3.2 fusion.28
  142.0 2.9 fusion.7
  145.2 3.9 convolution_convert_fusion.1
  149.1 124.0 %shard_map.132 = bf16[32,40,2048]{2,1,0:T(8,128)(2,1)} custom-call(bf16[32,40,2048]{2,1,0:T(8,128)(2,1)} %bitcast.62), custom_call_target="tpu_custom_call" | custom-call | bytes 10485760 | tf_op jit(solution)/shard_map/pallas_call | solution.py:183
  273.1 12.1 %fusion = f32[1280,1536]{1,0:T(8,128)S(1)} fusion(bf16[1280,2048]{1,0:T(8,128)(2,1)} %bitcast.66, bf16[1,2048,1536]{2,1,0:T(8,128)(2,1)} %param.20), kind=kOutput, calls=%fused_computation.2 | convolution fusion | flops 8053063680 | bytes 19398656 | tf_op jit(solution)/shard_map/dot_general | solution.py:202
  285.2 6.3 %convolution_convert_fusion = bf16[1280,2048]{1,0:T(8,128)(2,1)} fusion(bf16[1,768,2048]{2,1,0:T(8,128)(2,1)S(1)} %copy-done, f32[1280,1536]{1,0:T(8,128)S(1)} %fusion), kind=kOutput, calls=%fused_computation | convolution fusion | flops 4035051520 | bytes 16252928 | tf_op jit(solution)/shard_map/dot_general | solution.py:206
  291.5 120.5 %shard_map.133 = bf16[32,40,2048]{2,1,0:T(8,128)(2,1)} custom-call(bf16[32,40,2048]{2,1,0:T(8,128)(2,1)} %bitcast.67), custom_call_target="tpu_custom_call" | custom-call | bytes 10485760 | tf_op jit(solution)/shard_map/pallas_call | solution.py:183
  412.0 5.8 %fusion.8 = bf16[128,2048]{1,0:T(8,128)(2,1)} fusion(f32[128,1280]{1,0:T(8,128)} %select_reduce_fusion, bf16[1280,2048]{1,0:T(8,128)(2,1)} %bitcast.63, bf16[128,2048]{1,0:T(8,128)(2,1)} %copy-done.1), kind=kOutput, calls=%fused_computation.17 | convolution fusion | flops 4027318272 | bytes 6946816 | tf_op jit(solution)/shard_map/dot_general | solution.py:331
  (47 shorter events, 1.9 us)
Async XLA Ops:
  0.6 284.6 %copy-start = (bf16[1,768,2048]{2,1,0:T(8,128)(2,1)S(1)}, bf16[1,768,2048]{2,1,0:T(8,128)(2,1)}, u32[]{:S(2)}) copy-start(bf16[1,768,2048]{2,1,0:T(8,128)(2,1)} %param.21) | copy-start | bytes 9437188
  0.6 114.3 %copy-start.6 = (bf16[128,256]{1,0:T(8,128)(2,1)S(1)}, bf16[128,256]{1,0:T(8,128)(2,1)}, u32[]{:S(2)}) copy-start(bf16[128,256]{1,0:T(8,128)(2,1)} %param.13) | copy-start | bytes 196612
  0.7 114.4 %copy-start.7 = (bf16[128,256]{1,0:T(8,128)(2,1)S(1)}, bf16[128,256]{1,0:T(8,128)(2,1)}, u32[]{:S(2)}) copy-start(bf16[128,256]{1,0:T(8,128)(2,1)} %param.14) | copy-start | bytes 196612
  0.7 115.2 %copy-start.9 = (s32[128,8]{0,1:T(8,128)S(1)}, s32[128,8]{0,1:T(8,128)}, u32[]{:S(2)}) copy-start(s32[128,8]{0,1:T(8,128)} %param.22) | copy-start | bytes 12292
  0.7 116.2 %copy-start.11 = (f32[128,8]{0,1:T(8,128)S(1)}, f32[128,8]{0,1:T(8,128)}, u32[]{:S(2)}) copy-start(f32[128,8]{0,1:T(8,128)} %param.23) | copy-start | bytes 12292
  114.3 27.7 %collective-permute-start.2 = (bf16[1024,2048]{1,0:T(8,128)(2,1)}, bf16[1024,2048]{1,0:T(8,128)(2,1)}, u32[]{:S(2)}, u32[]{:S(2)}) collective-permute-start(bf16[1024,2048]{1,0:T(8,128)(2,1)} %bitcast.64), channel_id=1, source_target_pairs={{0,32},{32,0},{64,96},{96,64},{128,160},{160,128},{192,224},{224,1... | collective-permute-start | bytes 12582920 | tf_op jit(solution)/shard_map/ppermute | solution.py:274
  115.9 6.3 %collective-permute-start = (bf16[2,128,256]{1,2,0:T(8,128)(2,1)}, bf16[2,128,256]{1,2,0:T(8,128)(2,1)S(1)}, u32[]{:S(2)}, u32[]{:S(2)}) collective-permute-start(bf16[2,128,256]{1,2,0:T(8,128)(2,1)} %pad_maximum_fusion), channel_id=1, source_target_pairs={{0,32},{32,64},{64,96},{96,128},{128,160},{160,192},{192,224},{224... | collective-permute-start | bytes 393224 | tf_op jit(solution)/shard_map/ppermute | solution.py:21
  116.6 17.5 %copy-start.8 = (f32[128,16]{0,1:T(8,128)S(1)}, f32[128,16]{0,1:T(8,128)}, u32[]{:S(2)}) copy-start(f32[128,16]{0,1:T(8,128)} %param.16) | copy-start | bytes 24580
  122.1 9.3 %collective-permute-start.1 = (bf16[2,128,256]{1,2,0:T(8,128)(2,1)S(1)}, bf16[2,128,256]{1,2,0:T(8,128)(2,1)}, u32[]{:S(2)}, u32[]{:S(2)}) collective-permute-start(bf16[2,128,256]{1,2,0:T(8,128)(2,1)S(1)} %collective-permute-done), channel_id=1, source_target_pairs={{0,32},{32,64},{64,96},{96,128},{128,160},{160,192},{192,224},{224... | collective-permute-start | bytes 393224 | tf_op jit(solution)/shard_map/ppermute | solution.py:21
  131.4 3.0 copy-start.4
  135.0 0.8 copy-start.2
  138.8 3.2 copy-start.3
  138.8 3.2 copy-start.5
  142.0 3.2 copy-start.10
  145.0 4.1 copy-start.1

commit v9 on v8

--- a/solution.py
+++ b/solution.py
@@ -270,8 +270,14 @@
     model_width = out_proj.shape[1]
     core = ctx_here % 2
     column_rows = lax.all_gather(out_proj, "ctx", axis=0, tiled=True)
-    own_rows = share(column_rows, 0).reshape(-1, model_width)
-    other_rows = lax.ppermute(own_rows, "ctx", [(i, i ^ 1) for i in range(ctx_count)])
+    kernel_cols = model_width // 2
+    quarter = (model_width - kernel_cols) // 2
+    side_rows = lax.dynamic_slice_in_dim(column_rows, kernel_cols + core * quarter, quarter, axis=1)
+    side_rows = lax.all_gather(side_rows, "ep", axis=0, tiled=True)
+    own_rows = share(column_rows[:, :kernel_cols], 0).reshape(-1, kernel_cols)
+    swap = [(i, i ^ 1) for i in range(ctx_count)]
+    other_rows = lax.ppermute(own_rows, "ctx", swap)
+    other_side = lax.ppermute(side_rows, "ctx", swap)
     block_rows = out_proj.shape[0]
     attended_perm = (
         attended.reshape(local_rows, ctx_count, ep_count, block_rows)
@@ -280,10 +286,20 @@
     )
     k_half = own_rows.shape[0]
     first, second = attended_perm[:, :k_half], attended_perm[:, k_half:]
-    own_cols = jnp.where(core == 0, first, second)
-    other_cols = jnp.where(core == 0, second, first)
-    projected = jnp.dot(own_cols, own_rows, preferred_element_type=jnp.float32) + jnp.dot(
-        other_cols, other_rows, preferred_element_type=jnp.float32
+    own_k = jnp.where(core == 0, first, second)
+    other_k = jnp.where(core == 0, second, first)
+    kernel_part = jnp.dot(own_k, own_rows, preferred_element_type=jnp.float32) + jnp.dot(
+        other_k, other_rows, preferred_element_type=jnp.float32
+    )
+    own_side = jnp.dot(attended_perm, side_rows, preferred_element_type=jnp.float32)
+    far_side = jnp.dot(attended_perm, other_side, preferred_element_type=jnp.float32)
+    projected = jnp.zeros((local_rows, model_width), jnp.float32)
+    projected = lax.dynamic_update_slice_in_dim(projected, kernel_part, 0, axis=1)
+    projected = lax.dynamic_update_slice_in_dim(
+        projected, own_side, kernel_cols + core * quarter, axis=1
+    )
+    projected = lax.dynamic_update_slice_in_dim(
+        projected, far_side, kernel_cols + (1 - core) * quarter, axis=1
     )
     mixed_state = (residual.astype(jnp.float32) + projected).astype(jnp.bfloat16)
     state_f = lax.optimization_barrier(mixed_state).astype(jnp.float32)

time: 423 us -> 428 us (1.012)
  Pallas kernels: 344 us -> 297 us
  waiting for transfers between devices: 2.44 us -> 35.4 us
  between operations: 0.96 us -> 14.4 us
  local copies, waits for them, and re-layouts: 9.95 us -> 14.3 us
    pallas_call x1, Pallas kernels: 99.7 us -> 57 us  [share(): pl.pallas_call(share_kernel, out_shape=jax.ShapeDtypeStruct((half,) + src...]
    all_gather x0 -> x1, waiting for transfers between devices: none -> 35.4 us  [shards(): side_rows = lax.all_gather(side_rows, 'ep', axis=0, tiled=True)]
    pallas_call x2, Pallas kernels: 244 us -> 240 us  [exchange(): pl.pallas_call(functools.partial(exchange_kernel, per_peer), out_shape=ja...]
  transfers between devices with their start and end apart: 3 -> 5, of which waited for: 1 -> 1; matrix products, arithmetic and copies ran while one was open for 6% -> 7% of each run, Pallas kernels for 0% -> 14%
where the time goes in v9:
time: 428 us; the launch traced here: 421 us
  Pallas kernels  297 us (69%)
  matrix products  37.8 us (9%)
  waiting for transfers between devices  35.4 us (8%)
  between operations  14.4 us (3%)
  local copies, waits for them, and re-layouts  14.3 us (3%)
  blocking collectives  12.8 us (3%)
  other arithmetic  8.59 us (2%)
    pallas_call x2, Pallas kernels, exchange(): pl.pallas_call(functools.partial(exchange_kernel, per_peer), out_shape=ja...  240 us
    pallas_call x1, Pallas kernels, share(): pl.pallas_call(share_kernel, out_shape=jax.ShapeDtypeStruct((half,) + src...  57 us
    all_gather x1, waiting for transfers between devices, shards(): side_rows = lax.all_gather(side_rows, 'ep', axis=0, tiled=True)  35.4 us
    all_gather x1, blocking collectives, shards(): column_rows = lax.all_gather(out_proj, 'ctx', axis=0, tiled=True)  12.8 us
    dot_general x1, matrix products, run_expert(): gate_up = jnp.dot(flat_in, weight_in, preferred_element_type=jnp.float32)  12.1 us
    unnamed x31, local copies, waits for them, and re-layouts  8.62 us
  transfers between devices with their start and end apart: 5, of which 1 were waited for; matrix products, arithmetic and copies ran while one was open for 7% of the time, Pallas kernels for 14%

profile of v9, /device:TPU:94, one launch (start us, length us, event | category | flops | bytes accessed | tf_op | source)
XLA Modules:
  0.0 421.2 jit_solution(5759247038366925402)
XLA Ops:
  7.3 12.8 %all_gather.6 = bf16[64,2048]{1,0:T(8,128)(2,1)S(1)} all-gather(bf16[8,2048]{1,0:T(8,128)(2,1)} %param.18), channel_id=1, replica_groups=mesh['ctx'=8,'ep'=32] {'ctx'}, dimensions={0}, use_global_device_ids=true | all-gather | bytes 294912 | tf_op jit(solution)/shard_map/all_gather | solution.py:272
  20.7 1.0 copy.48
  21.7 1.0 copy.49
  24.4 57.0 %shard_map.131 = bf16[16,64,1024]{2,1,0:T(8,128)(2,1)} custom-call(bf16[1,64,1024]{2,1,0:T(8,128)(2,1)} %slice_bitcast_fusion.src_ref), custom_call_target="tpu_custom_call" | custom-call | bytes 4194304 | tf_op jit(solution)/shard_map/pallas_call | solution.py:162
  81.5 0.8 copy.54
  83.3 2.5 select_reduce_fusion
  86.5 4.6 %fusion.2 = pred[1280,128]{1,0:T(8,128)(4,1)S(1)} fusion(s32[128,8]{0,1:T(8,128)S(1)} %multiply_add_fusion), kind=kLoop, calls=%fused_computation.7 | loop fusion | flops 2457600 | bytes 167936 | tf_op jit(solution)/shard_map/reduce_or | solution.py:325
  91.2 2.0 copy.64
  93.1 2.3 copy.47
  95.4 0.9 constant_dynamic-update-slice_fusion.1
  97.1 35.4 %all-gather.2.cloned.1.call-done = bf16[2048,512]{1,0:T(8,128)(2,1)} async-done(((bf16[64,512]{1,0:T(8,128)(2,1)}), bf16[2048,512]{1,0:T(8,128)(2,1)}) %all-gather.2.cloned.1.call-update) | async-done | bytes 2097168 | tf_op jit(solution)/shard_map/all_gather | solution.py:276
  132.5 1.7 fusion.47
  135.1 0.8 copy-done.4
  135.9 0.9 copy.53
  136.9 2.0 copy.58
  138.9 2.4 fusion.26
  141.3 2.2 convolution_add_fusion.1
  144.2 2.1 convolution_dynamic-update-slice_fusion
  146.6 3.9 convolution_convert_fusion.1
  150.5 120.1 %shard_map.132 = bf16[32,40,2048]{2,1,0:T(8,128)(2,1)} custom-call(bf16[32,40,2048]{2,1,0:T(8,128)(2,1)} %bitcast.67), custom_call_target="tpu_custom_call" | custom-call | bytes 10485760 | tf_op jit(solution)/shard_map/pallas_call | solution.py:183
  270.6 12.1 %fusion = f32[1280,1536]{1,0:T(8,128)S(1)} fusion(bf16[1280,2048]{1,0:T(8,128)(2,1)} %bitcast.75, bf16[1,2048,1536]{2,1,0:T(8,128)(2,1)} %param.20), kind=kOutput, calls=%fused_computation.2 | convolution fusion | flops 8053063680 | bytes 19398656 | tf_op jit(solution)/shard_map/dot_general | solution.py:202
  282.7 6.1 %convolution_convert_fusion = bf16[1280,2048]{1,0:T(8,128)(2,1)} fusion(bf16[1,768,2048]{2,1,0:T(8,128)(2,1)S(1)} %copy-done, f32[1280,1536]{1,0:T(8,128)S(1)} %fusion), kind=kOutput, calls=%fused_computation | convolution fusion | flops 4035051520 | bytes 16252928 | tf_op jit(solution)/shard_map/dot_general | solution.py:206
  288.8 119.7 %shard_map.133 = bf16[32,40,2048]{2,1,0:T(8,128)(2,1)} custom-call(bf16[32,40,2048]{2,1,0:T(8,128)(2,1)} %bitcast.76), custom_call_target="tpu_custom_call" | custom-call | bytes 10485760 | tf_op jit(solution)/shard_map/pallas_call | solution.py:183
  408.5 5.8 %fusion.6 = bf16[128,2048]{1,0:T(8,128)(2,1)} fusion(f32[128,1280]{1,0:T(8,128)} %select_reduce_fusion, bf16[1280,2048]{1,0:T(8,128)(2,1)} %bitcast.68, bf16[128,2048]{1,0:T(8,128)(2,1)} %copy-done.2), kind=kOutput, calls=%fused_computation.14 | convolution fusion | flops 4027318272 | bytes 6946816 | tf_op jit(solution)/shard_map/dot_general | solution.py:347
  (58 shorter events, 6.7 us)
Async XLA Ops:
  7.2 275.6 %copy-start = (bf16[1,768,2048]{2,1,0:T(8,128)(2,1)S(1)}, bf16[1,768,2048]{2,1,0:T(8,128)(2,1)}, u32[]{:S(2)}) copy-start(bf16[1,768,2048]{2,1,0:T(8,128)(2,1)} %param.21) | copy-start | bytes 9437188
  7.2 75.9 %copy-start.9 = (s32[128,8]{0,1:T(8,128)S(1)}, s32[128,8]{0,1:T(8,128)}, u32[]{:S(2)}) copy-start(s32[128,8]{0,1:T(8,128)} %param.22) | copy-start | bytes 12292
  7.2 76.0 %copy-start.11 = (f32[128,8]{0,1:T(8,128)S(1)}, f32[128,8]{0,1:T(8,128)}, u32[]{:S(2)}) copy-start(f32[128,8]{0,1:T(8,128)} %param.23) | copy-start | bytes 12292
  7.2 125.3 %all-gather.2.cloned.1.call-start = ((), (), s32[]{:S(2)}) async-start(), calls=%async_computation | async-start | bytes 2162688 | tf_op jit(solution)/shard_map/all_gather | solution.py:276
  23.3 62.6 %collective-permute-start = (bf16[2,128,256]{1,2,0:T(8,128)(2,1)}, bf16[2,128,256]{1,2,0:T(8,128)(2,1)}, u32[]{:S(2)}, u32[]{:S(2)}) collective-permute-start(bf16[2,128,256]{1,2,0:T(8,128)(2,1)} %pad_maximum_fusion), channel_id=1, source_target_pairs={{0,32},{32,64},{64,96},{96,128},{128,160},{160,192},{192,224},{224... | collective-permute-start | bytes 393224 | tf_op jit(solution)/shard_map/ppermute | solution.py:21
  81.4 59.9 %collective-permute-start.2 = (bf16[1024,1024]{1,0:T(8,128)(2,1)}, bf16[1024,1024]{1,0:T(8,128)(2,1)}, u32[]{:S(2)}, u32[]{:S(2)}) collective-permute-start(bf16[1024,1024]{1,0:T(8,128)(2,1)} %bitcast.69), channel_id=1, source_target_pairs={{0,32},{32,0},{64,96},{96,64},{128,160},{160,128},{192,224},{224,1... | collective-permute-start | bytes 6291464 | tf_op jit(solution)/shard_map/ppermute | solution.py:279
  82.9 51.3 %copy-start.8 = (f32[128,16]{0,1:T(8,128)S(1)}, f32[128,16]{0,1:T(8,128)}, u32[]{:S(2)}) copy-start(f32[128,16]{0,1:T(8,128)} %param.16) | copy-start | bytes 24580
  86.0 10.4 %collective-permute-start.1 = (bf16[2,128,256]{1,2,0:T(8,128)(2,1)}, bf16[2,128,256]{1,2,0:T(8,128)(2,1)S(1)}, u32[]{:S(2)}, u32[]{:S(2)}) collective-permute-start(bf16[2,128,256]{1,2,0:T(8,128)(2,1)} %collective-permute-done), channel_id=1, source_target_pairs={{0,32},{32,64},{64,96},{96,128},{128,160},{160,192},{192,224},{224... | collective-permute-start | bytes 393224 | tf_op jit(solution)/shard_map/ppermute | solution.py:21
  132.5 2.0 copy-start.5
  132.5 2.0 copy-start.7
  132.5 11.7 %collective-permute-start.3 = (bf16[2048,512]{1,0:T(8,128)(2,1)}, bf16[2048,512]{1,0:T(8,128)(2,1)}, u32[]{:S(2)}, u32[]{:S(2)}) collective-permute-start(bf16[2048,512]{1,0:T(8,128)(2,1)} %all-gather.2.cloned.1.call-done), channel_id=1, source_target_pairs={{0,32},{32,0},{64,96},{96,64},{128,160},{160,128},{192,224},{224,1... | collective-permute-start | bytes 6291464 | tf_op jit(solution)/shard_map/ppermute | solution.py:280
  135.1 0.8 copy-start.4
  138.9 4.8 %copy-start.1 = (bf16[128,8,32,8]{0,3,1,2:T(8,128)(2,1)S(1)}, bf16[128,8,32,8]{0,3,1,2:T(8,128)(2,1)}, u32[]{:S(2)}) copy-start(bf16[128,8,32,8]{0,3,1,2:T(8,128)(2,1)} %copy.53) | copy-start | bytes 1572868
  138.9 4.8 %copy-start.3 = (bf16[2048,512]{1,0:T(8,128)(2,1)S(1)}, bf16[2048,512]{1,0:T(8,128)(2,1)}, u32[]{:S(2)}) copy-start(bf16[2048,512]{1,0:T(8,128)(2,1)} %all-gather.2.cloned.1.call-done) | copy-start | bytes 6291460
  143.5 2.7 copy-start.6
  143.7 2.9 copy-start.10
  146.4 4.1 copy-start.2
Sparse Core Ops, SparseCore 0:
  20.9 111.5 all-gather.1

commit v10 on v7

--- a/solution.py
+++ b/solution.py
@@ -222,21 +222,23 @@
     slot_ids = (flat_ids * capacity + rank).reshape(local_rows, top_count)
     slot_pos = jnp.arange(experts_all * capacity, dtype=jnp.int32)
     take = jnp.any(slot_ids[None, :, :] == slot_pos[:, None, None], axis=2).astype(jnp.bfloat16)
+    lanes = 128
+    chunk_rows = capacity * model_width // lanes
     outgoing = (
         jnp.dot(take, normed, preferred_element_type=jnp.float32)
         .astype(jnp.bfloat16)
-        .reshape(experts_all, capacity, model_width)
+        .reshape(experts_all, chunk_rows, lanes)
     )
     weight_in = expert_in[0]
     weight_out = expert_out[0]
     hidden_units = weight_out.shape[0]
     replies = run_expert(
-        exchange(outgoing, True, 1),
+        exchange(outgoing, True, 1).reshape(experts_all, capacity, model_width),
         weight_in,
         weight_out,
         hidden_units,
     )
-    returned = exchange(replies, True, 2)
+    returned = exchange(replies.reshape(experts_all, chunk_rows, lanes), True, 2)
     spread = jnp.sum(
         jnp.where(
             slot_ids[:, :, None] == slot_pos[None, None, :], route_weight[:, :, None], 0.0

time: 423 us -> 459 us (1.085)
  local copies, waits for them, and re-layouts: 10.7 us -> 46.8 us
    reshape x0 -> x2, local copies, waits for them, and re-layouts: none -> 17.7 us  [the longest x1 8.92 us: shards(): outgoing = jnp.dot(take, normed, preferred_element_type=jnp.float32).asty...]
    another operation x0 -> x2, local copies, waits for them, and re-layouts: none -> 17.7 us  [the longest x1 8.92 us: shards(): replies.reshape(experts_all, chunk_rows, lanes)]
  transfers between devices with their start and end apart: 3 -> 3, of which waited for: 1 -> 1; matrix products, arithmetic and copies ran while one was open for 6% -> 5% of each run, Pallas kernels for 0% -> 0%
where the time goes in v10:
time: 459 us; the launch traced here: 454 us
  Pallas kernels  345 us (75%)
  local copies, waits for them, and re-layouts  46.8 us (10%)
  matrix products  36.6 us (8%)
  blocking collectives  12.8 us (3%)
  other arithmetic  8.61 us (2%)
    pallas_call x3, Pallas kernels, exchange(): pl.pallas_call(functools.partial(exchange_kernel, per_peer), out_shape=ja...  345 us
    all_gather x1, blocking collectives, shards(): column_rows = lax.all_gather(out_proj, 'ctx', axis=0, tiled=True)  12.8 us
    dot_general x1, matrix products, run_expert(): gate_up = jnp.dot(flat_in, weight_in, preferred_element_type=jnp.float32)  12.1 us
  transfers between devices with their start and end apart: 3, of which 1 were waited for; matrix products, arithmetic and copies ran while one was open for 5% of the time, Pallas kernels for 0%

profile of v10, /device:TPU:94, one launch (start us, length us, event | category | flops | bytes accessed | tf_op | source)
XLA Modules:
  0.0 453.5 jit_solution(1892881010169497378)
XLA Ops:
  0.7 12.8 %all_gather.3 = bf16[64,2048]{1,0:T(8,128)(2,1)S(1)} all-gather(bf16[8,2048]{1,0:T(8,128)(2,1)} %param.18), channel_id=1, replica_groups=mesh['ctx'=8,'ep'=32] {'ctx'}, dimensions={0}, use_global_device_ids=true | all-gather | bytes 294912 | tf_op jit(solution)/shard_map/all_gather | solution.py:186
  14.2 101.2 %shard_map.131 = bf16[32,64,1024]{2,1,0:T(8,128)(2,1)} custom-call(bf16[1,64,1024]{2,1,0:T(8,128)(2,1)} %dynamic-slice_bitcast_fusion.src_ref), custom_call_target="tpu_custom_call" | custom-call | bytes 8388608 | tf_op jit(solution)/shard_map/pallas_call | solution.py:96
  118.1 2.5 select_reduce_fusion
  120.7 2.0 collective-permute-done
  123.0 4.6 %fusion.2 = pred[1280,128]{1,0:T(8,128)(4,1)S(1)} fusion(s32[128,8]{0,1:T(8,128)S(1)} %multiply_add_fusion), kind=kLoop, calls=%fused_computation.7 | loop fusion | flops 2457600 | bytes 167936 | tf_op jit(solution)/shard_map/reduce_or | solution.py:224
  127.7 2.0 copy.64
  129.6 2.3 copy.47
  132.0 1.0 constant_dynamic-update-slice_fusion
  133.0 1.6 fusion.38
  135.5 0.8 copy-done.3
  136.4 0.9 copy.53
  137.3 2.0 copy.58
  139.5 3.1 convolution_dynamic-update-slice_fusion.1
  142.6 2.9 convolution_dynamic-update-slice_fusion
  146.5 3.9 convolution_convert_fusion.1
  150.5 8.9 %reshape.99.src_ref = bf16[32,640,128]{2,1,0:T(8,128)(2,1)} reshape(bf16[1280,2048]{1,0:T(8,128)(2,1)} %convolution_convert_fusion.1) | data formatting | bytes 10485760 | tf_op jit(solution)/shard_map/reshape | solution.py:230
  159.4 121.5 %shard_map.132 = bf16[32,640,128]{2,1,0:T(8,128)(2,1)} custom-call(bf16[32,640,128]{2,1,0:T(8,128)(2,1)} %reshape.99.src_ref), custom_call_target="tpu_custom_call" | custom-call | bytes 10485760 | tf_op jit(solution)/shard_map/pallas_call | solution.py:96
  280.9 8.8 %reshape_reshape.10 = bf16[1280,2048]{1,0:T(8,128)(2,1)} reshape(bf16[32,640,128]{2,1,0:T(8,128)(2,1)} %shard_map.132) | data formatting | bytes 10485760 | tf_op jit(solution)/shard_map/reshape;reshape | solution.py:114
  289.7 12.1 %fusion = f32[1280,1536]{1,0:T(8,128)S(1)} fusion(bf16[1280,2048]{1,0:T(8,128)(2,1)} %reshape_reshape.10, bf16[1,2048,1536]{2,1,0:T(8,128)(2,1)} %param.20), kind=kOutput, calls=%fused_computation.2 | convolution fusion | flops 8053063680 | bytes 19398656 | tf_op jit(solution)/shard_map/dot_general | solution.py:115
  301.8 6.1 %convolution_convert_fusion = bf16[1280,2048]{1,0:T(8,128)(2,1)} fusion(bf16[1,768,2048]{2,1,0:T(8,128)(2,1)S(1)} %copy-done, f32[1280,1536]{1,0:T(8,128)S(1)} %fusion), kind=kOutput, calls=%fused_computation | convolution fusion | flops 4035051520 | bytes 16252928 | tf_op jit(solution)/shard_map/dot_general | solution.py:119
  307.9 8.9 %reshape_reshape.11.src_ref = bf16[32,640,128]{2,1,0:T(8,128)(2,1)} reshape(bf16[1280,2048]{1,0:T(8,128)(2,1)} %convolution_convert_fusion) | data formatting | bytes 10485760 | tf_op jit(solution)/shard_map/reshape;reshape | solution.py:241
  316.8 122.1 %shard_map.133 = bf16[32,640,128]{2,1,0:T(8,128)(2,1)} custom-call(bf16[32,640,128]{2,1,0:T(8,128)(2,1)} %reshape_reshape.11.src_ref), custom_call_target="tpu_custom_call" | custom-call | bytes 10485760 | tf_op jit(solution)/shard_map/pallas_call | solution.py:96
  438.9 8.8 %reshape.100 = bf16[1280,2048]{1,0:T(8,128)(2,1)} reshape(bf16[32,640,128]{2,1,0:T(8,128)(2,1)} %shard_map.133) | data formatting | bytes 10485760 | tf_op jit(solution)/shard_map/reshape | solution.py:250
  447.7 5.8 %fusion.6 = bf16[128,2048]{1,0:T(8,128)(2,1)} fusion(f32[128,1280]{1,0:T(8,128)} %select_reduce_fusion, bf16[1280,2048]{1,0:T(8,128)(2,1)} %reshape.100, bf16[128,2048]{1,0:T(8,128)(2,1)} %copy-done.1), kind=kOutput, calls=%fused_computation.14 | convolution fusion | flops 4027318272 | bytes 6946816 | tf_op jit(solution)/shard_map/dot_general | solution.py:248
  (54 shorter events, 5.7 us)
Async XLA Ops:
  0.6 301.2 %copy-start = (bf16[1,768,2048]{2,1,0:T(8,128)(2,1)S(1)}, bf16[1,768,2048]{2,1,0:T(8,128)(2,1)}, u32[]{:S(2)}) copy-start(bf16[1,768,2048]{2,1,0:T(8,128)(2,1)} %param.21) | copy-start | bytes 9437188
  0.6 114.8 %copy-start.6 = (bf16[128,256]{1,0:T(8,128)(2,1)S(1)}, bf16[128,256]{1,0:T(8,128)(2,1)}, u32[]{:S(2)}) copy-start(bf16[128,256]{1,0:T(8,128)(2,1)} %param.13) | copy-start | bytes 196612
  0.7 115.0 %copy-start.7 = (bf16[128,256]{1,0:T(8,128)(2,1)S(1)}, bf16[128,256]{1,0:T(8,128)(2,1)}, u32[]{:S(2)}) copy-start(bf16[128,256]{1,0:T(8,128)(2,1)} %param.14) | copy-start | bytes 196612
  0.7 116.2 %copy-start.9 = (s32[128,8]{0,1:T(8,128)S(1)}, s32[128,8]{0,1:T(8,128)}, u32[]{:S(2)}) copy-start(s32[128,8]{0,1:T(8,128)} %param.22) | copy-start | bytes 12292
  0.7 117.3 %copy-start.11 = (f32[128,8]{0,1:T(8,128)S(1)}, f32[128,8]{0,1:T(8,128)}, u32[]{:S(2)}) copy-start(f32[128,8]{0,1:T(8,128)} %param.23) | copy-start | bytes 12292
  115.4 27.2 %collective-permute-start.2 = (bf16[2048,1024]{1,0:T(8,128)(2,1)}, bf16[2048,1024]{1,0:T(8,128)(2,1)}, u32[]{:S(2)}, u32[]{:S(2)}) collective-permute-start(bf16[2048,1024]{1,0:T(8,128)(2,1)} %bitcast.61), channel_id=1, source_target_pairs={{0,32},{32,0},{64,96},{96,64},{128,160},{160,128},{192,224},{224,1... | collective-permute-start | bytes 12582920 | tf_op jit(solution)/shard_map/ppermute | solution.py:189
  116.4 6.2 %collective-permute-start = (bf16[2,128,256]{1,2,0:T(8,128)(2,1)}, bf16[2,128,256]{1,2,0:T(8,128)(2,1)S(1)}, u32[]{:S(2)}, u32[]{:S(2)}) collective-permute-start(bf16[2,128,256]{1,2,0:T(8,128)(2,1)} %pad_maximum_fusion), channel_id=1, source_target_pairs={{0,32},{32,64},{64,96},{96,128},{128,160},{160,192},{192,224},{224... | collective-permute-start | bytes 393224 | tf_op jit(solution)/shard_map/ppermute | solution.py:21
  117.6 17.0 %copy-start.8 = (f32[128,16]{0,1:T(8,128)S(1)}, f32[128,16]{0,1:T(8,128)}, u32[]{:S(2)}) copy-start(f32[128,16]{0,1:T(8,128)} %param.16) | copy-start | bytes 24580
  122.7 9.3 %collective-permute-start.1 = (bf16[2,128,256]{1,2,0:T(8,128)(2,1)S(1)}, bf16[2,128,256]{1,2,0:T(8,128)(2,1)}, u32[]{:S(2)}, u32[]{:S(2)}) collective-permute-start(bf16[2,128,256]{1,2,0:T(8,128)(2,1)S(1)} %collective-permute-done), channel_id=1, source_target_pairs={{0,32},{32,64},{64,96},{96,128},{128,160},{160,192},{192,224},{224... | collective-permute-start | bytes 393224 | tf_op jit(solution)/shard_map/ppermute | solution.py:21
  132.0 3.0 copy-start.4
  135.5 0.8 copy-start.3
  139.3 3.3 copy-start.2
  139.4 6.1 %copy-start.5 = (bf16[128,2048]{1,0:T(8,128)(2,1)S(1)}, bf16[128,2048]{1,0:T(8,128)(2,1)}, u32[]{:S(2)}) copy-start(bf16[128,2048]{1,0:T(8,128)(2,1)} %param.17) | copy-start | bytes 1572868
  142.6 3.9 copy-start.10
  145.7 0.8 copy-start.1

commit v11 on v7

--- a/solution.py
+++ b/solution.py
@@ -183,8 +183,14 @@
     model_width = out_proj.shape[1]
     column_half = model_width // 2
     core = ctx_here % 2
-    column_rows = lax.all_gather(out_proj, "ctx", axis=0, tiled=True)
+    block_count = out_proj.shape[0]
+    column_rows = jnp.zeros((ctx_count * block_count, model_width), out_proj.dtype)
+    column_rows = lax.dynamic_update_slice_in_dim(
+        column_rows, out_proj, ctx_here * block_count, axis=0
+    )
+    column_rows = lax.psum(column_rows, "ctx")
     own_half = lax.dynamic_slice_in_dim(column_rows, core * column_half, column_half, axis=1)
+    own_half, attended = lax.optimization_barrier((own_half, attended))
     own_half = exchange(own_half[None], False, 0).reshape(-1, column_half)
     other_half = lax.ppermute(own_half, "ctx", [(i, i ^ 1) for i in range(ctx_count)])
     block_rows = out_proj.shape[0]

time: 423 us -> 480 us (1.13)
  waiting for transfers between devices: 1.96 us -> 59.6 us
  between operations: 1.01 us -> 14.4 us
  blocking collectives: 12.8 us -> 0 us
    psum x0 -> x1, waiting for transfers between devices: none -> 55.3 us  [shards(): column_rows = lax.psum(column_rows, 'ctx')]
    all_gather x1 -> x0, blocking collectives: 12.8 us -> none  [shards(): column_rows = lax.all_gather(out_proj, 'ctx', axis=0, tiled=True)]
  transfers between devices with their start and end apart: 3 -> 4, of which waited for: 1 -> 2; matrix products, arithmetic and copies ran while one was open for 6% -> 5% of each run, Pallas kernels for 0% -> 0%
where the time goes in v11:
time: 480 us; the launch traced here: 474 us
  Pallas kernels  341 us (71%)
  waiting for transfers between devices  59.6 us (12%)
  matrix products  37.6 us (8%)
  between operations  14.4 us (3%)
  local copies, waits for them, and re-layouts  13.3 us (3%)
  other arithmetic  8.14 us (2%)
    pallas_call x3, Pallas kernels, exchange(): pl.pallas_call(functools.partial(exchange_kernel, per_peer), out_shape=ja...  341 us
    psum x1, waiting for transfers between devices, shards(): column_rows = lax.psum(column_rows, 'ctx')  55.3 us
    dot_general x1, matrix products, run_expert(): gate_up = jnp.dot(flat_in, weight_in, preferred_element_type=jnp.float32)  12.1 us
  transfers between devices with their start and end apart: 4, of which 2 were waited for; matrix products, arithmetic and copies ran while one was open for 5% of the time, Pallas kernels for 0%

profile of v11, /device:TPU:94, one launch (start us, length us, event | category | flops | bytes accessed | tf_op | source)
XLA Modules:
  0.0 474.2 jit_solution(14502989487302164837)
XLA Ops:
  7.3 0.9 constant_dynamic-update-slice_fusion.2
  8.2 0.7 copy-done.3
  8.9 1.0 copy.59
  9.9 1.0 copy.60
  11.0 4.4 collective-permute-done
  15.5 2.0 copy.75
  17.5 2.2 copy.58
  19.8 1.6 fusion.38
  21.8 1.3 fusion.13
  23.1 55.3 %all-reduce.2.cloned.1.call-done = bf16[64,2048]{1,0:T(8,128)(2,1)} async-done(((bf16[64,2048]{1,0:T(8,128)(2,1)}), bf16[64,2048]{1,0:T(8,128)(2,1)}) %all-reduce.2.cloned.1.call-update) | async-done | bytes 262160 | tf_op jit(solution)/shard_map/psum | solution.py:191
  78.4 1.6 constant_dynamic-slice_fusion
  80.0 100.9 %shard_map.131 = bf16[32,64,1024]{2,1,0:T(8,128)(2,1)} custom-call(bf16[1,64,1024]{2,1,0:T(8,128)(2,1)} %bitcast.76), custom_call_target="tpu_custom_call" | custom-call | bytes 8388608 | tf_op jit(solution)/shard_map/pallas_call | solution.py:96
  182.1 4.8 %fusion.2 = pred[1280,128]{1,0:T(8,128)(4,1)S(1)} fusion(s32[128,8]{0,1:T(8,128)S(1)} %multiply_add_fusion), kind=kLoop, calls=%fused_computation.7 | loop fusion | flops 2457600 | bytes 167936 | tf_op jit(solution)/shard_map/reduce_or | solution.py:230
  186.9 2.5 select_reduce_fusion
  189.4 2.0 copy.69
  191.4 1.2 copy.64
  192.7 3.0 convolution_dynamic-update-slice_fusion.1
  195.8 2.9 convolution_dynamic-update-slice_fusion
  199.1 3.9 convolution_convert_fusion.1
  203.0 120.1 %shard_map.132 = bf16[32,40,2048]{2,1,0:T(8,128)(2,1)} custom-call(bf16[32,40,2048]{2,1,0:T(8,128)(2,1)} %bitcast.64), custom_call_target="tpu_custom_call" | custom-call | bytes 10485760 | tf_op jit(solution)/shard_map/pallas_call | solution.py:96
  323.1 12.1 %fusion = f32[1280,1536]{1,0:T(8,128)S(1)} fusion(bf16[1280,2048]{1,0:T(8,128)(2,1)} %bitcast.68, bf16[1,2048,1536]{2,1,0:T(8,128)(2,1)} %param.20), kind=kOutput, calls=%fused_computation.2 | convolution fusion | flops 8053063680 | bytes 19398656 | tf_op jit(solution)/shard_map/dot_general | solution.py:115
  335.2 6.3 %convolution_convert_fusion = bf16[1280,2048]{1,0:T(8,128)(2,1)} fusion(bf16[1,768,2048]{2,1,0:T(8,128)(2,1)S(1)} %copy-done, f32[1280,1536]{1,0:T(8,128)S(1)} %fusion), kind=kOutput, calls=%fused_computation | convolution fusion | flops 4035051520 | bytes 16252928 | tf_op jit(solution)/shard_map/dot_general | solution.py:119
  341.5 120.0 %shard_map.133 = bf16[32,40,2048]{2,1,0:T(8,128)(2,1)} custom-call(bf16[32,40,2048]{2,1,0:T(8,128)(2,1)} %bitcast.69), custom_call_target="tpu_custom_call" | custom-call | bytes 10485760 | tf_op jit(solution)/shard_map/pallas_call | solution.py:96
  461.5 5.8 %fusion.6 = bf16[128,2048]{1,0:T(8,128)(2,1)} fusion(f32[128,1280]{1,0:T(8,128)} %select_reduce_fusion, bf16[1280,2048]{1,0:T(8,128)(2,1)} %bitcast.65, bf16[128,2048]{1,0:T(8,128)(2,1)} %copy-done.1), kind=kOutput, calls=%fused_computation.14 | convolution fusion | flops 4027318272 | bytes 6946816 | tf_op jit(solution)/shard_map/dot_general | solution.py:252
  (48 shorter events, 2.4 us)
Async XLA Ops:
  7.2 328.0 %copy-start = (bf16[1,768,2048]{2,1,0:T(8,128)(2,1)S(1)}, bf16[1,768,2048]{2,1,0:T(8,128)(2,1)}, u32[]{:S(2)}) copy-start(bf16[1,768,2048]{2,1,0:T(8,128)(2,1)} %param.21) | copy-start | bytes 9437188
  7.2 14.3 %copy-start.5 = (f32[128,16]{0,1:T(8,128)S(1)}, f32[128,16]{0,1:T(8,128)}, u32[]{:S(2)}) copy-start(f32[128,16]{0,1:T(8,128)} %param.16) | copy-start | bytes 24580
  7.2 71.2 %all-reduce.2.cloned.1.call-start = ((), (), s32[]{:S(2)}) async-start(), calls=%async_computation | async-start | bytes 524288 | tf_op jit(solution)/shard_map/psum | solution.py:191
  8.2 0.7 copy-start.3
  10.9 4.5 collective-permute-start
  15.3 4.4 collective-permute-start.1
  19.7 2.1 copy-start.2
  21.8 159.1 %copy-start.6 = (s32[128,8]{0,1:T(8,128)S(1)}, s32[128,8]{0,1:T(8,128)}, u32[]{:S(2)}) copy-start(s32[128,8]{0,1:T(8,128)} %param.22) | copy-start | bytes 12292
  23.1 158.8 %copy-start.8 = (f32[128,8]{0,1:T(8,128)S(1)}, f32[128,8]{0,1:T(8,128)}, u32[]{:S(2)}) copy-start(f32[128,8]{0,1:T(8,128)} %param.23) | copy-start | bytes 12292
  180.8 14.9 %collective-permute-start.2 = (bf16[2048,1024]{1,0:T(8,128)(2,1)}, bf16[2048,1024]{1,0:T(8,128)(2,1)}, u32[]{:S(2)}, u32[]{:S(2)}) collective-permute-start(bf16[2048,1024]{1,0:T(8,128)(2,1)} %bitcast.66), channel_id=1, source_target_pairs={{0,32},{32,0},{64,96},{96,64},{128,160},{160,128},{192,224},{224,1... | collective-permute-start | bytes 12582920 | tf_op jit(solution)/shard_map/ppermute | solution.py:195
  192.7 6.0 %copy-start.4 = (bf16[128,2048]{1,0:T(8,128)(2,1)S(1)}, bf16[128,2048]{1,0:T(8,128)(2,1)}, u32[]{:S(2)}) copy-start(bf16[128,2048]{1,0:T(8,128)(2,1)} %param.17) | copy-start | bytes 1572868
  195.7 3.3 copy-start.7
  198.8 4.1 copy-start.1
Sparse Core Ops, SparseCore 0:
  10.6 67.7 all-reduce.1

commit v12 on v7

--- a/solution.py
+++ b/solution.py
@@ -30,8 +30,13 @@
 
     core = ctx_me % 2
 
+    bits = max(n_ep - 1, 1).bit_length()
+
     def peer(j):
-        p = (me + j + core * (n_ep - 2 * j)) % n_ep
+        step = j + core * (n_ep - 2 * j)
+        p = 0
+        for b in range(bits):
+            p = p + ((me // 2**b + step // 2**b) % 2) * 2**b
         same = 1 - (p + me) % 2
         return p, same * ctx_me + (1 - same) * ctx_far
 

time: 423 us -> 423 us (level)
  no operation moved by 1% of the time
where the time goes in v12:
time: 423 us; the launch traced here: 419 us
  Pallas kernels  346 us (82%)
  matrix products  36.9 us (9%)
  blocking collectives  12.8 us (3%)
  local copies, waits for them, and re-layouts  10.7 us (3%)
  other arithmetic  8.61 us (2%)
    pallas_call x3, Pallas kernels, exchange(): pl.pallas_call(functools.partial(exchange_kernel, per_peer), out_shape=ja...  346 us
    all_gather x1, blocking collectives, shards(): column_rows = lax.all_gather(out_proj, 'ctx', axis=0, tiled=True)  12.8 us
    dot_general x1, matrix products, run_expert(): gate_up = jnp.dot(flat_in, weight_in, preferred_element_type=jnp.float32)  12.1 us
  transfers between devices with their start and end apart: 3, of which 1 were waited for; matrix products, arithmetic and copies ran while one was open for 6% of the time, Pallas kernels for 0%

profile of v12, /device:TPU:94, one launch (start us, length us, event | category | flops | bytes accessed | tf_op | source)
XLA Modules:
  0.0 419.4 jit_solution(11138886766270835342)
XLA Ops:
  0.7 12.8 %all_gather.3 = bf16[64,2048]{1,0:T(8,128)(2,1)S(1)} all-gather(bf16[8,2048]{1,0:T(8,128)(2,1)} %param.18), channel_id=1, replica_groups=mesh['ctx'=8,'ep'=32] {'ctx'}, dimensions={0}, use_global_device_ids=true | all-gather | bytes 294912 | tf_op jit(solution)/shard_map/all_gather | solution.py:191
  13.5 0.7 dynamic-slice_bitcast_fusion.src_ref
  14.2 103.3 %shard_map.131 = bf16[32,64,1024]{2,1,0:T(8,128)(2,1)} custom-call(bf16[1,64,1024]{2,1,0:T(8,128)(2,1)} %dynamic-slice_bitcast_fusion.src_ref), custom_call_target="tpu_custom_call" | custom-call | bytes 8388608 | tf_op jit(solution)/shard_map/pallas_call | solution.py:101
  117.9 0.7 pad_maximum_fusion
  119.3 0.5 fusion.15
  120.2 2.5 select_reduce_fusion
  122.9 2.0 collective-permute-done
  125.2 4.6 %fusion.2 = pred[1280,128]{1,0:T(8,128)(4,1)S(1)} fusion(s32[128,8]{0,1:T(8,128)S(1)} %multiply_add_fusion), kind=kLoop, calls=%fused_computation.7 | loop fusion | flops 2457600 | bytes 167936 | tf_op jit(solution)/shard_map/reduce_or | solution.py:229
  129.9 2.0 copy.64
  131.8 2.3 copy.47
  134.2 1.0 constant_dynamic-update-slice_fusion
  135.2 1.6 fusion.38
  137.1 0.5 fusion.13
  137.7 0.8 copy-done.3
  138.5 0.9 copy.53
  139.5 2.0 copy.58
  141.6 3.1 convolution_dynamic-update-slice_fusion.1
  144.8 2.9 convolution_dynamic-update-slice_fusion
  148.1 3.9 convolution_convert_fusion.1
  152.0 122.8 %shard_map.132 = bf16[32,40,2048]{2,1,0:T(8,128)(2,1)} custom-call(bf16[32,40,2048]{2,1,0:T(8,128)(2,1)} %bitcast.65), custom_call_target="tpu_custom_call" | custom-call | bytes 10485760 | tf_op jit(solution)/shard_map/pallas_call | solution.py:101
  274.8 12.1 %fusion = f32[1280,1536]{1,0:T(8,128)S(1)} fusion(bf16[1280,2048]{1,0:T(8,128)(2,1)} %bitcast.69, bf16[1,2048,1536]{2,1,0:T(8,128)(2,1)} %param.20), kind=kOutput, calls=%fused_computation.2 | convolution fusion | flops 8053063680 | bytes 19398656 | tf_op jit(solution)/shard_map/dot_general | solution.py:120
  286.9 6.3 %convolution_convert_fusion = bf16[1280,2048]{1,0:T(8,128)(2,1)} fusion(bf16[1,768,2048]{2,1,0:T(8,128)(2,1)S(1)} %copy-done, f32[1280,1536]{1,0:T(8,128)S(1)} %fusion), kind=kOutput, calls=%fused_computation | convolution fusion | flops 4035051520 | bytes 16252928 | tf_op jit(solution)/shard_map/dot_general | solution.py:124
  293.2 120.3 %shard_map.133 = bf16[32,40,2048]{2,1,0:T(8,128)(2,1)} custom-call(bf16[32,40,2048]{2,1,0:T(8,128)(2,1)} %bitcast.70), custom_call_target="tpu_custom_call" | custom-call | bytes 10485760 | tf_op jit(solution)/shard_map/pallas_call | solution.py:101
  413.6 5.8 %fusion.6 = bf16[128,2048]{1,0:T(8,128)(2,1)} fusion(f32[128,1280]{1,0:T(8,128)} %select_reduce_fusion, bf16[1280,2048]{1,0:T(8,128)(2,1)} %bitcast.66, bf16[128,2048]{1,0:T(8,128)(2,1)} %copy-done.1), kind=kOutput, calls=%fused_computation.14 | convolution fusion | flops 4027318272 | bytes 6946816 | tf_op jit(solution)/shard_map/dot_general | solution.py:251
  (50 shorter events, 2.7 us)
Async XLA Ops:
  0.6 286.3 %copy-start = (bf16[1,768,2048]{2,1,0:T(8,128)(2,1)S(1)}, bf16[1,768,2048]{2,1,0:T(8,128)(2,1)}, u32[]{:S(2)}) copy-start(bf16[1,768,2048]{2,1,0:T(8,128)(2,1)} %param.21) | copy-start | bytes 9437188
  0.6 117.0 %copy-start.6 = (bf16[128,256]{1,0:T(8,128)(2,1)S(1)}, bf16[128,256]{1,0:T(8,128)(2,1)}, u32[]{:S(2)}) copy-start(bf16[128,256]{1,0:T(8,128)(2,1)} %param.13) | copy-start | bytes 196612
  0.7 117.1 %copy-start.7 = (bf16[128,256]{1,0:T(8,128)(2,1)S(1)}, bf16[128,256]{1,0:T(8,128)(2,1)}, u32[]{:S(2)}) copy-start(bf16[128,256]{1,0:T(8,128)(2,1)} %param.14) | copy-start | bytes 196612
  0.7 118.4 %copy-start.9 = (s32[128,8]{0,1:T(8,128)S(1)}, s32[128,8]{0,1:T(8,128)}, u32[]{:S(2)}) copy-start(s32[128,8]{0,1:T(8,128)} %param.22) | copy-start | bytes 12292
  0.7 119.4 %copy-start.11 = (f32[128,8]{0,1:T(8,128)S(1)}, f32[128,8]{0,1:T(8,128)}, u32[]{:S(2)}) copy-start(f32[128,8]{0,1:T(8,128)} %param.23) | copy-start | bytes 12292
  117.6 27.2 %collective-permute-start.2 = (bf16[2048,1024]{1,0:T(8,128)(2,1)}, bf16[2048,1024]{1,0:T(8,128)(2,1)}, u32[]{:S(2)}, u32[]{:S(2)}) collective-permute-start(bf16[2048,1024]{1,0:T(8,128)(2,1)} %bitcast.67), channel_id=1, source_target_pairs={{0,32},{32,0},{64,96},{96,64},{128,160},{160,128},{192,224},{224,1... | collective-permute-start | bytes 12582920 | tf_op jit(solution)/shard_map/ppermute | solution.py:194
  118.6 6.2 %collective-permute-start = (bf16[2,128,256]{1,2,0:T(8,128)(2,1)}, bf16[2,128,256]{1,2,0:T(8,128)(2,1)S(1)}, u32[]{:S(2)}, u32[]{:S(2)}) collective-permute-start(bf16[2,128,256]{1,2,0:T(8,128)(2,1)} %pad_maximum_fusion), channel_id=1, source_target_pairs={{0,32},{32,64},{64,96},{96,128},{128,160},{160,192},{192,224},{224... | collective-permute-start | bytes 393224 | tf_op jit(solution)/shard_map/ppermute | solution.py:21
  119.8 17.0 %copy-start.8 = (f32[128,16]{0,1:T(8,128)S(1)}, f32[128,16]{0,1:T(8,128)}, u32[]{:S(2)}) copy-start(f32[128,16]{0,1:T(8,128)} %param.16) | copy-start | bytes 24580
  124.8 9.3 %collective-permute-start.1 = (bf16[2,128,256]{1,2,0:T(8,128)(2,1)S(1)}, bf16[2,128,256]{1,2,0:T(8,128)(2,1)}, u32[]{:S(2)}, u32[]{:S(2)}) collective-permute-start(bf16[2,128,256]{1,2,0:T(8,128)(2,1)S(1)} %collective-permute-done), channel_id=1, source_target_pairs={{0,32},{32,64},{64,96},{96,128},{128,160},{160,192},{192,224},{224... | collective-permute-start | bytes 393224 | tf_op jit(solution)/shard_map/ppermute | solution.py:21
  134.1 3.0 copy-start.4
  137.7 0.8 copy-start.3
  141.5 3.3 copy-start.2
  141.6 6.1 %copy-start.5 = (bf16[128,2048]{1,0:T(8,128)(2,1)S(1)}, bf16[128,2048]{1,0:T(8,128)(2,1)}, u32[]{:S(2)}) copy-start(bf16[128,2048]{1,0:T(8,128)(2,1)} %param.17) | copy-start | bytes 1572868
  144.8 3.3 copy-start.10
  147.9 4.1 copy-start.1

commit v13 on v12

--- a/solution.py
+++ b/solution.py
@@ -188,7 +188,16 @@
     model_width = out_proj.shape[1]
     column_half = model_width // 2
     core = ctx_here % 2
-    column_rows = lax.all_gather(out_proj, "ctx", axis=0, tiled=True)
+    block_count = out_proj.shape[0]
+    column_rows = jnp.zeros((ctx_count * block_count, model_width), out_proj.dtype)
+    column_rows = lax.dynamic_update_slice_in_dim(
+        column_rows, out_proj, ctx_here * block_count, axis=0
+    )
+    for shift in range(1, ctx_count):
+        arrived_block = passed_along(out_proj, "ctx", shift)
+        column_rows = lax.dynamic_update_slice_in_dim(
+            column_rows, arrived_block, ((ctx_here - shift) % ctx_count) * block_count, axis=0
+        )
     own_half = lax.dynamic_slice_in_dim(column_rows, core * column_half, column_half, axis=1)
     own_half = exchange(own_half[None], False, 0).reshape(-1, column_half)
     other_half = lax.ppermute(own_half, "ctx", [(i, i ^ 1) for i in range(ctx_count)])

time: 423 us -> 421 us (level)
  blocking collectives: 12.8 us -> 0 us
  starting transfers between devices: 0.95 us -> 8.52 us
  local copies, waits for them, and re-layouts: 10.7 us -> 15.3 us
    all_gather x1 -> x0, blocking collectives: 12.8 us -> none  [shards(): column_rows = lax.all_gather(out_proj, 'ctx', axis=0, tiled=True)]
    ppermute x2 -> x9, starting transfers between devices: 0.86 us -> 8.42 us  [passed_along(): lax.ppermute(shard, axis, [(i, (i + by) % devices) for i in range(devices)])]
    dynamic_update_slice x0 -> x8, local copies, waits for them, and re-layouts: none -> 4.62 us  [the longest x7 3.82 us: shards(): lax.dynamic_update_slice_in_dim(column_rows, arrived_block, (ctx_here - s...]
  transfers between devices with their start and end apart: 3 -> 10, of which waited for: 1 -> 1; matrix products, arithmetic and copies ran while one was open for 6% -> 7% of each run, Pallas kernels for 0% -> 0%
where the time goes in v13:
time: 421 us; the launch traced here: 417 us
  Pallas kernels  345 us (82%)
  matrix products  36.8 us (9%)
  local copies, waits for them, and re-layouts  15.3 us (4%)
  other arithmetic  8.59 us (2%)
  starting transfers between devices  8.52 us (2%)
    pallas_call x3, Pallas kernels, exchange(): pl.pallas_call(functools.partial(exchange_kernel, per_peer), out_shape=ja...  345 us
    dot_general x1, matrix products, run_expert(): gate_up = jnp.dot(flat_in, weight_in, preferred_element_type=jnp.float32)  12.1 us
    ppermute x9, starting transfers between devices, passed_along(): lax.ppermute(shard, axis, [(i, (i + by) % devices) for i in range(devices)])  8.42 us
  transfers between devices with their start and end apart: 10, of which 1 were waited for; matrix products, arithmetic and copies ran while one was open for 7% of the time, Pallas kernels for 0%

profile of v13, /device:TPU:94, one launch (start us, length us, event | category | flops | bytes accessed | tf_op | source)
XLA Modules:
  0.0 417.2 jit_solution(17739935670965183796)
XLA Ops:
  0.8 2.0 collective-permute-start.3
  3.2 2.4 collective-permute-start.5
  5.6 0.8 constant_dynamic-update-slice_fusion.9
  6.4 1.2 collective-permute-start.7
  8.4 1.5 collective-permute-start.8
  13.6 101.5 %shard_map.131 = bf16[32,64,1024]{2,1,0:T(8,128)(2,1)} custom-call(bf16[1,64,1024]{2,1,0:T(8,128)(2,1)} %dynamic-slice_bitcast_fusion.src_ref), custom_call_target="tpu_custom_call" | custom-call | bytes 8388608 | tf_op jit(solution)/shard_map/pallas_call | solution.py:101
  117.8 2.5 select_reduce_fusion
  120.4 2.0 collective-permute-done
  122.8 4.6 %fusion.2 = pred[1280,128]{1,0:T(8,128)(4,1)S(1)} fusion(s32[128,8]{0,1:T(8,128)S(1)} %multiply_add_fusion), kind=kLoop, calls=%fused_computation.7 | loop fusion | flops 2457600 | bytes 167936 | tf_op jit(solution)/shard_map/reduce_or | solution.py:238
  127.5 2.0 copy.64
  129.4 2.3 copy.47
  131.7 1.0 constant_dynamic-update-slice_fusion
  132.8 1.6 fusion.38
  135.3 0.8 copy-done.3
  136.1 0.9 copy.53
  137.0 2.0 copy.58
  139.2 3.1 convolution_dynamic-update-slice_fusion.1
  142.4 2.9 convolution_dynamic-update-slice_fusion
  145.7 3.9 convolution_convert_fusion.1
  149.6 123.5 %shard_map.132 = bf16[32,40,2048]{2,1,0:T(8,128)(2,1)} custom-call(bf16[32,40,2048]{2,1,0:T(8,128)(2,1)} %bitcast.65), custom_call_target="tpu_custom_call" | custom-call | bytes 10485760 | tf_op jit(solution)/shard_map/pallas_call | solution.py:101
  273.1 12.1 %fusion = f32[1280,1536]{1,0:T(8,128)S(1)} fusion(bf16[1280,2048]{1,0:T(8,128)(2,1)} %bitcast.69, bf16[1,2048,1536]{2,1,0:T(8,128)(2,1)} %param.20), kind=kOutput, calls=%fused_computation.2 | convolution fusion | flops 8053063680 | bytes 19398656 | tf_op jit(solution)/shard_map/dot_general | solution.py:120
  285.2 6.3 %convolution_convert_fusion = bf16[1280,2048]{1,0:T(8,128)(2,1)} fusion(bf16[1,768,2048]{2,1,0:T(8,128)(2,1)S(1)} %copy-done, f32[1280,1536]{1,0:T(8,128)S(1)} %fusion), kind=kOutput, calls=%fused_computation | convolution fusion | flops 4035051520 | bytes 16252928 | tf_op jit(solution)/shard_map/dot_general | solution.py:124
  291.5 119.9 %shard_map.133 = bf16[32,40,2048]{2,1,0:T(8,128)(2,1)} custom-call(bf16[32,40,2048]{2,1,0:T(8,128)(2,1)} %bitcast.70), custom_call_target="tpu_custom_call" | custom-call | bytes 10485760 | tf_op jit(solution)/shard_map/pallas_call | solution.py:101
  411.4 5.8 %fusion.6 = bf16[128,2048]{1,0:T(8,128)(2,1)} fusion(f32[128,1280]{1,0:T(8,128)} %select_reduce_fusion, bf16[1280,2048]{1,0:T(8,128)(2,1)} %bitcast.66, bf16[128,2048]{1,0:T(8,128)(2,1)} %copy-done.1), kind=kOutput, calls=%fused_computation.14 | convolution fusion | flops 4027318272 | bytes 6946816 | tf_op jit(solution)/shard_map/dot_general | solution.py:260
  (72 shorter events, 9.5 us)
Async XLA Ops:
  0.6 284.5 %copy-start = (bf16[1,768,2048]{2,1,0:T(8,128)(2,1)S(1)}, bf16[1,768,2048]{2,1,0:T(8,128)(2,1)}, u32[]{:S(2)}) copy-start(bf16[1,768,2048]{2,1,0:T(8,128)(2,1)} %param.21) | copy-start | bytes 9437188
  0.6 114.6 %copy-start.6 = (bf16[128,256]{1,0:T(8,128)(2,1)S(1)}, bf16[128,256]{1,0:T(8,128)(2,1)}, u32[]{:S(2)}) copy-start(bf16[128,256]{1,0:T(8,128)(2,1)} %param.13) | copy-start | bytes 196612
  0.7 114.7 %copy-start.7 = (bf16[128,256]{1,0:T(8,128)(2,1)S(1)}, bf16[128,256]{1,0:T(8,128)(2,1)}, u32[]{:S(2)}) copy-start(bf16[128,256]{1,0:T(8,128)(2,1)} %param.14) | copy-start | bytes 196612
  0.7 116.0 %copy-start.9 = (s32[128,8]{0,1:T(8,128)S(1)}, s32[128,8]{0,1:T(8,128)}, u32[]{:S(2)}) copy-start(s32[128,8]{0,1:T(8,128)} %param.22) | copy-start | bytes 12292
  0.7 117.0 %copy-start.11 = (f32[128,8]{0,1:T(8,128)S(1)}, f32[128,8]{0,1:T(8,128)}, u32[]{:S(2)}) copy-start(f32[128,8]{0,1:T(8,128)} %param.23) | copy-start | bytes 12292
  0.7 5.8 %collective-permute-start.2 = (bf16[8,2048]{1,0:T(8,128)(2,1)}, bf16[8,2048]{1,0:T(8,128)(2,1)}, u32[]{:S(2)}, u32[]{:S(2)}) collective-permute-start(bf16[8,2048]{1,0:T(8,128)(2,1)} %param.18), channel_id=1, source_target_pairs={{0,32},{32,64},{64,96},{96,128},{128,160},{160,192},{192,224},{224... | collective-permute-start | bytes 98312 | tf_op jit(solution)/shard_map/ppermute | solution.py:21
  0.8 7.6 %collective-permute-start.3 = (bf16[8,2048]{1,0:T(8,128)(2,1)}, bf16[8,2048]{1,0:T(8,128)(2,1)}, u32[]{:S(2)}, u32[]{:S(2)}) collective-permute-start(bf16[8,2048]{1,0:T(8,128)(2,1)} %param.18), channel_id=1, source_target_pairs={{0,64},{32,96},{64,128},{96,160},{128,192},{160,224},{192,0},{224,... | collective-permute-start | bytes 98312 | tf_op jit(solution)/shard_map/ppermute | solution.py:21
  2.8 7.8 %collective-permute-start.4 = (bf16[8,2048]{1,0:T(8,128)(2,1)}, bf16[8,2048]{1,0:T(8,128)(2,1)}, u32[]{:S(2)}, u32[]{:S(2)}) collective-permute-start(bf16[8,2048]{1,0:T(8,128)(2,1)} %param.18), channel_id=1, source_target_pairs={{0,96},{32,128},{64,160},{96,192},{128,224},{160,0},{192,32},{224,... | collective-permute-start | bytes 98312 | tf_op jit(solution)/shard_map/ppermute | solution.py:21
  3.2 8.1 %collective-permute-start.5 = (bf16[8,2048]{1,0:T(8,128)(2,1)}, bf16[8,2048]{1,0:T(8,128)(2,1)}, u32[]{:S(2)}, u32[]{:S(2)}) collective-permute-start(bf16[8,2048]{1,0:T(8,128)(2,1)} %param.18), channel_id=1, source_target_pairs={{0,128},{32,160},{64,192},{96,224},{128,0},{160,32},{192,64},{224,... | collective-permute-start | bytes 98312 | tf_op jit(solution)/shard_map/ppermute | solution.py:21
  5.6 6.5 %collective-permute-start.6 = (bf16[8,2048]{1,0:T(8,128)(2,1)}, bf16[8,2048]{1,0:T(8,128)(2,1)}, u32[]{:S(2)}, u32[]{:S(2)}) collective-permute-start(bf16[8,2048]{1,0:T(8,128)(2,1)} %param.18), channel_id=1, source_target_pairs={{0,160},{32,192},{64,224},{96,0},{128,32},{160,64},{192,96},{224,1... | collective-permute-start | bytes 98312 | tf_op jit(solution)/shard_map/ppermute | solution.py:21
  6.4 6.5 %collective-permute-start.7 = (bf16[8,2048]{1,0:T(8,128)(2,1)}, bf16[8,2048]{1,0:T(8,128)(2,1)S(1)}, u32[]{:S(2)}, u32[]{:S(2)}) collective-permute-start(bf16[8,2048]{1,0:T(8,128)(2,1)} %param.18), channel_id=1, source_target_pairs={{0,192},{32,224},{64,0},{96,32},{128,64},{160,96},{192,128},{224,1... | collective-permute-start | bytes 98312 | tf_op jit(solution)/shard_map/ppermute | solution.py:21
  8.4 4.6 %collective-permute-start.8 = (bf16[8,2048]{1,0:T(8,128)(2,1)}, bf16[8,2048]{1,0:T(8,128)(2,1)S(1)}, u32[]{:S(2)}, u32[]{:S(2)}) collective-permute-start(bf16[8,2048]{1,0:T(8,128)(2,1)} %param.18), channel_id=1, source_target_pairs={{0,224},{32,0},{64,32},{96,64},{128,96},{160,128},{192,160},{224,1... | collective-permute-start | bytes 98312 | tf_op jit(solution)/shard_map/ppermute | solution.py:21
  115.1 27.2 %collective-permute-start.9 = (bf16[2048,1024]{1,0:T(8,128)(2,1)}, bf16[2048,1024]{1,0:T(8,128)(2,1)}, u32[]{:S(2)}, u32[]{:S(2)}) collective-permute-start(bf16[2048,1024]{1,0:T(8,128)(2,1)} %bitcast.67), channel_id=1, source_target_pairs={{0,32},{32,0},{64,96},{96,64},{128,160},{160,128},{192,224},{224,1... | collective-permute-start | bytes 12582920 | tf_op jit(solution)/shard_map/ppermute | solution.py:203
  116.2 6.2 %collective-permute-start = (bf16[2,128,256]{1,2,0:T(8,128)(2,1)}, bf16[2,128,256]{1,2,0:T(8,128)(2,1)S(1)}, u32[]{:S(2)}, u32[]{:S(2)}) collective-permute-start(bf16[2,128,256]{1,2,0:T(8,128)(2,1)} %pad_maximum_fusion), channel_id=1, source_target_pairs={{0,32},{32,64},{64,96},{96,128},{128,160},{160,192},{192,224},{224... | collective-permute-start | bytes 393224 | tf_op jit(solution)/shard_map/ppermute | solution.py:21
  117.4 17.0 %copy-start.8 = (f32[128,16]{0,1:T(8,128)S(1)}, f32[128,16]{0,1:T(8,128)}, u32[]{:S(2)}) copy-start(f32[128,16]{0,1:T(8,128)} %param.16) | copy-start | bytes 24580
  122.4 9.3 %collective-permute-start.1 = (bf16[2,128,256]{1,2,0:T(8,128)(2,1)S(1)}, bf16[2,128,256]{1,2,0:T(8,128)(2,1)}, u32[]{:S(2)}, u32[]{:S(2)}) collective-permute-start(bf16[2,128,256]{1,2,0:T(8,128)(2,1)S(1)} %collective-permute-done), channel_id=1, source_target_pairs={{0,32},{32,64},{64,96},{96,128},{128,160},{160,192},{192,224},{224... | collective-permute-start | bytes 393224 | tf_op jit(solution)/shard_map/ppermute | solution.py:21
  131.7 3.0 copy-start.4
  135.3 0.8 copy-start.3
  139.1 3.3 copy-start.2
  139.2 6.1 %copy-start.5 = (bf16[128,2048]{1,0:T(8,128)(2,1)S(1)}, bf16[128,2048]{1,0:T(8,128)(2,1)}, u32[]{:S(2)}) copy-start(bf16[128,2048]{1,0:T(8,128)(2,1)} %param.17) | copy-start | bytes 1572868
  142.3 3.3 copy-start.10
  145.5 4.1 copy-start.1

commit v14 on v13

--- a/solution.py
+++ b/solution.py
@@ -199,6 +199,7 @@
             column_rows, arrived_block, ((ctx_here - shift) % ctx_count) * block_count, axis=0
         )
     own_half = lax.dynamic_slice_in_dim(column_rows, core * column_half, column_half, axis=1)
+    own_half, attended = lax.optimization_barrier((own_half, attended))
     own_half = exchange(own_half[None], False, 0).reshape(-1, column_half)
     other_half = lax.ppermute(own_half, "ctx", [(i, i ^ 1) for i in range(ctx_count)])
     block_rows = out_proj.shape[0]

time: 421 us -> 423 us (level)
  waiting for transfers between devices: 2 us -> 6.28 us
    ppermute x9, waiting for transfers between devices: 2 us -> 6.28 us  [passed_along(): lax.ppermute(shard, axis, [(i, (i + by) % devices) for i in range(devices)])]
  transfers between devices with their start and end apart: 10 -> 10, of which waited for: 1 -> 2; matrix products, arithmetic and copies ran while one was open for 7% -> 7% of each run, Pallas kernels for 0% -> 0%
where the time goes in v14:
time: 423 us; the launch traced here: 419 us
  Pallas kernels  342 us (81%)
  matrix products  37.5 us (9%)
  local copies, waits for them, and re-layouts  15.3 us (4%)
  other arithmetic  9.39 us (2%)
  starting transfers between devices  7.69 us (2%)
  waiting for transfers between devices  6.28 us (1%)
    pallas_call x3, Pallas kernels, exchange(): pl.pallas_call(functools.partial(exchange_kernel, per_peer), out_shape=ja...  342 us
    dot_general x1, matrix products, run_expert(): gate_up = jnp.dot(flat_in, weight_in, preferred_element_type=jnp.float32)  12.1 us
  transfers between devices with their start and end apart: 10, of which 2 were waited for; matrix products, arithmetic and copies ran while one was open for 7% of the time, Pallas kernels for 0%

profile of v14, /device:TPU:94, one launch (start us, length us, event | category | flops | bytes accessed | tf_op | source)
XLA Modules:
  0.0 419.2 jit_solution(18123473505547175033)
XLA Ops:
  0.7 2.0 collective-permute-start.1
  3.2 2.4 collective-permute-start.3
  6.6 1.0 copy.60
  9.7 2.0 copy.75
  11.7 2.2 copy.58
  13.9 1.2 collective-permute-start.5
  15.9 1.5 collective-permute-start.6
  20.5 2.6 collective-permute-done.7
  23.7 3.7 collective-permute-done.8
  27.5 1.6 fusion.38
  29.4 1.3 fusion.13
  30.8 100.5 %shard_map.131 = bf16[32,64,1024]{2,1,0:T(8,128)(2,1)} custom-call(bf16[1,64,1024]{2,1,0:T(8,128)(2,1)} %bitcast.76), custom_call_target="tpu_custom_call" | custom-call | bytes 8388608 | tf_op jit(solution)/shard_map/pallas_call | solution.py:101
  132.5 4.8 %fusion.2 = pred[1280,128]{1,0:T(8,128)(4,1)S(1)} fusion(s32[128,8]{0,1:T(8,128)S(1)} %multiply_add_fusion), kind=kLoop, calls=%fused_computation.7 | loop fusion | flops 2457600 | bytes 167936 | tf_op jit(solution)/shard_map/reduce_or | solution.py:239
  137.3 2.5 select_reduce_fusion
  139.8 2.0 copy.69
  141.8 1.2 copy.64
  143.1 3.0 convolution_dynamic-update-slice_fusion.1
  146.2 2.9 convolution_dynamic-update-slice_fusion
  149.5 3.9 convolution_convert_fusion.1
  153.4 122.9 %shard_map.132 = bf16[32,40,2048]{2,1,0:T(8,128)(2,1)} custom-call(bf16[32,40,2048]{2,1,0:T(8,128)(2,1)} %bitcast.64), custom_call_target="tpu_custom_call" | custom-call | bytes 10485760 | tf_op jit(solution)/shard_map/pallas_call | solution.py:101
  276.2 12.1 %fusion = f32[1280,1536]{1,0:T(8,128)S(1)} fusion(bf16[1280,2048]{1,0:T(8,128)(2,1)} %bitcast.68, bf16[1,2048,1536]{2,1,0:T(8,128)(2,1)} %param.20), kind=kOutput, calls=%fused_computation.2 | convolution fusion | flops 8053063680 | bytes 19398656 | tf_op jit(solution)/shard_map/dot_general | solution.py:120
  288.3 6.3 %convolution_convert_fusion = bf16[1280,2048]{1,0:T(8,128)(2,1)} fusion(bf16[1,768,2048]{2,1,0:T(8,128)(2,1)S(1)} %copy-done, f32[1280,1536]{1,0:T(8,128)S(1)} %fusion), kind=kOutput, calls=%fused_computation | convolution fusion | flops 4035051520 | bytes 16252928 | tf_op jit(solution)/shard_map/dot_general | solution.py:124
  294.6 118.8 %shard_map.133 = bf16[32,40,2048]{2,1,0:T(8,128)(2,1)} custom-call(bf16[32,40,2048]{2,1,0:T(8,128)(2,1)} %bitcast.69), custom_call_target="tpu_custom_call" | custom-call | bytes 10485760 | tf_op jit(solution)/shard_map/pallas_call | solution.py:101
  413.4 5.8 %fusion.6 = bf16[128,2048]{1,0:T(8,128)(2,1)} fusion(f32[128,1280]{1,0:T(8,128)} %select_reduce_fusion, bf16[1280,2048]{1,0:T(8,128)(2,1)} %bitcast.65, bf16[128,2048]{1,0:T(8,128)(2,1)} %copy-done.1), kind=kOutput, calls=%fused_computation.14 | convolution fusion | flops 4027318272 | bytes 6946816 | tf_op jit(solution)/shard_map/dot_general | solution.py:261
  (66 shorter events, 10.3 us)
Async XLA Ops:
  0.6 287.7 %copy-start = (bf16[1,768,2048]{2,1,0:T(8,128)(2,1)S(1)}, bf16[1,768,2048]{2,1,0:T(8,128)(2,1)}, u32[]{:S(2)}) copy-start(bf16[1,768,2048]{2,1,0:T(8,128)(2,1)} %param.21) | copy-start | bytes 9437188
  0.6 28.4 %copy-start.5 = (f32[128,16]{0,1:T(8,128)S(1)}, f32[128,16]{0,1:T(8,128)}, u32[]{:S(2)}) copy-start(f32[128,16]{0,1:T(8,128)} %param.16) | copy-start | bytes 24580
  0.7 13.2 %collective-permute-start = (bf16[8,2048]{1,0:T(8,128)(2,1)}, bf16[8,2048]{1,0:T(8,128)(2,1)}, u32[]{:S(2)}, u32[]{:S(2)}) collective-permute-start(bf16[8,2048]{1,0:T(8,128)(2,1)} %param.18), channel_id=1, source_target_pairs={{0,32},{32,64},{64,96},{96,128},{128,160},{160,192},{192,224},{224... | collective-permute-start | bytes 98312 | tf_op jit(solution)/shard_map/ppermute | solution.py:21
  0.7 15.1 %collective-permute-start.1 = (bf16[8,2048]{1,0:T(8,128)(2,1)}, bf16[8,2048]{1,0:T(8,128)(2,1)}, u32[]{:S(2)}, u32[]{:S(2)}) collective-permute-start(bf16[8,2048]{1,0:T(8,128)(2,1)} %param.18), channel_id=1, source_target_pairs={{0,64},{32,96},{64,128},{96,160},{128,192},{160,224},{192,0},{224,... | collective-permute-start | bytes 98312 | tf_op jit(solution)/shard_map/ppermute | solution.py:21
  2.7 15.4 %collective-permute-start.2 = (bf16[8,2048]{1,0:T(8,128)(2,1)}, bf16[8,2048]{1,0:T(8,128)(2,1)}, u32[]{:S(2)}, u32[]{:S(2)}) collective-permute-start(bf16[8,2048]{1,0:T(8,128)(2,1)} %param.18), channel_id=1, source_target_pairs={{0,96},{32,128},{64,160},{96,192},{128,224},{160,0},{192,32},{224,... | collective-permute-start | bytes 98312 | tf_op jit(solution)/shard_map/ppermute | solution.py:21
  3.2 15.7 %collective-permute-start.3 = (bf16[8,2048]{1,0:T(8,128)(2,1)}, bf16[8,2048]{1,0:T(8,128)(2,1)}, u32[]{:S(2)}, u32[]{:S(2)}) collective-permute-start(bf16[8,2048]{1,0:T(8,128)(2,1)} %param.18), channel_id=1, source_target_pairs={{0,128},{32,160},{64,192},{96,224},{128,0},{160,32},{192,64},{224,... | collective-permute-start | bytes 98312 | tf_op jit(solution)/shard_map/ppermute | solution.py:21
  5.6 14.1 %collective-permute-start.4 = (bf16[8,2048]{1,0:T(8,128)(2,1)}, bf16[8,2048]{1,0:T(8,128)(2,1)}, u32[]{:S(2)}, u32[]{:S(2)}) collective-permute-start(bf16[8,2048]{1,0:T(8,128)(2,1)} %param.18), channel_id=1, source_target_pairs={{0,160},{32,192},{64,224},{96,0},{128,32},{160,64},{192,96},{224,1... | collective-permute-start | bytes 98312 | tf_op jit(solution)/shard_map/ppermute | solution.py:21
  9.7 17.7 %copy-start.4 = (pred[128,256]{0,1:T(8,128)(4,1)S(1)}, pred[128,256]{0,1:T(8,128)(4,1)}, u32[]{:S(2)}) copy-start(pred[128,256]{0,1:T(8,128)(4,1)} %fusion.26) | copy-start | bytes 98308
  13.9 15.5 %copy-start.2 = (f32[128,2048]{0,1:T(8,128)S(1)}, f32[128,2048]{0,1:T(8,128)}, u32[]{:S(2)}) copy-start(f32[128,2048]{0,1:T(8,128)} %copy.58) | copy-start | bytes 3145732
  13.9 6.5 %collective-permute-start.5 = (bf16[8,2048]{1,0:T(8,128)(2,1)}, bf16[8,2048]{1,0:T(8,128)(2,1)S(1)}, u32[]{:S(2)}, u32[]{:S(2)}) collective-permute-start(bf16[8,2048]{1,0:T(8,128)(2,1)} %param.18), channel_id=1, source_target_pairs={{0,192},{32,224},{64,0},{96,32},{128,64},{160,96},{192,128},{224,1... | collective-permute-start | bytes 98312 | tf_op jit(solution)/shard_map/ppermute | solution.py:21
  15.9 4.6 %collective-permute-start.6 = (bf16[8,2048]{1,0:T(8,128)(2,1)}, bf16[8,2048]{1,0:T(8,128)(2,1)S(1)}, u32[]{:S(2)}, u32[]{:S(2)}) collective-permute-start(bf16[8,2048]{1,0:T(8,128)(2,1)} %param.18), channel_id=1, source_target_pairs={{0,224},{32,0},{64,32},{96,64},{128,96},{160,128},{192,160},{224,1... | collective-permute-start | bytes 98312 | tf_op jit(solution)/shard_map/ppermute | solution.py:21
  18.1 4.9 %collective-permute-start.7 = (bf16[2,128,256]{1,2,0:T(8,128)(2,1)}, bf16[2,128,256]{1,2,0:T(8,128)(2,1)S(1)}, u32[]{:S(2)}, u32[]{:S(2)}) collective-permute-start(bf16[2,128,256]{1,2,0:T(8,128)(2,1)} %pad_maximum_fusion), channel_id=1, source_target_pairs={{0,32},{32,64},{64,96},{96,128},{128,160},{160,192},{192,224},{224... | collective-permute-start | bytes 393224 | tf_op jit(solution)/shard_map/ppermute | solution.py:21
  23.0 4.4 %collective-permute-start.8 = (bf16[2,128,256]{1,2,0:T(8,128)(2,1)S(1)}, bf16[2,128,256]{1,2,0:T(8,128)(2,1)S(1)}, u32[]{:S(2)}, u32[]{:S(2)}) collective-permute-start(bf16[2,128,256]{1,2,0:T(8,128)(2,1)S(1)} %collective-permute-done.7), channel_id=1, source_target_pairs={{0,32},{32,64},{64,96},{96,128},{128,160},{160,192},{192,224},{224... | collective-permute-start | bytes 393224 | tf_op jit(solution)/shard_map/ppermute | solution.py:21
  29.4 101.9 %copy-start.6 = (s32[128,8]{0,1:T(8,128)S(1)}, s32[128,8]{0,1:T(8,128)}, u32[]{:S(2)}) copy-start(s32[128,8]{0,1:T(8,128)} %param.22) | copy-start | bytes 12292
  30.8 101.6 %copy-start.8 = (f32[128,8]{0,1:T(8,128)S(1)}, f32[128,8]{0,1:T(8,128)}, u32[]{:S(2)}) copy-start(f32[128,8]{0,1:T(8,128)} %param.23) | copy-start | bytes 12292
  131.2 14.9 %collective-permute-start.9 = (bf16[2048,1024]{1,0:T(8,128)(2,1)}, bf16[2048,1024]{1,0:T(8,128)(2,1)}, u32[]{:S(2)}, u32[]{:S(2)}) collective-permute-start(bf16[2048,1024]{1,0:T(8,128)(2,1)} %bitcast.66), channel_id=1, source_target_pairs={{0,32},{32,0},{64,96},{96,64},{128,160},{160,128},{192,224},{224,1... | collective-permute-start | bytes 12582920 | tf_op jit(solution)/shard_map/ppermute | solution.py:204
  143.1 6.0 %copy-start.3 = (bf16[128,2048]{1,0:T(8,128)(2,1)S(1)}, bf16[128,2048]{1,0:T(8,128)(2,1)}, u32[]{:S(2)}) copy-start(bf16[128,2048]{1,0:T(8,128)(2,1)} %param.17) | copy-start | bytes 1572868
  146.1 3.3 copy-start.7
  149.2 4.1 copy-start.1

commit v15 on v13

--- a/solution.py
+++ b/solution.py
@@ -193,11 +193,11 @@
     column_rows = lax.dynamic_update_slice_in_dim(
         column_rows, out_proj, ctx_here * block_count, axis=0
     )
-    for shift in range(1, ctx_count):
-        arrived_block = passed_along(out_proj, "ctx", shift)
-        column_rows = lax.dynamic_update_slice_in_dim(
-            column_rows, arrived_block, ((ctx_here - shift) % ctx_count) * block_count, axis=0
-        )
+    distance = 1
+    while distance < ctx_count:
+        partner = [(i, i ^ distance) for i in range(ctx_count)]
+        column_rows = column_rows + lax.ppermute(column_rows, "ctx", partner)
+        distance *= 2
     own_half = lax.dynamic_slice_in_dim(column_rows, core * column_half, column_half, axis=1)
     own_half = exchange(own_half[None], False, 0).reshape(-1, column_half)
     other_half = lax.ppermute(own_half, "ctx", [(i, i ^ 1) for i in range(ctx_count)])

time: 421 us -> 433 us (1.029)
  waiting for transfers between devices: 2 us -> 21.2 us
  starting transfers between devices: 8.52 us -> 3.05 us
    ppermute x0 -> x3, waiting for transfers between devices: none -> 19.2 us  [shards(): column_rows = column_rows + lax.ppermute(column_rows, 'ctx', partner)]
    ppermute x9 -> x2, starting transfers between devices: 8.42 us -> 0.86 us  [passed_along(): lax.ppermute(shard, axis, [(i, (i + by) % devices) for i in range(devices)])]
  transfers between devices with their start and end apart: 10 -> 6, of which waited for: 1 -> 4; matrix products, arithmetic and copies ran while one was open for 7% -> 5% of each run, Pallas kernels for 0% -> 0%
where the time goes in v15:
time: 433 us; the launch traced here: 430 us
  Pallas kernels  346 us (80%)
  matrix products  36.9 us (9%)
  waiting for transfers between devices  21.2 us (5%)
  local copies, waits for them, and re-layouts  11 us (3%)
  other arithmetic  11 us (3%)
    pallas_call x3, Pallas kernels, exchange(): pl.pallas_call(functools.partial(exchange_kernel, per_peer), out_shape=ja...  346 us
    ppermute x3, waiting for transfers between devices, shards(): column_rows = column_rows + lax.ppermute(column_rows, 'ctx', partner)  19.2 us
    dot_general x1, matrix products, run_expert(): gate_up = jnp.dot(flat_in, weight_in, preferred_element_type=jnp.float32)  12.1 us
  transfers between devices with their start and end apart: 6, of which 4 were waited for; matrix products, arithmetic and copies ran while one was open for 5% of the time, Pallas kernels for 0%

profile of v15, /device:TPU:94, one launch (start us, length us, event | category | flops | bytes accessed | tf_op | source)
XLA Modules:
  0.0 430.2 jit_solution(17911217008823835492)
XLA Ops:
  0.7 0.9 constant_dynamic-update-slice_fusion.2
  1.6 1.5 collective-permute-done.2
  3.9 2.0 collective-permute-start.3
  6.0 6.6 %collective-permute-done.3 = bf16[64,2048]{1,0:T(8,128)(2,1)S(1)} collective-permute-done((bf16[64,2048]{1,0:T(8,128)(2,1)S(1)}, bf16[64,2048]{1,0:T(8,128)(2,1)S(1)}, u32[]{:S(2)}, u32[]{:S(2)}) %collective-permute-start.3) | collective-permute-done | bytes 262176 | tf_op jit(solution)/shard_map/ppermute | solution.py:199
  12.7 11.1 %collective-permute-done.4 = bf16[64,2048]{1,0:T(8,128)(2,1)} collective-permute-done((bf16[64,2048]{1,0:T(8,128)(2,1)S(1)}, bf16[64,2048]{1,0:T(8,128)(2,1)}, u32[]{:S(2)}, u32[]{:S(2)}) %collective-permute-start.4) | collective-permute-done | bytes 262176 | tf_op jit(solution)/shard_map/ppermute | solution.py:199
  23.9 1.6 fusion.25.src_ref
  25.4 103.7 %shard_map.131 = bf16[32,64,1024]{2,1,0:T(8,128)(2,1)} custom-call(bf16[1,64,1024]{2,1,0:T(8,128)(2,1)} %fusion.25.src_ref), custom_call_target="tpu_custom_call" | custom-call | bytes 8388608 | tf_op jit(solution)/shard_map/pallas_call | solution.py:101
  131.8 2.5 select_reduce_fusion
  134.4 2.0 collective-permute-done
  136.8 4.6 %fusion.2 = pred[1280,128]{1,0:T(8,128)(4,1)S(1)} fusion(s32[128,8]{0,1:T(8,128)S(1)} %multiply_add_fusion), kind=kLoop, calls=%fused_computation.7 | loop fusion | flops 2457600 | bytes 167936 | tf_op jit(solution)/shard_map/reduce_or | solution.py:238
  141.4 2.0 copy.64
  143.4 2.3 copy.47
  145.7 1.0 constant_dynamic-update-slice_fusion
  146.8 1.6 fusion.39
  150.1 0.9 copy.53
  151.0 2.0 copy.58
  153.2 3.2 convolution_dynamic-update-slice_fusion.1
  156.4 3.0 convolution_dynamic-update-slice_fusion
  159.7 3.9 convolution_convert_fusion.1
  163.6 121.7 %shard_map.132 = bf16[32,40,2048]{2,1,0:T(8,128)(2,1)} custom-call(bf16[32,40,2048]{2,1,0:T(8,128)(2,1)} %bitcast.65), custom_call_target="tpu_custom_call" | custom-call | bytes 10485760 | tf_op jit(solution)/shard_map/pallas_call | solution.py:101
  285.3 12.1 %fusion = f32[1280,1536]{1,0:T(8,128)S(1)} fusion(bf16[1280,2048]{1,0:T(8,128)(2,1)} %bitcast.69, bf16[1,2048,1536]{2,1,0:T(8,128)(2,1)} %param.20), kind=kOutput, calls=%fused_computation.2 | convolution fusion | flops 8053063680 | bytes 19398656 | tf_op jit(solution)/shard_map/dot_general | solution.py:120
  297.4 6.3 %convolution_convert_fusion = bf16[1280,2048]{1,0:T(8,128)(2,1)} fusion(bf16[1,768,2048]{2,1,0:T(8,128)(2,1)S(1)} %copy-done, f32[1280,1536]{1,0:T(8,128)S(1)} %fusion), kind=kOutput, calls=%fused_computation | convolution fusion | flops 4035051520 | bytes 16252928 | tf_op jit(solution)/shard_map/dot_general | solution.py:124
  303.7 120.7 %shard_map.133 = bf16[32,40,2048]{2,1,0:T(8,128)(2,1)} custom-call(bf16[32,40,2048]{2,1,0:T(8,128)(2,1)} %bitcast.70), custom_call_target="tpu_custom_call" | custom-call | bytes 10485760 | tf_op jit(solution)/shard_map/pallas_call | solution.py:101
  424.4 5.8 %fusion.6 = bf16[128,2048]{1,0:T(8,128)(2,1)} fusion(f32[128,1280]{1,0:T(8,128)} %select_reduce_fusion, bf16[1280,2048]{1,0:T(8,128)(2,1)} %bitcast.66, bf16[128,2048]{1,0:T(8,128)(2,1)} %copy-done.1), kind=kOutput, calls=%fused_computation.14 | convolution fusion | flops 4027318272 | bytes 6946816 | tf_op jit(solution)/shard_map/dot_general | solution.py:260
  (59 shorter events, 6.2 us)
Async XLA Ops:
  0.6 296.8 %copy-start = (bf16[1,768,2048]{2,1,0:T(8,128)(2,1)S(1)}, bf16[1,768,2048]{2,1,0:T(8,128)(2,1)}, u32[]{:S(2)}) copy-start(bf16[1,768,2048]{2,1,0:T(8,128)(2,1)} %param.21) | copy-start | bytes 9437188
  0.6 128.6 %copy-start.6 = (bf16[128,256]{1,0:T(8,128)(2,1)S(1)}, bf16[128,256]{1,0:T(8,128)(2,1)}, u32[]{:S(2)}) copy-start(bf16[128,256]{1,0:T(8,128)(2,1)} %param.13) | copy-start | bytes 196612
  0.7 128.7 %copy-start.7 = (bf16[128,256]{1,0:T(8,128)(2,1)S(1)}, bf16[128,256]{1,0:T(8,128)(2,1)}, u32[]{:S(2)}) copy-start(bf16[128,256]{1,0:T(8,128)(2,1)} %param.14) | copy-start | bytes 196612
  0.7 130.0 %copy-start.9 = (s32[128,8]{0,1:T(8,128)S(1)}, s32[128,8]{0,1:T(8,128)}, u32[]{:S(2)}) copy-start(s32[128,8]{0,1:T(8,128)} %param.22) | copy-start | bytes 12292
  0.7 131.0 %copy-start.11 = (f32[128,8]{0,1:T(8,128)S(1)}, f32[128,8]{0,1:T(8,128)}, u32[]{:S(2)}) copy-start(f32[128,8]{0,1:T(8,128)} %param.23) | copy-start | bytes 12292
  1.6 1.5 collective-permute-start.2
  3.9 8.6 %collective-permute-start.3 = (bf16[64,2048]{1,0:T(8,128)(2,1)S(1)}, bf16[64,2048]{1,0:T(8,128)(2,1)S(1)}, u32[]{:S(2)}, u32[]{:S(2)}) collective-permute-start(bf16[64,2048]{1,0:T(8,128)(2,1)S(1)} %add_dynamic-update-slice_fusion), channel_id=1, source_target_pairs={{0,64},{32,96},{64,0},{96,32},{128,192},{160,224},{192,128},{224,1... | collective-permute-start | bytes 786440 | tf_op jit(solution)/shard_map/ppermute | solution.py:199
  12.6 11.2 %collective-permute-start.4 = (bf16[64,2048]{1,0:T(8,128)(2,1)S(1)}, bf16[64,2048]{1,0:T(8,128)(2,1)}, u32[]{:S(2)}, u32[]{:S(2)}) collective-permute-start(bf16[64,2048]{1,0:T(8,128)(2,1)S(1)} %add.99), channel_id=1, source_target_pairs={{0,128},{32,160},{64,192},{96,224},{128,0},{160,32},{192,64},{224,... | collective-permute-start | bytes 786440 | tf_op jit(solution)/shard_map/ppermute | solution.py:199
  129.1 27.2 %collective-permute-start.5 = (bf16[2048,1024]{1,0:T(8,128)(2,1)}, bf16[2048,1024]{1,0:T(8,128)(2,1)}, u32[]{:S(2)}, u32[]{:S(2)}) collective-permute-start(bf16[2048,1024]{1,0:T(8,128)(2,1)} %bitcast.67), channel_id=1, source_target_pairs={{0,32},{32,0},{64,96},{96,64},{128,160},{160,128},{192,224},{224,1... | collective-permute-start | bytes 12582920 | tf_op jit(solution)/shard_map/ppermute | solution.py:203
  130.2 6.2 %collective-permute-start = (bf16[2,128,256]{1,2,0:T(8,128)(2,1)}, bf16[2,128,256]{1,2,0:T(8,128)(2,1)S(1)}, u32[]{:S(2)}, u32[]{:S(2)}) collective-permute-start(bf16[2,128,256]{1,2,0:T(8,128)(2,1)} %pad_maximum_fusion), channel_id=1, source_target_pairs={{0,32},{32,64},{64,96},{96,128},{128,160},{160,192},{192,224},{224... | collective-permute-start | bytes 393224 | tf_op jit(solution)/shard_map/ppermute | solution.py:21
  131.4 17.0 %copy-start.8 = (f32[128,16]{0,1:T(8,128)S(1)}, f32[128,16]{0,1:T(8,128)}, u32[]{:S(2)}) copy-start(f32[128,16]{0,1:T(8,128)} %param.16) | copy-start | bytes 24580
  136.4 9.3 %collective-permute-start.1 = (bf16[2,128,256]{1,2,0:T(8,128)(2,1)S(1)}, bf16[2,128,256]{1,2,0:T(8,128)(2,1)}, u32[]{:S(2)}, u32[]{:S(2)}) collective-permute-start(bf16[2,128,256]{1,2,0:T(8,128)(2,1)S(1)} %collective-permute-done), channel_id=1, source_target_pairs={{0,32},{32,64},{64,96},{96,128},{128,160},{160,192},{192,224},{224... | collective-permute-start | bytes 393224 | tf_op jit(solution)/shard_map/ppermute | solution.py:21
  145.7 3.0 copy-start.4
  149.2 0.8 copy-start.3
  153.0 3.3 copy-start.2
  153.1 6.2 %copy-start.5 = (bf16[128,2048]{1,0:T(8,128)(2,1)S(1)}, bf16[128,2048]{1,0:T(8,128)(2,1)}, u32[]{:S(2)}) copy-start(bf16[128,2048]{1,0:T(8,128)(2,1)} %param.17) | copy-start | bytes 1572868
  156.3 3.3 copy-start.10
  159.5 4.1 copy-start.1
